TPU v7x, 32 devices: a whole 2x2x4 slice. The times are simulated.
32 devices in a mesh: col: 4 (over x, core), slab: 8 (over z, y).
Axes of the slice: x: 2, y: 2, z: 4, core: 2. Of those that a mesh axis runs over, the one named last changes fastest.
Arguments:
- labels: int32 [32, 64, 128], P('col', 'slab'), may hold values from 0 to 2
- table: float32 [3], replicated, may hold values from 0.3 to 3
- factor: float32 [32, 64, 128], P('col', 'slab'), may hold values from 0.5 to 2
- chi: float32 [3, 32, 64, 128], P(None, 'col', 'slab'), may hold values from -2.5 to 2.5
- weights: float32 [3, 3], replicated, may hold values from -3.5 to 3.5
Outputs:
- adjoint: float32 [3, 32, 64, 128], P(None, 'col', 'slab')
- gradient: float32 [32, 64, 128], P('col', 'slab')
All inputs are finite; a program needn't handle non-finite values.
Results may differ from a plain program's by a relative error of at most 0.0001.
Values sent between devices are 32-bit elements; how exact they have to be, the bound alone decides.
No kernel may reach another device: no remote copies, remote signals or barrier semaphores. Data moves between devices by JAX's collectives and lax.ppermute only.
A program may use at most 64 MiB of HBM per device.

v0:
```python
import jax
import jax.numpy as jnp
from jax import lax
from jax.sharding import PartitionSpec as P

ITERS = 3


mass_shift = 0.01


def extended(block, sides, width):
    for axis, dim in sides:
        count = lax.axis_size(axis)
        forward = [(i, i + 1) for i in range(count - 1)]
        forward.append((count - 1, 0))
        backward = [(target, source) for source, target in forward]
        low = lax.ppermute(
            lax.slice_in_dim(block, block.shape[dim] - width, None, axis=dim), axis, forward
        )
        high = lax.ppermute(lax.slice_in_dim(block, 0, width, axis=dim), axis, backward)
        block = jnp.concatenate([low, block, high], axis=dim)
    return block


def neighbour_pair(padded, field, spatial):
    if spatial == 0:
        return (padded[..., :-1, 1:-1, :], padded[..., 1:, 1:-1, :])
    if spatial == 1:
        return (padded[..., 1:-1, :-1, :], padded[..., 1:-1, 1:, :])
    return (field, jnp.roll(field, -1, axis=-1))


def split_faces(full, spatial):
    if spatial == 0:
        return (full[..., 1:, :, :], full[..., :-1, :, :])
    if spatial == 1:
        return (full[..., :, 1:, :], full[..., :, :-1, :])
    return (full, jnp.roll(full, 1, axis=-1))


def neighbours(padded, centre, spatial):
    if spatial == 0:
        return (padded[:, :-2, 1:-1, :], padded[:, 2:, 1:-1, :])
    if spatial == 1:
        return (padded[:, 1:-1, :-2, :], padded[:, 1:-1, 2:, :])
    return (jnp.roll(centre, 1, axis=-1), jnp.roll(centre, -1, axis=-1))


def widen(values):
    return values[:, None, None, None]


def apply_operator(padded, centre, cond_full):
    result = mass_shift * centre
    for d in range(3):
        c_now, c_prev = split_faces(cond_full[d], d)
        before, after = neighbours(padded, centre, d)
        result = result + c_now * (centre - after) + c_prev * (centre - before)
    return result


def squares(residual):
    return lax.psum(jnp.sum(residual * residual, axis=(1, 2, 3)), ("col", "slab"))


def shards(labels, table, factor, chi, weights):
    conduct = jnp.where(labels == 0, table[0], jnp.where(labels == 1, table[1], table[2])) * factor
    stacked = jnp.concatenate([chi, conduct[None]], axis=0)
    padded = extended(stacked, (("col", 1), ("slab", 2)), 1)
    chi_pad = padded[:3]
    cond_pad = padded[3]
    cond_full, strain_full, kpairs = ([], [], [])
    for d in range(3):
        here, after = neighbour_pair(cond_pad, conduct, d)
        cond_full.append(2.0 * here * after / (here + after))
        kpairs.append((here, after))
        c_here, c_after = neighbour_pair(chi_pad, chi, d)
        strain_full.append(
            jnp.stack([(1.0 if j == d else 0.0) + (c_after[j] - c_here[j]) for j in range(3)])
        )
    drive = jnp.zeros_like(chi)
    for d in range(3):
        flux_now, flux_prev = split_faces(cond_full[d] * strain_full[d], d)
        drive = drive + (flux_prev - flux_now)
    source = jnp.stack(
        [
            weights[i, 0] * drive[0] + weights[i, 1] * drive[1] + weights[i, 2] * drive[2]
            for i in range(3)
        ]
    )
    adjoint = jnp.zeros_like(source)
    residual = source
    direction = source
    norm_now = squares(residual)
    for step in range(ITERS):
        dir_pad = extended(direction, (("col", 1), ("slab", 2)), 1)
        image = apply_operator(dir_pad, direction, cond_full)
        curve = lax.psum(jnp.sum(direction * image, axis=(1, 2, 3)), ("col", "slab"))
        alpha = norm_now / curve
        adjoint = adjoint + widen(alpha) * direction
        residual = residual - widen(alpha) * image
        norm_next = squares(residual)
        direction = residual + widen(norm_next / norm_now) * direction
        norm_now = norm_next
    lam_pad = extended(adjoint, (("col", 1), ("slab", 2)), 1)
    gradient = jnp.zeros_like(conduct)
    for d in range(3):
        lam_here, lam_after = neighbour_pair(lam_pad, adjoint, d)
        lam_diff = lam_after - lam_here
        local = strain_full[d]
        energy = jnp.zeros_like(local[0])
        for i in range(3):
            for j in range(3):
                energy = energy + weights[i, j] * local[i] * local[j]
        h_term = energy - (lam_diff[0] * local[0] + lam_diff[1] * local[1] + lam_diff[2] * local[2])
        here, after = kpairs[d]
        square_sum = (here + after) ** 2
        part_here = 2.0 * after * after / square_sum
        part_after = 2.0 * here * here / square_sum
        term_now, unused_prev = split_faces(h_term * part_here, d)
        unused_now, term_prev = split_faces(h_term * part_after, d)
        gradient = gradient + term_now + term_prev
    return (adjoint, gradient)


def solution(mesh):
    in_specs = (
        P("col", "slab", None),
        P(),
        P("col", "slab", None),
        P(None, "col", "slab", None),
        P(),
    )
    out_specs = (P(None, "col", "slab", None), P("col", "slab", None))
    return jax.shard_map(shards, mesh=mesh, in_specs=in_specs, out_specs=out_specs, check_vma=False)
```

profile of v0, /device:TPU:0, one launch (start us, length us, event | category | flops | bytes accessed | tf_op | source)
XLA Modules:
  0.0 283.4 jit_solution(14369096348308002320)
XLA Ops:
  0.6 1.4 fusion.147
  2.0 2.6 select_multiply_fusion
  5.1 2.0 collective-permute-start.1
  9.1 5.4 %collective-permute-start.3 = (f32[4,10,1,128]{3,2,1,0:T(1,128)S(1)}, f32[4,10,1,128]{3,2,1,0:T(1,128)S(1)}, u32[]{:S(2)}, u32[]{:S(2)}) collective-permute-start(f32[4,10,1,128]{3,2,1,0:T(1,128)S(1)} %get-tuple-element.19), channel_id=1, source_target_pairs={{1,0},{2,1},{3,2},{4,3},{5,4},{6,5},{7,6},{0,7},{9,8},{10,9},{11,1... | collective-permute-start | bytes 61448 | tf_op jit(solution)/shard_map/ppermute | solution.py:21
  14.5 1.5 collective-permute-done.3
  15.9 5.1 %collective-permute-done.2 = f32[4,10,1,128]{3,2,1,0:T(1,128)S(1)} collective-permute-done((f32[4,10,1,128]{3,2,1,0:T(1,128)S(1)}, f32[4,10,1,128]{3,2,1,0:T(1,128)S(1)}, u32[]{:S(2)}, u32[]{:S(2)}) %collective-permute-start.2) | collective-permute-done | bytes 20512 | tf_op jit(solution)/shard_map/ppermute | solution.py:18
  21.3 5.6 %multiply_add_fusion.5 = (f32[1,8,8,128]{3,2,1,0:T(8,128)S(1)}, f32[1,8,8,128]{3,2,1,0:T(8,128)S(1)}, f32[1,8,8,128]{3,2,1,0:T(8,128)S(1)}) fusion(f32[3,8,8,128]{3,2,1,0:T(8,128)S(1)} %fusion.46, f32[]{:T(128)} %bitcast.7, f32[]{:T(128)} %bitcast.6, f32[]{:T(128)} %bitcast, f32[]{:T(128)} %bitcast.10, f32[]{:T(128)} %bitcast.9, f32[]{:T(128)} %bitcast.8, ...), kind=kLoop, calls=%fused_computation.280 | loop fusion | flops 122880 | bytes 196644 | tf_op jit(solution)/shard_map/add | solution.py:88
  27.3 1.7 collective-permute-start.4
  29.1 1.3 collective-permute-done.5
  30.5 2.0 collective-permute-start.7
  32.5 1.7 collective-permute-done.6
  34.2 2.8 collective-permute-done.7
  37.2 36.9 %all-reduce = (f32[3]{0:T(128)S(1)}, f32[3]{0:T(128)S(1)}) all-reduce(f32[3]{0:T(128)S(1)} %get-tuple-element.3, f32[3]{0:T(128)S(1)} %get-tuple-element.2), channel_id=1, replica_groups=mesh['col'=4,'slab'=8] {'col','slab'}, use_global_device_ids=true, to_apply=%region_1.2 | all-reduce | flops 6 | bytes 48 | tf_op jit(solution)/shard_map/psum | solution.py:64
  74.3 42.2 %psum.44 = f32[3]{0:T(128)S(1)} all-reduce(f32[3]{0:T(128)S(1)} %get-tuple-element.10), channel_id=1, replica_groups=mesh['col'=4,'slab'=8] {'col','slab'}, use_global_device_ids=true, to_apply=%region_5.6 | all-reduce | flops 3 | bytes 24 | tf_op jit(solution)/shard_map/psum | solution.py:64
  116.7 1.7 collective-permute-start.8
  118.5 1.3 collective-permute-done.9
  119.9 3.3 %collective-permute-start.10 = (f32[3,10,1,128]{3,2,1,0:T(1,128)S(1)}, f32[3,10,1,128]{3,2,1,0:T(1,128)S(1)}, u32[]{:S(2)}, u32[]{:S(2)}) collective-permute-start(f32[3,10,1,128]{3,2,1,0:T(1,128)S(1)} %get-tuple-element.27), channel_id=1, source_target_pairs={{1,0},{2,1},{3,2},{4,3},{5,4},{6,5},{7,6},{0,7},{9,8},{10,9},{11,1... | collective-permute-start | bytes 46088 | tf_op jit(solution)/shard_map/ppermute | solution.py:21
  123.3 1.3 collective-permute-done.10
  124.6 5.0 %collective-permute-done.11 = f32[3,10,1,128]{3,2,1,0:T(1,128)S(1)} collective-permute-done((f32[3,10,1,128]{3,2,1,0:T(1,128)S(1)}, f32[3,10,1,128]{3,2,1,0:T(1,128)S(1)}, u32[]{:S(2)}, u32[]{:S(2)}) %collective-permute-start.11) | collective-permute-done | bytes 15392 | tf_op jit(solution)/shard_map/ppermute | solution.py:18
  129.8 36.8 %psum.45 = f32[3]{0:T(128)S(1)} all-reduce(f32[3]{0:T(128)S(1)} %get-tuple-element.8), channel_id=1, replica_groups=mesh['col'=4,'slab'=8] {'col','slab'}, use_global_device_ids=true, to_apply=%region_7.8 | all-reduce | flops 3 | bytes 24 | tf_op jit(solution)/shard_map/psum | solution.py:99
  166.9 41.4 %psum.46 = f32[3]{0:T(128)S(1)} all-reduce(f32[3]{0:T(128)S(1)} %multiply_reduce_fusion), channel_id=1, replica_groups=mesh['col'=4,'slab'=8] {'col','slab'}, use_global_device_ids=true, to_apply=%region_9.10 | all-reduce | flops 3 | bytes 24 | tf_op jit(solution)/shard_map/psum | solution.py:64
  208.5 1.7 collective-permute-start.12
  210.3 1.3 collective-permute-done.13
  211.7 3.3 %collective-permute-start.14 = (f32[3,10,1,128]{3,2,1,0:T(1,128)S(1)}, f32[3,10,1,128]{3,2,1,0:T(1,128)S(1)}, u32[]{:S(2)}, u32[]{:S(2)}) collective-permute-start(f32[3,10,1,128]{3,2,1,0:T(1,128)S(1)} %get-tuple-element.25), channel_id=1, source_target_pairs={{1,0},{2,1},{3,2},{4,3},{5,4},{6,5},{7,6},{0,7},{9,8},{10,9},{11,1... | collective-permute-start | bytes 46088 | tf_op jit(solution)/shard_map/ppermute | solution.py:21
  215.1 1.3 collective-permute-done.14
  216.4 5.0 %collective-permute-done.15 = f32[3,10,1,128]{3,2,1,0:T(1,128)S(1)} collective-permute-done((f32[3,10,1,128]{3,2,1,0:T(1,128)S(1)}, f32[3,10,1,128]{3,2,1,0:T(1,128)S(1)}, u32[]{:S(2)}, u32[]{:S(2)}) %collective-permute-start.15) | collective-permute-done | bytes 15392 | tf_op jit(solution)/shard_map/ppermute | solution.py:18
  221.6 36.8 %psum.47 = f32[3]{0:T(128)S(1)} all-reduce(f32[3]{0:T(128)S(1)} %fusion.7), channel_id=1, replica_groups=mesh['col'=4,'slab'=8] {'col','slab'}, use_global_device_ids=true, to_apply=%region_11.12 | all-reduce | flops 3 | bytes 24 | tf_op jit(solution)/shard_map/psum | solution.py:99
  258.8 1.7 collective-permute-start.16
  260.6 5.7 %fusion.94 = (f32[8,8,128]{2,1,0:T(8,128)S(1)}, f32[8,8,128]{2,1,0:T(8,128)S(1)}) fusion(f32[8,8,128]{2,1,0:T(8,128)S(1)} %select_multiply_fusion, f32[8,8,1]{2,1,0:T(8,128)S(1)} %bitcast.219, f32[8,8,127]{2,1,0:T(8,128)S(1)} %slice.582, f32[3,8,8,128]{3,2,1,0:T(8,128)S(1)} %maximum_subtract_fusion.8, f32[]{:T(128)} %bitcast.13, f32[]{:T(128)} %bitcast.12, ...), kind=kLoop, calls=%fused_computation.222 | loop fusion | flops 319488 | bytes 327716 | tf_op jit(solution)/shard_map/mul | solution.py:122
  266.4 4.0 %collective-permute-start.18 = (f32[3,10,1,128]{3,2,1,0:T(1,128)S(1)}, f32[3,10,1,128]{3,2,1,0:T(1,128)S(1)}, u32[]{:S(2)}, u32[]{:S(2)}) collective-permute-start(f32[3,10,1,128]{3,2,1,0:T(1,128)S(1)} %get-tuple-element.23), channel_id=1, source_target_pairs={{1,0},{2,1},{3,2},{4,3},{5,4},{6,5},{7,6},{0,7},{9,8},{10,9},{11,1... | collective-permute-start | bytes 46088 | tf_op jit(solution)/shard_map/ppermute | solution.py:21
  270.5 5.7 %fusion.81 = f32[9,8,128]{2,1,0:T(8,128)S(1)} fusion(f32[3,9,8,128]{3,2,1,0:T(8,128)S(1)} %maximum_subtract_fusion, f32[1,9,8,128]{3,2,1,0:T(8,128)S(1)} %get-tuple-element.18, f32[1,9,8,128]{3,2,1,0:T(8,128)S(1)} %get-tuple-element.17, f32[1,9,8,128]{3,2,1,0:T(8,128)S(1)} %get-tuple-element.16, f32[]{:T(128)} %bitcast.13, f32[]{:T(128)} %bitcast.12, ...), kind=kLoop, calls=%fused_computation.190 | loop fusion | flops 294912 | bytes 258084 | tf_op jit(solution)/shard_map/sub | solution.py:116
  276.9 5.7 %fusion.62 = f32[8,9,128]{2,1,0:T(8,128)S(1)} fusion(f32[3,8,9,128]{3,2,1,0:T(8,128)S(1)} %fusion, f32[1,8,9,128]{3,2,1,0:T(8,128)S(1)} %fusion.68, f32[1,8,9,128]{3,2,1,0:T(8,128)S(1)} %fusion.69, f32[1,8,9,128]{3,2,1,0:T(8,128)S(1)} %maximum_subtract_fusion.10, f32[]{:T(128)} %bitcast.13, f32[]{:T(128)} %bitcast.12, f32[]{:T(128)} %bitcast.11, ...), kind=kLoop, calls=%fused_computation.137 | loop fusion | flops 294912 | bytes 258084 | tf_op jit(solution)/shard_map/sub | solution.py:116
  (81 shorter events, 6.9 us)
Async XLA Ops:
  0.6 4.0 %copy-start = (f32[3,8,8,128]{3,2,1,0:T(8,128)S(1)}, f32[3,8,8,128]{3,2,1,0:T(8,128)}, u32[]{:S(2)}) copy-start(f32[3,8,8,128]{3,2,1,0:T(8,128)} %param.8) | copy-start | bytes 294916
  4.6 4.4 %collective-permute-start = (f32[4,1,8,128]{3,2,1,0:T(8,128)S(1)}, f32[4,1,8,128]{3,2,1,0:T(8,128)S(1)}, u32[]{:S(2)}, u32[]{:S(2)}) collective-permute-start(f32[4,1,8,128]{3,2,1,0:T(8,128)S(1)} %get-tuple-element.21), channel_id=1, source_target_pairs={{0,8},{8,16},{16,24},{24,0},{1,9},{9,17},{17,25},{25,1},{2,10},{10... | collective-permute-start | bytes 49160 | tf_op jit(solution)/shard_map/ppermute | solution.py:18
  5.1 3.9 %collective-permute-start.1 = (f32[4,1,8,128]{3,2,1,0:T(8,128)S(1)}, f32[4,1,8,128]{3,2,1,0:T(8,128)S(1)}, u32[]{:S(2)}, u32[]{:S(2)}) collective-permute-start(f32[4,1,8,128]{3,2,1,0:T(8,128)S(1)} %get-tuple-element.22), channel_id=1, source_target_pairs={{8,0},{16,8},{24,16},{0,24},{9,1},{17,9},{25,17},{1,25},{10,2},{18... | collective-permute-start | bytes 49160 | tf_op jit(solution)/shard_map/ppermute | solution.py:21
  7.5 0.7 copy-start.2
  9.1 6.8 %collective-permute-start.3 = (f32[4,10,1,128]{3,2,1,0:T(1,128)S(1)}, f32[4,10,1,128]{3,2,1,0:T(1,128)S(1)}, u32[]{:S(2)}, u32[]{:S(2)}) collective-permute-start(f32[4,10,1,128]{3,2,1,0:T(1,128)S(1)} %get-tuple-element.19), channel_id=1, source_target_pairs={{1,0},{2,1},{3,2},{4,3},{5,4},{6,5},{7,6},{0,7},{9,8},{10,9},{11,1... | collective-permute-start | bytes 61448 | tf_op jit(solution)/shard_map/ppermute | solution.py:21
  14.5 6.5 %collective-permute-start.2 = (f32[4,10,1,128]{3,2,1,0:T(1,128)S(1)}, f32[4,10,1,128]{3,2,1,0:T(1,128)S(1)}, u32[]{:S(2)}, u32[]{:S(2)}) collective-permute-start(f32[4,10,1,128]{3,2,1,0:T(1,128)S(1)} %get-tuple-element.20), channel_id=1, source_target_pairs={{0,1},{1,2},{2,3},{3,4},{4,5},{5,6},{6,7},{7,0},{8,9},{9,10},{10,1... | collective-permute-start | bytes 61448 | tf_op jit(solution)/shard_map/ppermute | solution.py:18
  27.2 3.2 %collective-permute-start.5 = (f32[3,1,8,128]{3,2,1,0:T(8,128)S(1)}, f32[3,1,8,128]{3,2,1,0:T(8,128)S(1)}, u32[]{:S(2)}, u32[]{:S(2)}) collective-permute-start(f32[3,1,8,128]{3,2,1,0:T(8,128)S(1)} %get-tuple-element.45), channel_id=1, source_target_pairs={{0,8},{8,16},{16,24},{24,0},{1,9},{9,17},{17,25},{25,1},{2,10},{10... | collective-permute-start | bytes 36872 | tf_op jit(solution)/shard_map/ppermute | solution.py:18
  27.3 3.1 %collective-permute-start.4 = (f32[3,1,8,128]{3,2,1,0:T(8,128)S(1)}, f32[3,1,8,128]{3,2,1,0:T(8,128)S(1)}, u32[]{:S(2)}, u32[]{:S(2)}) collective-permute-start(f32[3,1,8,128]{3,2,1,0:T(8,128)S(1)} %get-tuple-element.46), channel_id=1, source_target_pairs={{8,0},{16,8},{24,16},{0,24},{9,1},{17,9},{25,17},{1,25},{10,2},{18... | collective-permute-start | bytes 36872 | tf_op jit(solution)/shard_map/ppermute | solution.py:21
  30.4 3.8 %collective-permute-start.6 = (f32[3,10,1,128]{3,2,1,0:T(1,128)S(1)}, f32[3,10,1,128]{3,2,1,0:T(1,128)S(1)}, u32[]{:S(2)}, u32[]{:S(2)}) collective-permute-start(f32[3,10,1,128]{3,2,1,0:T(1,128)S(1)} %get-tuple-element.29), channel_id=1, source_target_pairs={{1,0},{2,1},{3,2},{4,3},{5,4},{6,5},{7,6},{0,7},{9,8},{10,9},{11,1... | collective-permute-start | bytes 46088 | tf_op jit(solution)/shard_map/ppermute | solution.py:21
  30.5 6.5 %collective-permute-start.7 = (f32[3,10,1,128]{3,2,1,0:T(1,128)S(1)}, f32[3,10,1,128]{3,2,1,0:T(1,128)S(1)}, u32[]{:S(2)}, u32[]{:S(2)}) collective-permute-start(f32[3,10,1,128]{3,2,1,0:T(1,128)S(1)} %get-tuple-element.30), channel_id=1, source_target_pairs={{0,1},{1,2},{2,3},{3,4},{4,5},{5,6},{6,7},{7,0},{8,9},{9,10},{10,1... | collective-permute-start | bytes 46088 | tf_op jit(solution)/shard_map/ppermute | solution.py:18
  116.6 3.2 %collective-permute-start.9 = (f32[3,1,8,128]{3,2,1,0:T(8,128)S(1)}, f32[3,1,8,128]{3,2,1,0:T(8,128)S(1)}, u32[]{:S(2)}, u32[]{:S(2)}) collective-permute-start(f32[3,1,8,128]{3,2,1,0:T(8,128)S(1)} %get-tuple-element.39), channel_id=1, source_target_pairs={{0,8},{8,16},{16,24},{24,0},{1,9},{9,17},{17,25},{25,1},{2,10},{10... | collective-permute-start | bytes 36872 | tf_op jit(solution)/shard_map/ppermute | solution.py:18
  116.7 3.1 %collective-permute-start.8 = (f32[3,1,8,128]{3,2,1,0:T(8,128)S(1)}, f32[3,1,8,128]{3,2,1,0:T(8,128)S(1)}, u32[]{:S(2)}, u32[]{:S(2)}) collective-permute-start(f32[3,1,8,128]{3,2,1,0:T(8,128)S(1)} %get-tuple-element.40), channel_id=1, source_target_pairs={{8,0},{16,8},{24,16},{0,24},{9,1},{17,9},{25,17},{1,25},{10,2},{18... | collective-permute-start | bytes 36872 | tf_op jit(solution)/shard_map/ppermute | solution.py:21
  119.9 4.7 %collective-permute-start.10 = (f32[3,10,1,128]{3,2,1,0:T(1,128)S(1)}, f32[3,10,1,128]{3,2,1,0:T(1,128)S(1)}, u32[]{:S(2)}, u32[]{:S(2)}) collective-permute-start(f32[3,10,1,128]{3,2,1,0:T(1,128)S(1)} %get-tuple-element.27), channel_id=1, source_target_pairs={{1,0},{2,1},{3,2},{4,3},{5,4},{6,5},{7,6},{0,7},{9,8},{10,9},{11,1... | collective-permute-start | bytes 46088 | tf_op jit(solution)/shard_map/ppermute | solution.py:21
  123.2 6.4 %collective-permute-start.11 = (f32[3,10,1,128]{3,2,1,0:T(1,128)S(1)}, f32[3,10,1,128]{3,2,1,0:T(1,128)S(1)}, u32[]{:S(2)}, u32[]{:S(2)}) collective-permute-start(f32[3,10,1,128]{3,2,1,0:T(1,128)S(1)} %get-tuple-element.28), channel_id=1, source_target_pairs={{0,1},{1,2},{2,3},{3,4},{4,5},{5,6},{6,7},{7,0},{8,9},{9,10},{10,1... | collective-permute-start | bytes 46088 | tf_op jit(solution)/shard_map/ppermute | solution.py:18
  208.4 3.2 %collective-permute-start.13 = (f32[3,1,8,128]{3,2,1,0:T(8,128)S(1)}, f32[3,1,8,128]{3,2,1,0:T(8,128)S(1)}, u32[]{:S(2)}, u32[]{:S(2)}) collective-permute-start(f32[3,1,8,128]{3,2,1,0:T(8,128)S(1)} %get-tuple-element.37), channel_id=1, source_target_pairs={{0,8},{8,16},{16,24},{24,0},{1,9},{9,17},{17,25},{25,1},{2,10},{10... | collective-permute-start | bytes 36872 | tf_op jit(solution)/shard_map/ppermute | solution.py:18
  208.5 3.1 %collective-permute-start.12 = (f32[3,1,8,128]{3,2,1,0:T(8,128)S(1)}, f32[3,1,8,128]{3,2,1,0:T(8,128)S(1)}, u32[]{:S(2)}, u32[]{:S(2)}) collective-permute-start(f32[3,1,8,128]{3,2,1,0:T(8,128)S(1)} %get-tuple-element.38), channel_id=1, source_target_pairs={{8,0},{16,8},{24,16},{0,24},{9,1},{17,9},{25,17},{1,25},{10,2},{18... | collective-permute-start | bytes 36872 | tf_op jit(solution)/shard_map/ppermute | solution.py:21
  211.7 4.7 %collective-permute-start.14 = (f32[3,10,1,128]{3,2,1,0:T(1,128)S(1)}, f32[3,10,1,128]{3,2,1,0:T(1,128)S(1)}, u32[]{:S(2)}, u32[]{:S(2)}) collective-permute-start(f32[3,10,1,128]{3,2,1,0:T(1,128)S(1)} %get-tuple-element.25), channel_id=1, source_target_pairs={{1,0},{2,1},{3,2},{4,3},{5,4},{6,5},{7,6},{0,7},{9,8},{10,9},{11,1... | collective-permute-start | bytes 46088 | tf_op jit(solution)/shard_map/ppermute | solution.py:21
  215.0 6.4 %collective-permute-start.15 = (f32[3,10,1,128]{3,2,1,0:T(1,128)S(1)}, f32[3,10,1,128]{3,2,1,0:T(1,128)S(1)}, u32[]{:S(2)}, u32[]{:S(2)}) collective-permute-start(f32[3,10,1,128]{3,2,1,0:T(1,128)S(1)} %get-tuple-element.26), channel_id=1, source_target_pairs={{0,1},{1,2},{2,3},{3,4},{4,5},{5,6},{6,7},{7,0},{8,9},{9,10},{10,1... | collective-permute-start | bytes 46088 | tf_op jit(solution)/shard_map/ppermute | solution.py:18
  258.6 18.3 %copy-start.1 = (f32[3,8,8,128]{3,2,1,0:T(8,128)}, f32[3,8,8,128]{3,2,1,0:T(8,128)S(1)}, u32[]{:S(2)}) copy-start(f32[3,8,8,128]{3,2,1,0:T(8,128)S(1)} %multiply_add_fusion) | copy-start | bytes 294916
  258.7 7.7 %collective-permute-start.17 = (f32[3,1,8,128]{3,2,1,0:T(8,128)S(1)}, f32[3,1,8,128]{3,2,1,0:T(8,128)S(1)}, u32[]{:S(2)}, u32[]{:S(2)}) collective-permute-start(f32[3,1,8,128]{3,2,1,0:T(8,128)S(1)} %get-tuple-element.31), channel_id=1, source_target_pairs={{0,8},{8,16},{16,24},{24,0},{1,9},{9,17},{17,25},{25,1},{2,10},{10... | collective-permute-start | bytes 36872 | tf_op jit(solution)/shard_map/ppermute | solution.py:18
  258.8 7.6 %collective-permute-start.16 = (f32[3,1,8,128]{3,2,1,0:T(8,128)S(1)}, f32[3,1,8,128]{3,2,1,0:T(8,128)S(1)}, u32[]{:S(2)}, u32[]{:S(2)}) collective-permute-start(f32[3,1,8,128]{3,2,1,0:T(8,128)S(1)} %get-tuple-element.32), channel_id=1, source_target_pairs={{8,0},{16,8},{24,16},{0,24},{9,1},{17,9},{25,17},{1,25},{10,2},{18... | collective-permute-start | bytes 36872 | tf_op jit(solution)/shard_map/ppermute | solution.py:21
  266.4 9.7 %collective-permute-start.18 = (f32[3,10,1,128]{3,2,1,0:T(1,128)S(1)}, f32[3,10,1,128]{3,2,1,0:T(1,128)S(1)}, u32[]{:S(2)}, u32[]{:S(2)}) collective-permute-start(f32[3,10,1,128]{3,2,1,0:T(1,128)S(1)} %get-tuple-element.23), channel_id=1, source_target_pairs={{1,0},{2,1},{3,2},{4,3},{5,4},{6,5},{7,6},{0,7},{9,8},{10,9},{11,1... | collective-permute-start | bytes 46088 | tf_op jit(solution)/shard_map/ppermute | solution.py:21
  270.5 6.4 %collective-permute-start.19 = (f32[3,10,1,128]{3,2,1,0:T(1,128)S(1)}, f32[3,10,1,128]{3,2,1,0:T(1,128)S(1)}, u32[]{:S(2)}, u32[]{:S(2)}) collective-permute-start(f32[3,10,1,128]{3,2,1,0:T(1,128)S(1)} %get-tuple-element.24), channel_id=1, source_target_pairs={{0,1},{1,2},{2,3},{3,4},{4,5},{5,6},{6,7},{7,0},{8,9},{9,10},{10,1... | collective-permute-start | bytes 46088 | tf_op jit(solution)/shard_map/ppermute | solution.py:18
where the time goes:
time: 285 us; the launch traced here: 283 us
  blocking collectives  194 us (68%)
  other arithmetic  28.3 us (10%)
  waiting for transfers between devices  28.3 us (10%)
  starting transfers between devices  27.8 us (10%)
  local copies, waits for them, and re-layouts  3.7 us (1%)
    psum x3, blocking collectives, squares(): lax.psum(jnp.sum(residual * residual, axis=(1, 2, 3)), ('col', 'slab'))  121 us
    psum x2, blocking collectives, shards(): lax.psum(jnp.sum(direction * image, axis=(1, 2, 3)), ('col', 'slab'))  73.7 us
    ppermute x10, starting transfers between devices, extended(): lax.ppermute(lax.slice_in_dim(block, 0, width, axis=dim), axis, backward)  25 us
    ppermute x10, waiting for transfers between devices, extended(): lax.ppermute(lax.slice_in_dim(block, block.shape[dim] - width, None, axis...  22.4 us
    sub x2, other arithmetic, shards(): energy - (lam_diff[0] * local[0] + lam_diff[1] * local[1] + lam_diff[2] *...  11.4 us
    ppermute x10, waiting for transfers between devices, extended(): lax.ppermute(lax.slice_in_dim(block, 0, width, axis=dim), axis, backward)  5.95 us
    mul x1, other arithmetic, shards(): unused_now, term_prev = split_faces(h_term * part_after, d)  5.72 us
  transfers between devices with their start and end apart: 20, of which 12 were waited for; matrix products, arithmetic and copies ran while one was open for 5% of the time, Pallas kernels for 0%

commit v1 on v0

v1 whole, which is shorter than its diff:
```python
import functools

import jax
import jax.numpy as jnp
from jax import lax
from jax.experimental import pallas as pl
from jax.experimental.pallas import tpu as pltpu
from jax.sharding import PartitionSpec as P


mass_shift = 0.01
HALO = 4
STEP = 16
MOMENTS = 6

VMEM = pl.BlockSpec(memory_space=pltpu.VMEM)
SMEM = pl.BlockSpec(memory_space=pltpu.SMEM)


def tile_iota(axis):
    return lax.broadcasted_iota(jnp.int32, (8, 128), axis)


def y_next(tile):
    return pltpu.roll(tile, 127, 1)


def y_prev(tile):
    return pltpu.roll(tile, 1, 1)


def z_next(pair):
    last = tile_iota(0) == 7
    first, second = (pltpu.roll(tile, 7, 0) for tile in pair)
    return jnp.where(last, second, first), jnp.where(last, first, second)


def z_prev(pair):
    top = tile_iota(0) == 0
    first, second = (pltpu.roll(tile, 1, 0) for tile in pair)
    return jnp.where(top, second, first), jnp.where(top, first, second)


def prepare(labels, table, factor, chi, weights, own, low_rows, high_rows, splat):
    layers = factor.shape[0]
    for x in range(layers):
        label = labels[x]
        conduct = jnp.where(label == 0, table[0], jnp.where(label == 1, table[1], table[2])) * factor[x]
        own[3, x] = conduct
        for j in range(3):
            own[j, x] = chi[j, x]
    for i in range(3):
        for j in range(3):
            splat[3 * i + j] = jnp.full((8, 128), weights[i, j], jnp.float32)
    half = tile_iota(0) < 4
    for f in range(4):
        for i in range(layers // 2):
            even, odd = own[f, 2 * i], own[f, 2 * i + 1]
            low_rows[f, i] = jnp.where(half, even, pltpu.roll(odd, 4, 0))
            high_rows[f, i] = jnp.where(half, pltpu.roll(even, 4, 0), odd)


def krylov(layers, peers, own, z_low, z_high, x_low, x_high, splat, near, basis, sums, ring, cond, field):
    total = layers + 2 * HALO
    half = tile_iota(0) < 4

    def ring_tiles(f, low, high, i):
        up, down = high[f, i] if not callable(high) else high(f, i), low[f, i] if not callable(low) else low(f, i)
        return jnp.where(half, up, pltpu.roll(down, 4, 0)), jnp.where(half, pltpu.roll(up, 4, 0), down)

    pairs = HALO // 2
    for f in range(4):
        for i in range(layers // 2):
            ring[f, HALO + 2 * i], ring[f, HALO + 2 * i + 1] = ring_tiles(f, z_low, z_high, i)
        for block, start in ((x_low, 0), (x_high, HALO + layers)):
            for i in range(pairs):
                ring[f, start + 2 * i], ring[f, start + 2 * i + 1] = ring_tiles(
                    f, lambda g, k: block[g, HALO + k], lambda g, k: block[g, HALO + pairs + k], i
                )

    def grid(f, x):
        if x < HALO:
            return x_low[f, x], ring[f, x]
        if x >= HALO + layers:
            return x_high[f, x - HALO - layers], ring[f, x]
        return own[f, x - HALO], ring[f, x]

    def harmonic(here, after):
        return 2.0 * here * after / (here + after)

    for x in range(total - 1):
        here = grid(3, x)
        after = grid(3, x + 1)
        beside = z_next(here)
        for t in range(2):
            cond[0, x, t] = harmonic(here[t], after[t])
            cond[1, x, t] = harmonic(here[t], beside[t])
            cond[2, x, t] = harmonic(here[t], y_next(here[t]))

    def out_flow(x, here, after, offset, flows):
        beside = z_next(here)
        added = []
        z_flux = []
        for t in range(2):
            z_flux.append(cond[1, x, t] * (offset[1] + (beside[t] - here[t])))
        z_back = z_prev(z_flux)
        for t in range(2):
            x_flux = cond[0, x, t] * (offset[0] + (after[t] - here[t]))
            y_flux = cond[2, x, t] * (offset[2] + (y_next(here[t]) - here[t]))
            before = flows[t]
            flows[t] = x_flux
            if before is not None:
                added.append((before - x_flux) + (z_back[t] - z_flux[t]) + (y_prev(y_flux) - y_flux))
        return added

    flows = [[None, None] for _ in range(3)]
    for j in range(3):
        for t in range(2):
            here, after = grid(j, 0)[t], grid(j, 1)[t]
            flows[j][t] = cond[0, 0, t] * ((1.0 if j == 0 else 0.0) + (after - here))
    for x in range(1, total - 1):
        drive = []
        for j in range(3):
            offset = [1.0 if d == j else 0.0 for d in range(3)]
            drive.append(out_flow(x, grid(j, x), grid(j, x + 1), offset, flows[j]))
        for i in range(3):
            for t in range(2):
                field[0, i, x, t] = (
                    splat[3 * i] * drive[0][t] + splat[3 * i + 1] * drive[1][t] + splat[3 * i + 2] * drive[2][t]
                )

    for k in (1, 2):
        for i in range(3):
            first = k
            flow = [cond[0, first, t] * (field[k - 1, i, first + 1, t] - field[k - 1, i, first, t]) for t in range(2)]
            for x in range(first + 1, total - 1 - k):
                here = (field[k - 1, i, x, 0], field[k - 1, i, x, 1])
                after = (field[k - 1, i, x + 1, 0], field[k - 1, i, x + 1, 1])
                added = out_flow(x, here, after, (0.0, 0.0, 0.0), flow)
                for t in range(2):
                    field[k, i, x, t] = mass_shift * here[t] + added[t]

    lane = tile_iota(1)
    packed = jnp.zeros((8, 128), jnp.float32)
    for i in range(3):
        flow = [cond[0, HALO - 1, 0] * (field[2, i, HALO, 0] - field[2, i, HALO - 1, 0]), jnp.zeros((8, 128), jnp.float32)]
        partial = [jnp.zeros((8, 128), jnp.float32) for _ in range(MOMENTS)]
        for x in range(HALO, HALO + layers):
            here = (field[2, i, x, 0], field[2, i, x, 1])
            after = (field[2, i, x + 1, 0], field[2, i, x + 1, 1])
            added = out_flow(x, here, after, (0.0, 0.0, 0.0), flow)
            v = [field[0, i, x, 0], field[1, i, x, 0], here[0], mass_shift * here[0] + added[0]]
            for m, (a, b) in enumerate(((0, 0), (0, 1), (1, 1), (1, 2), (2, 2), (2, 3))):
                partial[m] = partial[m] + v[a] * v[b]
        for m in range(MOMENTS):
            packed = jnp.where(lane == STEP * m + i, jnp.sum(partial[m], axis=1, keepdims=True), packed)
    row = jnp.sum(packed, axis=0, keepdims=True)
    sums[...] = jnp.broadcast_to(row, (peers, 128))

    for x in range(layers + 2):
        for t in range(2):
            for f in range(4):
                near[f, x, t] = grid(f, x + HALO - 1)[t]
            for k in range(3):
                for i in range(3):
                    basis[k, i, x, t] = field[k, i, x + HALO - 1, t]


def coefficients(sums):
    row = jnp.broadcast_to(jnp.sum(sums[...], axis=0, keepdims=True), (8, 128))
    m0, m1, m2, m3, m4, m5 = [row if m == 0 else pltpu.roll(row, 128 - STEP * m, 1) for m in range(MOMENTS)]
    alpha0 = m0 / m1
    norm1 = alpha0 * (alpha0 * m2 - m1)
    grow = 1.0 + norm1 / m0
    alpha1 = norm1 / (grow * grow * m1 - 2.0 * grow * alpha0 * m2 + alpha0 * alpha0 * m3)
    r1 = -(alpha0 + alpha1 * grow)
    r2 = alpha1 * alpha0
    norm2 = m0 + 2.0 * r1 * m1 + (r1 * r1 + 2.0 * r2) * m2 + 2.0 * r1 * r2 * m3 + r2 * r2 * m4
    beta1 = norm2 / norm1
    p0, p1, p2 = 1.0 + beta1 * grow, r1 - beta1 * alpha0, r2
    curve2 = (
        p0 * p0 * m1 + 2.0 * p0 * p1 * m2 + (p1 * p1 + 2.0 * p0 * p2) * m3 + 2.0 * p1 * p2 * m4 + p2 * p2 * m5
    )
    alpha2 = norm2 / curve2
    return alpha0 + alpha1 * grow + alpha2 * p0, alpha2 * p1 - alpha1 * alpha0, alpha2 * p2


def finish(layers, sums, near, basis, splat, adjoint, gradient, lam):
    lane = tile_iota(1)
    scale = []
    for c in coefficients(sums):
        scale.append([jnp.sum(jnp.where(lane == i, c, 0.0), axis=1, keepdims=True) for i in range(3)])
    for i in range(3):
        for x in range(layers + 2):
            for t in range(2):
                if t == 1 and x in (0, layers + 1):
                    continue
                value = scale[0][i] * basis[0, i, x, t] + scale[1][i] * basis[1, i, x, t] + scale[2][i] * basis[2, i, x, t]
                lam[i, x, t] = value
                if t == 0 and 0 < x <= layers:
                    adjoint[i, x - 1] = value

    def face(d, here, after, chi_here, chi_after, lam_here, lam_after):
        local = [(1.0 if j == d else 0.0) + (chi_after[j] - chi_here[j]) for j in range(3)]
        h_term = None
        for i in range(3):
            inner = splat[3 * i] * local[0] + splat[3 * i + 1] * local[1] + splat[3 * i + 2] * local[2]
            part = local[i] * (inner - (lam_after[i] - lam_here[i]))
            h_term = part if h_term is None else h_term + part
        inverse = 1.0 / (here + after)
        share = after * inverse
        rest = here * inverse
        return h_term * (2.0 * share * share), h_term * (2.0 * rest * rest)

    carried = None
    for x in range(layers + 1):
        now, back = face(
            0,
            near[3, x, 0],
            near[3, x + 1, 0],
            [near[j, x, 0] for j in range(3)],
            [near[j, x + 1, 0] for j in range(3)],
            [lam[j, x, 0] for j in range(3)],
            [lam[j, x + 1, 0] for j in range(3)],
        )
        if x > 0:
            total = now + carried
            here = near[3, x, 0]
            chi_here = [near[j, x, 0] for j in range(3)]
            lam_here = [lam[j, x, 0] for j in range(3)]
            y_now, y_back = face(
                2, here, y_next(here), chi_here, [y_next(c) for c in chi_here], lam_here, [y_next(c) for c in lam_here]
            )
            total = total + y_now + y_prev(y_back)
            pair = (here, near[3, x, 1])
            chi_pair = [(near[j, x, 0], near[j, x, 1]) for j in range(3)]
            lam_pair = [(lam[j, x, 0], lam[j, x, 1]) for j in range(3)]
            beside = z_next(pair)
            chi_beside = [z_next(c) for c in chi_pair]
            lam_beside = [z_next(c) for c in lam_pair]
            z_now, z_back = zip(
                *[
                    face(
                        1,
                        pair[t],
                        beside[t],
                        [c[t] for c in chi_pair],
                        [c[t] for c in chi_beside],
                        [c[t] for c in lam_pair],
                        [c[t] for c in lam_beside],
                    )
                    for t in range(2)
                ]
            )
            gradient[x - 1] = total + z_now[0] + z_prev(z_back)[0]
        carried = back


def ring_steps(axis):
    count = lax.axis_size(axis)
    forward = [(i, (i + 1) % count) for i in range(count)]
    return forward, [(target, source) for source, target in forward]


def shards(labels, table, factor, chi, weights):
    layers, rows, columns = factor.shape
    assert rows == 8 and columns == 128 and layers % 2 == 0 and layers >= HALO
    peers = lax.axis_size("col") * lax.axis_size("slab")
    f32 = functools.partial(jax.ShapeDtypeStruct, dtype=jnp.float32)
    pairs = HALO // 2

    own, low_rows, high_rows, splat = pl.pallas_call(
        prepare,
        out_shape=(f32((4, layers, 8, 128)), f32((4, layers // 2, 8, 128)), f32((4, layers // 2, 8, 128)), f32((9, 8, 128))),
        in_specs=[VMEM, SMEM, VMEM, VMEM, SMEM],
        out_specs=(VMEM,) * 4,
        name="prepare",
    )(labels, table, factor, chi, weights)

    forward, backward = ring_steps("slab")
    z_low = lax.ppermute(high_rows, "slab", forward)
    z_high = lax.ppermute(low_rows, "slab", backward)
    forward, backward = ring_steps("col")
    tail = layers // 2 - pairs
    x_low = lax.ppermute(
        jnp.concatenate([own[:, layers - HALO :], z_low[:, tail:], z_high[:, tail:]], axis=1), "col", forward
    )
    x_high = lax.ppermute(jnp.concatenate([own[:, :HALO], z_low[:, :pairs], z_high[:, :pairs]], axis=1), "col", backward)

    total = layers + 2 * HALO
    near, basis, sums = pl.pallas_call(
        functools.partial(krylov, layers, peers),
        out_shape=(f32((4, layers + 2, 2, 8, 128)), f32((3, 3, layers + 2, 2, 8, 128)), f32((peers, 128))),
        in_specs=[VMEM] * 6,
        out_specs=(VMEM,) * 3,
        scratch_shapes=[
            pltpu.VMEM((4, total, 8, 128), jnp.float32),
            pltpu.VMEM((3, total, 2, 8, 128), jnp.float32),
            pltpu.VMEM((3, 3, total, 2, 8, 128), jnp.float32),
        ],
        name="krylov",
    )(own, z_low, z_high, x_low, x_high, splat)

    gathered = lax.all_to_all(sums, ("col", "slab"), 0, 0, tiled=True)

    return pl.pallas_call(
        functools.partial(finish, layers),
        out_shape=(f32((3, layers, 8, 128)), f32((layers, 8, 128))),
        in_specs=[VMEM] * 4,
        out_specs=(VMEM,) * 2,
        scratch_shapes=[pltpu.VMEM((3, layers + 2, 2, 8, 128), jnp.float32)],
        name="finish",
    )(gathered, near, basis, splat)


def solution(mesh):
    in_specs = (
        P("col", "slab", None),
        P(),
        P("col", "slab", None),
        P(None, "col", "slab", None),
        P(),
    )
    out_specs = (P(None, "col", "slab", None), P("col", "slab", None))
    return jax.shard_map(shards, mesh=mesh, in_specs=in_specs, out_specs=out_specs, check_vma=False)
```

time: 285 us -> 37 us (0.13)
  blocking collectives: 194 us -> 13.4 us
  other arithmetic: 28.3 us -> 0.02 us
  waiting for transfers between devices: 28.3 us -> 4.91 us
  starting transfers between devices: 27.8 us -> 7.87 us
  Pallas kernels: 0 us -> 7.71 us
    psum x5 -> x0, blocking collectives: 194 us -> none  [the longest x3 121 us: squares(): lax.psum(jnp.sum(residual * residual, axis=(1, 2, 3)), ('col', 'slab'))]
    ppermute x20 -> x4, waiting for transfers between devices: 28.3 us -> 4.91 us  [the longest x1 2.58 us: shards(): lax.ppermute(jnp.concatenate([own[:, layers - HALO:], z_low[:, tail:], z_...]
    ppermute x20 -> x4, starting transfers between devices: 27.8 us -> 7.87 us  [the longest x1 3.07 us: shards(): z_high = lax.ppermute(low_rows, 'slab', backward)]
    all_to_all x0 -> x1, blocking collectives: none -> 13.4 us  [shards(): gathered = lax.all_to_all(sums, ('col', 'slab'), 0, 0, tiled=True)]
    sub x8 -> x0, other arithmetic: 11.6 us -> none  [the longest x2 11.4 us: shards(): energy - (lam_diff[0] * local[0] + lam_diff[1] * local[1] + lam_diff[2] *...]
    mul x5 -> x0, other arithmetic: 8.4 us -> none  [the longest x1 5.72 us: shards(): unused_now, term_prev = split_faces(h_term * part_after, d)]
    pallas_call x0 -> x3, Pallas kernels: none -> 7.71 us  [the longest x1 3.79 us: shards(): pl.pallas_call(functools.partial(krylov, layers, peers), out_shape=(f32((...]
    add x8 -> x0, other arithmetic: 6.78 us -> none  [the longest x1 5.65 us: shards(): weights[i, 0] * drive[0] + weights[i, 1] * drive[1]]
  transfers between devices with their start and end apart: 20 -> 4, of which waited for: 12 -> 4; matrix products, arithmetic and copies ran while one was open for 5% -> 2% of each run, Pallas kernels for 0% -> 0%
where the time goes in v1:
time: 37 us; the launch traced here: 36.7 us
  blocking collectives  13.4 us (36%)
  starting transfers between devices  7.87 us (21%)
  Pallas kernels  7.71 us (21%)
  waiting for transfers between devices  4.91 us (13%)
  local copies, waits for them, and re-layouts  2.15 us (6%)
  between operations  0.67 us (2%)
    all_to_all x1, blocking collectives, shards(): gathered = lax.all_to_all(sums, ('col', 'slab'), 0, 0, tiled=True)  13.4 us
    pallas_call x1, Pallas kernels, shards(): pl.pallas_call(functools.partial(krylov, layers, peers), out_shape=(f32((...  3.79 us
    ppermute x1, starting transfers between devices, shards(): z_high = lax.ppermute(low_rows, 'slab', backward)  3.07 us
    ppermute x1, starting transfers between devices, shards(): z_low = lax.ppermute(high_rows, 'slab', forward)  2.97 us
    ppermute x1, waiting for transfers between devices, shards(): lax.ppermute(jnp.concatenate([own[:, layers - HALO:], z_low[:, tail:], z_...  2.58 us
    pallas_call x1, Pallas kernels, shards(): pl.pallas_call(functools.partial(finish, layers), out_shape=(f32((3, laye...  2.26 us
    ppermute x1, starting transfers between devices, shards(): lax.ppermute(jnp.concatenate([own[:, :HALO], z_low[:, :pairs], z_high[:,...  1.78 us
    pallas_call x1, Pallas kernels, shards(): pl.pallas_call(prepare, out_shape=(f32((4, layers, 8, 128)), f32((4, laye...  1.67 us
  transfers between devices with their start and end apart: 4, of which 4 were waited for; matrix products, arithmetic and copies ran while one was open for 2% of the time, Pallas kernels for 0%

profile of v1, /device:TPU:0, one launch (start us, length us, event | category | flops | bytes accessed | tf_op | source)
XLA Modules:
  0.0 36.7 jit_solution(1971699602497122853)
XLA Ops:
  0.6 1.7 %prepare.1 = (f32[4,8,8,128]{3,2,1,0:T(8,128)}, f32[4,4,8,128]{3,2,1,0:T(8,128)}, f32[4,4,8,128]{3,2,1,0:T(8,128)}, f32[9,8,128]{2,1,0:T(8,128)}) custom-call(s32[8,8,128]{2,1,0:T(8,128)} %labels.1, f32[3]{0:T(128)} %table.1, f32[8,8,128]{2,1,0:T(8,128)} %factor.1, f32[3,8,8,128]{3,2,1,0:T(8,128)} %chi.1, f32[3,3]{1,0:T(4,128)} %weights.1), custom_call_target="tpu_custom_call" | custom-call | tf_op jit(solution)/shard_map/prepare/pallas_call | solution.py:272
  2.3 3.0 %collective-permute-start = (f32[4,4,8,128]{3,2,1,0:T(8,128)}, f32[4,4,8,128]{3,2,1,0:T(8,128)S(1)}, u32[]{:S(2)}, u32[]{:S(2)}) collective-permute-start(f32[4,4,8,128]{3,2,1,0:T(8,128)} %get-tuple-element.10), channel_id=1, source_target_pairs={{0,1},{1,2},{2,3},{3,4},{4,5},{5,6},{6,7},{7,0},{8,9},{9,10},{10,1... | collective-permute-start | bytes 196616 | tf_op jit(solution)/shard_map/ppermute | solution.py:281
  5.3 3.1 %collective-permute-start.1 = (f32[4,4,8,128]{3,2,1,0:T(8,128)}, f32[4,4,8,128]{3,2,1,0:T(8,128)S(1)}, u32[]{:S(2)}, u32[]{:S(2)}) collective-permute-start(f32[4,4,8,128]{3,2,1,0:T(8,128)} %get-tuple-element.11), channel_id=1, source_target_pairs={{1,0},{2,1},{3,2},{4,3},{5,4},{6,5},{7,6},{0,7},{9,8},{10,9},{11,1... | collective-permute-start | bytes 196616 | tf_op jit(solution)/shard_map/ppermute | solution.py:282
  8.3 0.9 %fusion = (f32[4,4,8,128]{3,2,1,0:T(8,128)S(1)}, f32[4,4,8,128]{3,2,1,0:T(8,128)S(1)}) fusion(f32[4,8,8,128]{3,2,1,0:T(8,128)} %get-tuple-element.9.own), kind=kLoop, calls=%fused_computation.2 | loop fusion | bytes 262144 | tf_op jit(solution)/shard_map/slice | solution.py:288
  9.2 1.6 %collective-permute-done.z_low = f32[4,4,8,128]{3,2,1,0:T(8,128)S(1)} collective-permute-done((f32[4,4,8,128]{3,2,1,0:T(8,128)}, f32[4,4,8,128]{3,2,1,0:T(8,128)S(1)}, u32[]{:S(2)}, u32[]{:S(2)}) %collective-permute-start) | collective-permute-done | bytes 65568 | tf_op jit(solution)/shard_map/ppermute | solution.py:281
  10.8 0.0 copy-start
  10.8 0.3 collective-permute-done.1.z_high
  11.1 0.0 copy-start.1
  11.2 0.3 copy-done
  11.4 0.3 copy-done.1
  11.8 0.1 collective-permute-start.2
  11.9 1.8 %collective-permute-start.3 = (f32[4,8,8,128]{3,2,1,0:T(8,128)S(1)}, f32[4,8,8,128]{3,2,1,0:T(8,128)S(1)}, u32[]{:S(2)}, u32[]{:S(2)}) collective-permute-start(f32[4,8,8,128]{3,2,1,0:T(8,128)S(1)} %pad_maximum_fusion.1), channel_id=1, source_target_pairs={{8,0},{16,8},{24,16},{0,24},{9,1},{17,9},{25,17},{1,25},{10,2},{18... | collective-permute-start | bytes 393224 | tf_op jit(solution)/shard_map/ppermute | solution.py:288
  13.7 2.6 %collective-permute-done.2.x_low = f32[4,8,8,128]{3,2,1,0:T(8,128)S(1)} collective-permute-done((f32[4,8,8,128]{3,2,1,0:T(8,128)S(1)}, f32[4,8,8,128]{3,2,1,0:T(8,128)S(1)}, u32[]{:S(2)}, u32[]{:S(2)}) %collective-permute-start.2) | collective-permute-done | bytes 131104 | tf_op jit(solution)/shard_map/ppermute | solution.py:285
  16.2 0.0 copy-start.2
  16.2 0.4 %collective-permute-done.3.x_high = f32[4,8,8,128]{3,2,1,0:T(8,128)S(1)} collective-permute-done((f32[4,8,8,128]{3,2,1,0:T(8,128)S(1)}, f32[4,8,8,128]{3,2,1,0:T(8,128)S(1)}, u32[]{:S(2)}, u32[]{:S(2)}) %collective-permute-start.3) | collective-permute-done | bytes 131104 | tf_op jit(solution)/shard_map/ppermute | solution.py:288
  16.6 0.0 copy-start.3
  16.7 0.2 copy-done.2
  16.9 0.4 %copy-done.3 = f32[4,8,8,128]{3,2,1,0:T(8,128)} copy-done((f32[4,8,8,128]{3,2,1,0:T(8,128)}, f32[4,8,8,128]{3,2,1,0:T(8,128)S(1)}, u32[]{:S(2)}) %copy-start.3) | copy-done | bytes 131096
  17.3 3.8 %krylov.1 = (f32[4,10,2,8,128]{4,3,2,1,0:T(8,128)}, f32[3,3,10,2,8,128]{5,4,3,2,1,0:T(8,128)}, f32[32,128]{1,0:T(8,128)}) custom-call(f32[4,8,8,128]{3,2,1,0:T(8,128)} %get-tuple-element.9.own, f32[4,4,8,128]{3,2,1,0:T(8,128)} %copy-done, f32[4,4,8,128]{3,2,1,0:T(8,128)} %copy-done.1, f32[4,8,8,128]{3,2,1,0:T(8,128)} %copy-done.2, ...), custom_call_target="tpu_custom_call" | custom-call | tf_op jit(solution)/shard_map/krylov/pallas_call | solution.py:291
  21.1 13.4 %all_to_all.11 = f32[32,1,128]{2,1,0:T(1,128)} all-to-all(f32[32,1,128]{2,1,0:T(1,128)} %bitcast.5), channel_id=1, replica_groups=mesh['col'=4,'slab'=8] {'col','slab'}, dimensions={0} | all-to-all | bytes 32768 | tf_op jit(solution)/shard_map/all_to_all | solution.py:304
  34.4 2.3 %finish.1 = (f32[3,8,8,128]{3,2,1,0:T(8,128)}, f32[8,8,128]{2,1,0:T(8,128)}) custom-call(f32[32,128]{1,0:T(8,128)} %bitcast.4, f32[4,10,2,8,128]{4,3,2,1,0:T(8,128)} %get-tuple-element.14.near, f32[3,3,10,2,8,128]{5,4,3,2,1,0:T(8,128)} %get-tuple-element.15.basis, f32[9,8,128]{2,1,0:T(8,128)} %get-tuple-element.12.splat), custom_call_target="tpu_custom_call" | custom-call | tf_op jit(solution)/shard_map/finish/pallas_call | solution.py:306
  (4 shorter events, 0.0 us)
Async XLA Ops:
  2.3 8.5 %collective-permute-start = (f32[4,4,8,128]{3,2,1,0:T(8,128)}, f32[4,4,8,128]{3,2,1,0:T(8,128)S(1)}, u32[]{:S(2)}, u32[]{:S(2)}) collective-permute-start(f32[4,4,8,128]{3,2,1,0:T(8,128)} %get-tuple-element.10), channel_id=1, source_target_pairs={{0,1},{1,2},{2,3},{3,4},{4,5},{5,6},{6,7},{7,0},{8,9},{9,10},{10,1... | collective-permute-start | bytes 196616 | tf_op jit(solution)/shard_map/ppermute | solution.py:281
  5.3 5.9 %collective-permute-start.1 = (f32[4,4,8,128]{3,2,1,0:T(8,128)}, f32[4,4,8,128]{3,2,1,0:T(8,128)S(1)}, u32[]{:S(2)}, u32[]{:S(2)}) collective-permute-start(f32[4,4,8,128]{3,2,1,0:T(8,128)} %get-tuple-element.11), channel_id=1, source_target_pairs={{1,0},{2,1},{3,2},{4,3},{5,4},{6,5},{7,6},{0,7},{9,8},{10,9},{11,1... | collective-permute-start | bytes 196616 | tf_op jit(solution)/shard_map/ppermute | solution.py:282
  10.8 0.6 %copy-start = (f32[4,4,8,128]{3,2,1,0:T(8,128)}, f32[4,4,8,128]{3,2,1,0:T(8,128)S(1)}, u32[]{:S(2)}) copy-start(f32[4,4,8,128]{3,2,1,0:T(8,128)S(1)} %collective-permute-done.z_low) | copy-start | bytes 196612
  11.1 0.6 %copy-start.1 = (f32[4,4,8,128]{3,2,1,0:T(8,128)}, f32[4,4,8,128]{3,2,1,0:T(8,128)S(1)}, u32[]{:S(2)}) copy-start(f32[4,4,8,128]{3,2,1,0:T(8,128)S(1)} %collective-permute-done.1.z_high) | copy-start | bytes 196612
  11.8 4.4 %collective-permute-start.2 = (f32[4,8,8,128]{3,2,1,0:T(8,128)S(1)}, f32[4,8,8,128]{3,2,1,0:T(8,128)S(1)}, u32[]{:S(2)}, u32[]{:S(2)}) collective-permute-start(f32[4,8,8,128]{3,2,1,0:T(8,128)S(1)} %pad_maximum_fusion), channel_id=1, source_target_pairs={{0,8},{8,16},{16,24},{24,0},{1,9},{9,17},{17,25},{25,1},{2,10},{10... | collective-permute-start | bytes 393224 | tf_op jit(solution)/shard_map/ppermute | solution.py:285
  11.9 4.8 %collective-permute-start.3 = (f32[4,8,8,128]{3,2,1,0:T(8,128)S(1)}, f32[4,8,8,128]{3,2,1,0:T(8,128)S(1)}, u32[]{:S(2)}, u32[]{:S(2)}) collective-permute-start(f32[4,8,8,128]{3,2,1,0:T(8,128)S(1)} %pad_maximum_fusion.1), channel_id=1, source_target_pairs={{8,0},{16,8},{24,16},{0,24},{9,1},{17,9},{25,17},{1,25},{10,2},{18... | collective-permute-start | bytes 393224 | tf_op jit(solution)/shard_map/ppermute | solution.py:288
  16.2 0.7 %copy-start.2 = (f32[4,8,8,128]{3,2,1,0:T(8,128)}, f32[4,8,8,128]{3,2,1,0:T(8,128)S(1)}, u32[]{:S(2)}) copy-start(f32[4,8,8,128]{3,2,1,0:T(8,128)S(1)} %collective-permute-done.2.x_low) | copy-start | bytes 393220
  16.6 0.6 %copy-start.3 = (f32[4,8,8,128]{3,2,1,0:T(8,128)}, f32[4,8,8,128]{3,2,1,0:T(8,128)S(1)}, u32[]{:S(2)}) copy-start(f32[4,8,8,128]{3,2,1,0:T(8,128)S(1)} %collective-permute-done.3.x_high) | copy-start | bytes 393220

commit v2 on v1

--- a/solution.py
+++ b/solution.py
@@ -14,7 +14,8 @@
 MOMENTS = 6
 
 VMEM = pl.BlockSpec(memory_space=pltpu.VMEM)
-SMEM = pl.BlockSpec(memory_space=pltpu.SMEM)
+HBM = pl.BlockSpec(memory_space=pltpu.HBM)
+PARAMS = pltpu.CompilerParams(vmem_limit_bytes=8 * 2**20)
 
 
 def tile_iota(axis):
@@ -41,14 +42,26 @@
     return jnp.where(top, second, first), jnp.where(top, first, second)
 
 
-def prepare(labels, table, factor, chi, weights, own, low_rows, high_rows, splat):
+def prepare(
+    labels_hbm, table_hbm, factor_hbm, chi_hbm, weights_hbm, own, low_rows, high_rows, splat,
+    labels, table, factor, weights, sems,
+):
     layers = factor.shape[0]
+    moves = (
+        (labels_hbm, labels),
+        (table_hbm, table),
+        (factor_hbm, factor),
+        (chi_hbm, own.at[pl.ds(0, 3)]),
+        (weights_hbm, weights),
+    )
+    copies = [pltpu.make_async_copy(source, target, sems.at[n]) for n, (source, target) in enumerate(moves)]
+    for copy in copies:
+        copy.start()
+    for copy in copies:
+        copy.wait()
     for x in range(layers):
         label = labels[x]
-        conduct = jnp.where(label == 0, table[0], jnp.where(label == 1, table[1], table[2])) * factor[x]
-        own[3, x] = conduct
-        for j in range(3):
-            own[j, x] = chi[j, x]
+        own[3, x] = jnp.where(label == 0, table[0], jnp.where(label == 1, table[1], table[2])) * factor[x]
     for i in range(3):
         for j in range(3):
             splat[3 * i + j] = jnp.full((8, 128), weights[i, j], jnp.float32)
@@ -272,8 +285,16 @@
     own, low_rows, high_rows, splat = pl.pallas_call(
         prepare,
         out_shape=(f32((4, layers, 8, 128)), f32((4, layers // 2, 8, 128)), f32((4, layers // 2, 8, 128)), f32((9, 8, 128))),
-        in_specs=[VMEM, SMEM, VMEM, VMEM, SMEM],
+        in_specs=[HBM] * 5,
         out_specs=(VMEM,) * 4,
+        scratch_shapes=[
+            pltpu.VMEM((layers, 8, 128), jnp.int32),
+            pltpu.SMEM((3,), jnp.float32),
+            pltpu.VMEM((layers, 8, 128), jnp.float32),
+            pltpu.SMEM((3, 3), jnp.float32),
+            pltpu.SemaphoreType.DMA((5,)),
+        ],
+        compiler_params=PARAMS,
         name="prepare",
     )(labels, table, factor, chi, weights)
 
@@ -298,6 +319,7 @@
             pltpu.VMEM((3, total, 2, 8, 128), jnp.float32),
             pltpu.VMEM((3, 3, total, 2, 8, 128), jnp.float32),
         ],
+        compiler_params=PARAMS,
         name="krylov",
     )(own, z_low, z_high, x_low, x_high, splat)
 
@@ -309,6 +331,7 @@
         in_specs=[VMEM] * 4,
         out_specs=(VMEM,) * 2,
         scratch_shapes=[pltpu.VMEM((3, layers + 2, 2, 8, 128), jnp.float32)],
+        compiler_params=PARAMS,
         name="finish",
     )(gathered, near, basis, splat)
 

time: 37 us -> 35 us (0.946)
  Pallas kernels: 7.71 us -> 3.57 us
  local copies, waits for them, and re-layouts: 2.15 us -> 3.76 us
  waiting for transfers between devices: 4.91 us -> 5.54 us
    unnamed x8 -> x10, local copies, waits for them, and re-layouts: 1.26 us -> 3.74 us
    pallas_call x1, Pallas kernels: 3.79 us -> 1.73 us  [shards(): pl.pallas_call(functools.partial(krylov, layers, peers), out_shape=(f32((...]
    pallas_call x1, Pallas kernels: 2.26 us -> 1.05 us  [shards(): pl.pallas_call(functools.partial(finish, layers), out_shape=(f32((3, laye...]
    pallas_call x1, Pallas kernels: 1.67 us -> 0.8 us  [shards(): pl.pallas_call(prepare, out_shape=(f32((4, layers, 8, 128)), f32((4, laye...]
    slice x1, local copies, waits for them, and re-layouts: 0.88 us -> 0.01 us  [shards(): own[:, :HALO]]
    ppermute x1, waiting for transfers between devices: 1.59 us -> 2.22 us  [shards(): z_low = lax.ppermute(high_rows, 'slab', forward)]
  transfers between devices with their start and end apart: 4 -> 4, of which waited for: 4 -> 4; matrix products, arithmetic and copies ran while one was open for 2% -> 0% of each run, Pallas kernels for 0% -> 0%
where the time goes in v2:
time: 35 us; the launch traced here: 34.7 us
  blocking collectives  13.1 us (37%)
  starting transfers between devices  7.96 us (23%)
  waiting for transfers between devices  5.54 us (16%)
  local copies, waits for them, and re-layouts  3.76 us (11%)
  Pallas kernels  3.57 us (10%)
  between operations  0.69 us (2%)
    all_to_all x1, blocking collectives, shards(): gathered = lax.all_to_all(sums, ('col', 'slab'), 0, 0, tiled=True)  13.1 us
    unnamed x10, local copies, waits for them, and re-layouts  3.74 us
    ppermute x1, starting transfers between devices, shards(): z_high = lax.ppermute(low_rows, 'slab', backward)  3.1 us
    ppermute x1, starting transfers between devices, shards(): z_low = lax.ppermute(high_rows, 'slab', forward)  3.02 us
    ppermute x1, waiting for transfers between devices, shards(): lax.ppermute(jnp.concatenate([own[:, layers - HALO:], z_low[:, tail:], z_...  2.58 us
    ppermute x1, waiting for transfers between devices, shards(): z_low = lax.ppermute(high_rows, 'slab', forward)  2.22 us
    ppermute x1, starting transfers between devices, shards(): lax.ppermute(jnp.concatenate([own[:, :HALO], z_low[:, :pairs], z_high[:,...  1.78 us
    pallas_call x1, Pallas kernels, shards(): pl.pallas_call(functools.partial(krylov, layers, peers), out_shape=(f32((...  1.73 us
  transfers between devices with their start and end apart: 4, of which 4 were waited for; matrix products, arithmetic and copies ran while one was open for 0% of the time, Pallas kernels for 0%

profile of v2, /device:TPU:0, one launch (start us, length us, event | category | flops | bytes accessed | tf_op | source)
XLA Modules:
  0.0 34.7 jit_solution(8566090145201041872)
XLA Ops:
  0.6 0.0 copy-start
  0.6 0.9 %copy-done = f32[3,8,8,128]{3,2,1,0:T(8,128)S(1)} copy-done((f32[3,8,8,128]{3,2,1,0:T(8,128)S(1)}, f32[3,8,8,128]{3,2,1,0:T(8,128)}, u32[]{:S(2)}) %copy-start) | copy-done | bytes 98328
  1.5 0.0 copy-start.1
  1.5 0.8 %copy-done.1 = s32[8,8,128]{2,1,0:T(8,128)S(1)} copy-done((s32[8,8,128]{2,1,0:T(8,128)S(1)}, s32[8,8,128]{2,1,0:T(8,128)}, u32[]{:S(2)}) %copy-start.1) | copy-done | bytes 32792
  2.3 0.0 copy-start.2
  2.3 0.8 %copy-done.2 = f32[8,8,128]{2,1,0:T(8,128)S(1)} copy-done((f32[8,8,128]{2,1,0:T(8,128)S(1)}, f32[8,8,128]{2,1,0:T(8,128)}, u32[]{:S(2)}) %copy-start.2) | copy-done | bytes 32792
  3.0 0.0 copy-start.3
  3.0 0.7 %copy-done.3 = f32[3,3]{1,0:T(4,128)S(1)} copy-done((f32[3,3]{1,0:T(4,128)S(1)}, f32[3,3]{1,0:T(4,128)}, u32[]{:S(2)}) %copy-start.3) | copy-done | bytes 60
  3.7 0.0 copy-start.4
  3.7 0.7 %copy-done.4 = f32[3]{0:T(128)S(1)} copy-done((f32[3]{0:T(128)S(1)}, f32[3]{0:T(128)}, u32[]{:S(2)}) %copy-start.4) | copy-done | bytes 36
  4.4 0.8 %prepare.1 = (f32[4,8,8,128]{3,2,1,0:T(8,128)S(1)}, f32[4,4,8,128]{3,2,1,0:T(8,128)S(1)}, f32[4,4,8,128]{3,2,1,0:T(8,128)S(1)}, f32[9,8,128]{2,1,0:T(8,128)S(1)}) custom-call(s32[8,8,128]{2,1,0:T(8,128)S(1)} %copy-done.1, f32[3]{0:T(128)S(1)} %copy-done.4, f32[8,8,128]{2,1,0:T(8,128)S(1)} %copy-done.2, f32[3,8,8,128]{3,2,1,0:T(8,128)S(1)} %copy-done, ...), custom_call_target="tpu_custom_call" | custom-call | tf_op jit(solution)/shard_map/prepare/pallas_call | solution.py:285
  5.2 3.0 %collective-permute-start = (f32[4,4,8,128]{3,2,1,0:T(8,128)S(1)}, f32[4,4,8,128]{3,2,1,0:T(8,128)S(1)}, u32[]{:S(2)}, u32[]{:S(2)}) collective-permute-start(f32[4,4,8,128]{3,2,1,0:T(8,128)S(1)} %get-tuple-element.10), channel_id=1, source_target_pairs={{0,1},{1,2},{2,3},{3,4},{4,5},{5,6},{6,7},{7,0},{8,9},{9,10},{10,1... | collective-permute-start | bytes 196616 | tf_op jit(solution)/shard_map/ppermute | solution.py:302
  8.2 3.1 %collective-permute-start.1 = (f32[4,4,8,128]{3,2,1,0:T(8,128)S(1)}, f32[4,4,8,128]{3,2,1,0:T(8,128)S(1)}, u32[]{:S(2)}, u32[]{:S(2)}) collective-permute-start(f32[4,4,8,128]{3,2,1,0:T(8,128)S(1)} %get-tuple-element.11), channel_id=1, source_target_pairs={{1,0},{2,1},{3,2},{4,3},{5,4},{6,5},{7,6},{0,7},{9,8},{10,9},{11,1... | collective-permute-start | bytes 196616 | tf_op jit(solution)/shard_map/ppermute | solution.py:303
  11.3 2.2 %collective-permute-done.z_low = f32[4,4,8,128]{3,2,1,0:T(8,128)S(1)} collective-permute-done((f32[4,4,8,128]{3,2,1,0:T(8,128)S(1)}, f32[4,4,8,128]{3,2,1,0:T(8,128)S(1)}, u32[]{:S(2)}, u32[]{:S(2)}) %collective-permute-start) | collective-permute-done | bytes 65568 | tf_op jit(solution)/shard_map/ppermute | solution.py:302
  13.6 0.3 collective-permute-done.1.z_high
  13.9 0.1 collective-permute-start.2
  14.0 1.8 %collective-permute-start.3 = (f32[4,8,8,128]{3,2,1,0:T(8,128)S(1)}, f32[4,8,8,128]{3,2,1,0:T(8,128)S(1)}, u32[]{:S(2)}, u32[]{:S(2)}) collective-permute-start(f32[4,8,8,128]{3,2,1,0:T(8,128)S(1)} %pad_maximum_fusion.1), channel_id=1, source_target_pairs={{8,0},{16,8},{24,16},{0,24},{9,1},{17,9},{25,17},{1,25},{10,2},{18... | collective-permute-start | bytes 393224 | tf_op jit(solution)/shard_map/ppermute | solution.py:309
  15.8 2.6 %collective-permute-done.2.x_low = f32[4,8,8,128]{3,2,1,0:T(8,128)S(1)} collective-permute-done((f32[4,8,8,128]{3,2,1,0:T(8,128)S(1)}, f32[4,8,8,128]{3,2,1,0:T(8,128)S(1)}, u32[]{:S(2)}, u32[]{:S(2)}) %collective-permute-start.2) | collective-permute-done | bytes 131104 | tf_op jit(solution)/shard_map/ppermute | solution.py:306
  18.3 0.4 %collective-permute-done.3.x_high = f32[4,8,8,128]{3,2,1,0:T(8,128)S(1)} collective-permute-done((f32[4,8,8,128]{3,2,1,0:T(8,128)S(1)}, f32[4,8,8,128]{3,2,1,0:T(8,128)S(1)}, u32[]{:S(2)}, u32[]{:S(2)}) %collective-permute-start.3) | collective-permute-done | bytes 131104 | tf_op jit(solution)/shard_map/ppermute | solution.py:309
  18.8 1.7 %krylov.1 = (f32[4,10,2,8,128]{4,3,2,1,0:T(8,128)S(1)}, f32[3,3,10,2,8,128]{5,4,3,2,1,0:T(8,128)S(1)}, f32[32,128]{1,0:T(8,128)S(1)}) custom-call(f32[4,8,8,128]{3,2,1,0:T(8,128)S(1)} %get-tuple-element.9.own, f32[4,4,8,128]{3,2,1,0:T(8,128)S(1)} %collective-permute-done.z_low, f32[4,4,8,128]{3,2,1,0:T(8,128)S(1)} %collective-permute-done.1.z_high, ...), custom_call_target="tpu_custom_call" | custom-call | tf_op jit(solution)/shard_map/krylov/pallas_call | solution.py:312
  20.5 13.1 %all_to_all.11 = f32[32,1,128]{2,1,0:T(1,128)S(1)} all-to-all(f32[32,1,128]{2,1,0:T(1,128)S(1)} %bitcast.5), channel_id=1, replica_groups=mesh['col'=4,'slab'=8] {'col','slab'}, dimensions={0} | all-to-all | bytes 32768 | tf_op jit(solution)/shard_map/all_to_all | solution.py:326
  33.6 1.0 %finish.1 = (f32[3,8,8,128]{3,2,1,0:T(8,128)}, f32[8,8,128]{2,1,0:T(8,128)}) custom-call(f32[32,128]{1,0:T(8,128)S(1)} %bitcast.4, f32[4,10,2,8,128]{4,3,2,1,0:T(8,128)S(1)} %get-tuple-element.14.near, f32[3,3,10,2,8,128]{5,4,3,2,1,0:T(8,128)S(1)} %get-tuple-element.15.basis, f32[9,8,128]{2,1,0:T(8,128)S(1)} %get-tuple-element.12.splat), custom_call_target="tpu_custom_call" | custom-call | tf_op jit(solution)/shard_map/finish/pallas_call | solution.py:328
  (5 shorter events, 0.0 us)
Async XLA Ops:
  0.6 0.9 %copy-start = (f32[3,8,8,128]{3,2,1,0:T(8,128)S(1)}, f32[3,8,8,128]{3,2,1,0:T(8,128)}, u32[]{:S(2)}) copy-start(f32[3,8,8,128]{3,2,1,0:T(8,128)} %chi_hbm.1) | copy-start | bytes 294916
  1.5 0.8 %copy-start.1 = (s32[8,8,128]{2,1,0:T(8,128)S(1)}, s32[8,8,128]{2,1,0:T(8,128)}, u32[]{:S(2)}) copy-start(s32[8,8,128]{2,1,0:T(8,128)} %labels_hbm.1) | copy-start | bytes 98308
  2.3 0.8 %copy-start.2 = (f32[8,8,128]{2,1,0:T(8,128)S(1)}, f32[8,8,128]{2,1,0:T(8,128)}, u32[]{:S(2)}) copy-start(f32[8,8,128]{2,1,0:T(8,128)} %factor_hbm.1) | copy-start | bytes 98308
  3.0 0.7 %copy-start.3 = (f32[3,3]{1,0:T(4,128)S(1)}, f32[3,3]{1,0:T(4,128)}, u32[]{:S(2)}) copy-start(f32[3,3]{1,0:T(4,128)} %weights_hbm.1) | copy-start | bytes 112
  3.7 0.7 %copy-start.4 = (f32[3]{0:T(128)S(1)}, f32[3]{0:T(128)}, u32[]{:S(2)}) copy-start(f32[3]{0:T(128)} %table_hbm.1) | copy-start | bytes 40
  5.2 8.4 %collective-permute-start = (f32[4,4,8,128]{3,2,1,0:T(8,128)S(1)}, f32[4,4,8,128]{3,2,1,0:T(8,128)S(1)}, u32[]{:S(2)}, u32[]{:S(2)}) collective-permute-start(f32[4,4,8,128]{3,2,1,0:T(8,128)S(1)} %get-tuple-element.10), channel_id=1, source_target_pairs={{0,1},{1,2},{2,3},{3,4},{4,5},{5,6},{6,7},{7,0},{8,9},{9,10},{10,1... | collective-permute-start | bytes 196616 | tf_op jit(solution)/shard_map/ppermute | solution.py:302
  8.2 5.7 %collective-permute-start.1 = (f32[4,4,8,128]{3,2,1,0:T(8,128)S(1)}, f32[4,4,8,128]{3,2,1,0:T(8,128)S(1)}, u32[]{:S(2)}, u32[]{:S(2)}) collective-permute-start(f32[4,4,8,128]{3,2,1,0:T(8,128)S(1)} %get-tuple-element.11), channel_id=1, source_target_pairs={{1,0},{2,1},{3,2},{4,3},{5,4},{6,5},{7,6},{0,7},{9,8},{10,9},{11,1... | collective-permute-start | bytes 196616 | tf_op jit(solution)/shard_map/ppermute | solution.py:303
  13.9 4.4 %collective-permute-start.2 = (f32[4,8,8,128]{3,2,1,0:T(8,128)S(1)}, f32[4,8,8,128]{3,2,1,0:T(8,128)S(1)}, u32[]{:S(2)}, u32[]{:S(2)}) collective-permute-start(f32[4,8,8,128]{3,2,1,0:T(8,128)S(1)} %pad_maximum_fusion), channel_id=1, source_target_pairs={{0,8},{8,16},{16,24},{24,0},{1,9},{9,17},{17,25},{25,1},{2,10},{10... | collective-permute-start | bytes 393224 | tf_op jit(solution)/shard_map/ppermute | solution.py:306
  14.0 4.8 %collective-permute-start.3 = (f32[4,8,8,128]{3,2,1,0:T(8,128)S(1)}, f32[4,8,8,128]{3,2,1,0:T(8,128)S(1)}, u32[]{:S(2)}, u32[]{:S(2)}) collective-permute-start(f32[4,8,8,128]{3,2,1,0:T(8,128)S(1)} %pad_maximum_fusion.1), channel_id=1, source_target_pairs={{8,0},{16,8},{24,16},{0,24},{9,1},{17,9},{25,17},{1,25},{10,2},{18... | collective-permute-start | bytes 393224 | tf_op jit(solution)/shard_map/ppermute | solution.py:309

commit v3 on v2

--- a/solution.py
+++ b/solution.py
@@ -10,7 +10,6 @@
 
 mass_shift = 0.01
 HALO = 4
-STEP = 16
 MOMENTS = 6
 
 VMEM = pl.BlockSpec(memory_space=pltpu.VMEM)
@@ -43,15 +42,15 @@
 
 
 def prepare(
-    labels_hbm, table_hbm, factor_hbm, chi_hbm, weights_hbm, own, low_rows, high_rows, splat,
+    labels_hbm, table_hbm, factor_hbm, chi_hbm, weights_hbm, own_low, own_high, low_rows, high_rows, splat,
     labels, table, factor, weights, sems,
 ):
-    layers = factor.shape[0]
     moves = (
         (labels_hbm, labels),
         (table_hbm, table),
         (factor_hbm, factor),
-        (chi_hbm, own.at[pl.ds(0, 3)]),
+        (chi_hbm.at[:, pl.ds(0, HALO)], own_low.at[pl.ds(0, 3)]),
+        (chi_hbm.at[:, pl.ds(HALO, HALO)], own_high.at[pl.ds(0, 3)]),
         (weights_hbm, weights),
     )
     copies = [pltpu.make_async_copy(source, target, sems.at[n]) for n, (source, target) in enumerate(moves)]
@@ -59,44 +58,114 @@
         copy.start()
     for copy in copies:
         copy.wait()
-    for x in range(layers):
+    for x in range(2 * HALO):
         label = labels[x]
-        own[3, x] = jnp.where(label == 0, table[0], jnp.where(label == 1, table[1], table[2])) * factor[x]
+        block = own_low if x < HALO else own_high
+        block[3, x % HALO] = jnp.where(label == 0, table[0], jnp.where(label == 1, table[1], table[2])) * factor[x]
     for i in range(3):
         for j in range(3):
             splat[3 * i + j] = jnp.full((8, 128), weights[i, j], jnp.float32)
     half = tile_iota(0) < 4
     for f in range(4):
-        for i in range(layers // 2):
-            even, odd = own[f, 2 * i], own[f, 2 * i + 1]
+        for i in range(HALO):
+            block = own_low if 2 * i < HALO else own_high
+            even, odd = block[f, 2 * i % HALO], block[f, (2 * i + 1) % HALO]
             low_rows[f, i] = jnp.where(half, even, pltpu.roll(odd, 4, 0))
             high_rows[f, i] = jnp.where(half, pltpu.roll(even, 4, 0), odd)
 
 
-def krylov(layers, peers, own, z_low, z_high, x_low, x_high, splat, near, basis, sums, ring, cond, field):
-    total = layers + 2 * HALO
+def fold(z_low, z_high, ring, low_corner, high_corner):
     half = tile_iota(0) < 4
-
-    def ring_tiles(f, low, high, i):
-        up, down = high[f, i] if not callable(high) else high(f, i), low[f, i] if not callable(low) else low(f, i)
-        return jnp.where(half, up, pltpu.roll(down, 4, 0)), jnp.where(half, pltpu.roll(up, 4, 0), down)
-
-    pairs = HALO // 2
     for f in range(4):
-        for i in range(layers // 2):
-            ring[f, HALO + 2 * i], ring[f, HALO + 2 * i + 1] = ring_tiles(f, z_low, z_high, i)
-        for block, start in ((x_low, 0), (x_high, HALO + layers)):
-            for i in range(pairs):
-                ring[f, start + 2 * i], ring[f, start + 2 * i + 1] = ring_tiles(
-                    f, lambda g, k: block[g, HALO + k], lambda g, k: block[g, HALO + pairs + k], i
-                )
+        tiles = []
+        for i in range(HALO):
+            up, down = z_high[f, i], z_low[f, i]
+            tiles.append(jnp.where(half, up, pltpu.roll(down, 4, 0)))
+            tiles.append(jnp.where(half, pltpu.roll(up, 4, 0), down))
+        for x, tile in enumerate(tiles):
+            ring[f, x] = tile
+        outer = (tile_iota(0) < 2) | (tile_iota(0) >= 6)
+        for corner, (first, second, third) in ((low_corner, tiles[:3]), (high_corner, tiles[:-4:-1])):
+            corner[f, 0] = first
+            corner[f, 1] = jnp.where(outer, second, jnp.where(half, pltpu.roll(third, 2, 0), pltpu.roll(third, 6, 0)))
+
+
+def two_sum(a, b):
+    total = a + b
+    part = total - a
+    return total, (a - (total - part)) + (b - part)
+
+
+def two_product(a, b):
+    product = a * b
+    a_top, b_top = [4097.0 * v - (4097.0 * v - v) for v in (a, b)]
+    a_rest, b_rest = a - a_top, b - b_top
+    return product, ((a_top * b_top - product) + a_top * b_rest + a_rest * b_top) + a_rest * b_rest
+
+
+def pair_sum(a, b):
+    total, error = two_sum(a[0], b[0])
+    return total, error + (a[1] + b[1])
+
+
+def pair_product(a, b):
+    product, error = two_product(a[0], b[0])
+    return product, error + (a[0] * b[1] + a[1] * b[0])
+
+
+def total_row(tiles):
+    row = tile_iota(0)
+    lane = tile_iota(1)
+    pairs = [(tile, jnp.zeros((8, 128), jnp.float32)) for tile in tiles]
+    place = [[n] for n in range(len(tiles))]
+    for width in (4, 2, 1):
+        lower = (row & width) == 0
+        merged, spots = [], []
+        for n in range(0, len(pairs), 2):
+            first, second = pairs[n], pairs[min(n + 1, len(pairs) - 1)]
+            kept = [jnp.where(lower, a, b) for a, b in zip(first, second)]
+            moved = [jnp.where(lower, pltpu.roll(a, 8 - width, 0), pltpu.roll(b, width, 0)) for a, b in zip(first, second)]
+            merged.append(pair_sum(kept, moved))
+            spots.append((place[n], place[n + 1] if n + 1 < len(pairs) else None))
+        pairs, place = merged, spots
+    result = jnp.zeros((8, 128), jnp.float32)
+
+    def home(spot, at, width):
+        if spot is None:
+            return
+        if len(spot) == 1:
+            yield spot[0], at
+            return
+        yield from home(spot[0], at, 2 * width)
+        yield from home(spot[1], at + width, 2 * width)
+
+    for pair, spot in zip(pairs, place):
+        for shift in (64, 32, 16, 8, 4, 2, 1):
+            pair = pair_sum(pair, [pltpu.roll(a, shift, 1) for a in pair])
+        for n, at in home(spot, 0, 1):
+            result = jnp.where((row == at) & (lane == 4 * n), pair[0], result)
+            result = jnp.where((row == at) & (lane == 4 * n + 1), pair[1], result)
+    return jnp.sum(result, axis=0, keepdims=True)
+
+
+def krylov(peers, own_low, own_high, z_ring, x_low, x_high, corner_low, corner_high, splat, near, basis, sums, ring, cond, field):
+    layers = 2 * HALO
+    total = 2 * layers
+    half = tile_iota(0) < 4
+
+    for f in range(4):
+        for corner, spots in ((corner_low, (3, 2, 1, 0)), (corner_high, (12, 13, 14, 15))):
+            shared = corner[f, 1]
+            ring[f, spots[0]] = corner[f, 0]
+            ring[f, spots[1]] = shared
+            third = jnp.where(half, pltpu.roll(shared, 6, 0), pltpu.roll(shared, 2, 0))
+            ring[f, spots[2]] = third
+            ring[f, spots[3]] = third
 
     def grid(f, x):
-        if x < HALO:
-            return x_low[f, x], ring[f, x]
-        if x >= HALO + layers:
-            return x_high[f, x - HALO - layers], ring[f, x]
-        return own[f, x - HALO], ring[f, x]
+        block = (x_low, own_low, own_high, x_high)[x // HALO]
+        inside = HALO <= x < HALO + layers
+        return block[f, x % HALO], z_ring[f, x - HALO] if inside else ring[f, x]
 
     def harmonic(here, after):
         return 2.0 * here * after / (here + after)
@@ -153,22 +222,17 @@
                 for t in range(2):
                     field[k, i, x, t] = mass_shift * here[t] + added[t]
 
-    lane = tile_iota(1)
-    packed = jnp.zeros((8, 128), jnp.float32)
+    partial = [jnp.zeros((8, 128), jnp.float32) for _ in range(3 * MOMENTS)]
     for i in range(3):
         flow = [cond[0, HALO - 1, 0] * (field[2, i, HALO, 0] - field[2, i, HALO - 1, 0]), jnp.zeros((8, 128), jnp.float32)]
-        partial = [jnp.zeros((8, 128), jnp.float32) for _ in range(MOMENTS)]
         for x in range(HALO, HALO + layers):
             here = (field[2, i, x, 0], field[2, i, x, 1])
             after = (field[2, i, x + 1, 0], field[2, i, x + 1, 1])
             added = out_flow(x, here, after, (0.0, 0.0, 0.0), flow)
             v = [field[0, i, x, 0], field[1, i, x, 0], here[0], mass_shift * here[0] + added[0]]
             for m, (a, b) in enumerate(((0, 0), (0, 1), (1, 1), (1, 2), (2, 2), (2, 3))):
-                partial[m] = partial[m] + v[a] * v[b]
-        for m in range(MOMENTS):
-            packed = jnp.where(lane == STEP * m + i, jnp.sum(partial[m], axis=1, keepdims=True), packed)
-    row = jnp.sum(packed, axis=0, keepdims=True)
-    sums[...] = jnp.broadcast_to(row, (peers, 128))
+                partial[3 * m + i] = partial[3 * m + i] + v[a] * v[b]
+    sums[...] = jnp.broadcast_to(total_row(partial), (peers, 128))
 
     for x in range(layers + 2):
         for t in range(2):
@@ -179,30 +243,74 @@
                     basis[k, i, x, t] = field[k, i, x + HALO - 1, t]
 
 
+def quadratic(terms):
+    products = [pair_product(a, b) for a, b in terms]
+    total = products[0]
+    for product in products[1:]:
+        total = pair_sum(total, product)
+    return total[0] + total[1]
+
+
 def coefficients(sums):
-    row = jnp.broadcast_to(jnp.sum(sums[...], axis=0, keepdims=True), (8, 128))
-    m0, m1, m2, m3, m4, m5 = [row if m == 0 else pltpu.roll(row, 128 - STEP * m, 1) for m in range(MOMENTS)]
-    alpha0 = m0 / m1
-    norm1 = alpha0 * (alpha0 * m2 - m1)
-    grow = 1.0 + norm1 / m0
-    alpha1 = norm1 / (grow * grow * m1 - 2.0 * grow * alpha0 * m2 + alpha0 * alpha0 * m3)
+    count = sums.shape[0] // 8
+    pairs = [(sums[8 * n : 8 * n + 8], jnp.zeros((8, 128), jnp.float32)) for n in range(count)]
+    while len(pairs) > 1:
+        tail = pairs[len(pairs) // 2 * 2 :]
+        pairs = [pair_sum(pairs[n], pairs[n + 1]) for n in range(0, len(pairs) - 1, 2)] + tail
+    pair = pairs[0]
+    for shift in (4, 2, 1):
+        pair = pair_sum(pair, [pltpu.roll(a, shift, 0) for a in pair])
+    value, error = pair[0], pair[1] + pltpu.roll(pair[0], 127, 1)
+
+    def moment(m):
+        if m == 0:
+            return value, error
+        return pltpu.roll(value, 128 - 12 * m, 1), pltpu.roll(error, 128 - 12 * m, 1)
+
+    m0, m1, m2, m3, m4, m5 = [moment(m) for m in range(MOMENTS)]
+    none = jnp.zeros((8, 128), jnp.float32)
+    one = (jnp.ones((8, 128), jnp.float32), none)
+    alpha0 = m0[0] / m1[0]
+    alpha0_squared = two_product(alpha0, alpha0)
+    norm1 = quadratic(((one, m0), ((-2.0 * alpha0, none), m1), (alpha0_squared, m2)))
+    grow = 1.0 + norm1 / m0[0]
+    curve1 = quadratic(
+        ((two_product(grow, grow), m1), (two_product(-2.0 * grow, alpha0), m2), (alpha0_squared, m3))
+    )
+    alpha1 = norm1 / curve1
     r1 = -(alpha0 + alpha1 * grow)
     r2 = alpha1 * alpha0
-    norm2 = m0 + 2.0 * r1 * m1 + (r1 * r1 + 2.0 * r2) * m2 + 2.0 * r1 * r2 * m3 + r2 * r2 * m4
+    norm2 = quadratic(
+        (
+            (one, m0),
+            ((2.0 * r1, none), m1),
+            (pair_sum(two_product(r1, r1), (2.0 * r2, none)), m2),
+            (two_product(2.0 * r1, r2), m3),
+            (two_product(r2, r2), m4),
+        )
+    )
     beta1 = norm2 / norm1
     p0, p1, p2 = 1.0 + beta1 * grow, r1 - beta1 * alpha0, r2
-    curve2 = (
-        p0 * p0 * m1 + 2.0 * p0 * p1 * m2 + (p1 * p1 + 2.0 * p0 * p2) * m3 + 2.0 * p1 * p2 * m4 + p2 * p2 * m5
+    curve2 = quadratic(
+        (
+            (two_product(p0, p0), m1),
+            (two_product(2.0 * p0, p1), m2),
+            (pair_sum(two_product(p1, p1), two_product(2.0 * p0, p2)), m3),
+            (two_product(2.0 * p1, p2), m4),
+            (two_product(p2, p2), m5),
+        )
     )
     alpha2 = norm2 / curve2
     return alpha0 + alpha1 * grow + alpha2 * p0, alpha2 * p1 - alpha1 * alpha0, alpha2 * p2
 
 
-def finish(layers, sums, near, basis, splat, adjoint, gradient, lam):
+def finish(sums, near, basis, splat, adjoint_hbm, gradient_hbm, adjoint, gradient, lam, sems):
+    layers = 2 * HALO
     lane = tile_iota(1)
+    copies = []
     scale = []
     for c in coefficients(sums):
-        scale.append([jnp.sum(jnp.where(lane == i, c, 0.0), axis=1, keepdims=True) for i in range(3)])
+        scale.append([jnp.sum(jnp.where(lane == 4 * i, c, 0.0), axis=1, keepdims=True) for i in range(3)])
     for i in range(3):
         for x in range(layers + 2):
             for t in range(2):
@@ -212,6 +320,8 @@
                 lam[i, x, t] = value
                 if t == 0 and 0 < x <= layers:
                     adjoint[i, x - 1] = value
+        copies.append(pltpu.make_async_copy(adjoint.at[i], adjoint_hbm.at[i], sems.at[i]))
+        copies[-1].start()
 
     def face(d, here, after, chi_here, chi_after, lam_here, lam_after):
         local = [(1.0 if j == d else 0.0) + (chi_after[j] - chi_here[j]) for j in range(3)]
@@ -266,7 +376,13 @@
                 ]
             )
             gradient[x - 1] = total + z_now[0] + z_prev(z_back)[0]
+            if x % HALO == 0:
+                part = pl.ds(x - HALO, HALO)
+                copies.append(pltpu.make_async_copy(gradient.at[part], gradient_hbm.at[part], sems.at[2 + x // HALO]))
+                copies[-1].start()
         carried = back
+    for copy in copies:
+        copy.wait()
 
 
 def ring_steps(axis):
@@ -275,62 +391,79 @@
     return forward, [(target, source) for source, target in forward]
 
 
+def in_hbm(*arrays):
+    return [pltpu.with_memory_space_constraint(a, pltpu.HBM) for a in arrays]
+
+
 def shards(labels, table, factor, chi, weights):
-    layers, rows, columns = factor.shape
-    assert rows == 8 and columns == 128 and layers % 2 == 0 and layers >= HALO
+    layers = factor.shape[0]
+    assert factor.shape == (2 * HALO, 8, 128)
     peers = lax.axis_size("col") * lax.axis_size("slab")
     f32 = functools.partial(jax.ShapeDtypeStruct, dtype=jnp.float32)
-    pairs = HALO // 2
-
-    own, low_rows, high_rows, splat = pl.pallas_call(
+    scratch = functools.partial(pltpu.VMEM, dtype=jnp.float32)
+    half_block = f32((4, HALO, 8, 128))
+
+    own_low, own_high, low_rows, high_rows, splat = pl.pallas_call(
         prepare,
-        out_shape=(f32((4, layers, 8, 128)), f32((4, layers // 2, 8, 128)), f32((4, layers // 2, 8, 128)), f32((9, 8, 128))),
+        out_shape=(half_block,) * 4 + (f32((9, 8, 128)),),
         in_specs=[HBM] * 5,
-        out_specs=(VMEM,) * 4,
+        out_specs=(VMEM,) * 5,
         scratch_shapes=[
             pltpu.VMEM((layers, 8, 128), jnp.int32),
             pltpu.SMEM((3,), jnp.float32),
-            pltpu.VMEM((layers, 8, 128), jnp.float32),
+            scratch((layers, 8, 128)),
             pltpu.SMEM((3, 3), jnp.float32),
-            pltpu.SemaphoreType.DMA((5,)),
+            pltpu.SemaphoreType.DMA((6,)),
         ],
         compiler_params=PARAMS,
         name="prepare",
-    )(labels, table, factor, chi, weights)
+    )(*in_hbm(labels, table, factor, chi, weights))
 
     forward, backward = ring_steps("slab")
     z_low = lax.ppermute(high_rows, "slab", forward)
     z_high = lax.ppermute(low_rows, "slab", backward)
     forward, backward = ring_steps("col")
-    tail = layers // 2 - pairs
-    x_low = lax.ppermute(
-        jnp.concatenate([own[:, layers - HALO :], z_low[:, tail:], z_high[:, tail:]], axis=1), "col", forward
-    )
-    x_high = lax.ppermute(jnp.concatenate([own[:, :HALO], z_low[:, :pairs], z_high[:, :pairs]], axis=1), "col", backward)
-
-    total = layers + 2 * HALO
+    x_low = lax.ppermute(own_high, "col", forward)
+    x_high = lax.ppermute(own_low, "col", backward)
+
+    ring, low_corner, high_corner = pl.pallas_call(
+        fold,
+        out_shape=(f32((4, layers, 8, 128)), f32((4, 2, 8, 128)), f32((4, 2, 8, 128))),
+        in_specs=[VMEM] * 2,
+        out_specs=(VMEM,) * 3,
+        compiler_params=PARAMS,
+        name="fold",
+    )(z_low, z_high)
+    corner_low = lax.ppermute(high_corner, "col", forward)
+    corner_high = lax.ppermute(low_corner, "col", backward)
+
     near, basis, sums = pl.pallas_call(
-        functools.partial(krylov, layers, peers),
+        functools.partial(krylov, peers),
         out_shape=(f32((4, layers + 2, 2, 8, 128)), f32((3, 3, layers + 2, 2, 8, 128)), f32((peers, 128))),
-        in_specs=[VMEM] * 6,
+        in_specs=[VMEM] * 8,
         out_specs=(VMEM,) * 3,
         scratch_shapes=[
-            pltpu.VMEM((4, total, 8, 128), jnp.float32),
-            pltpu.VMEM((3, total, 2, 8, 128), jnp.float32),
-            pltpu.VMEM((3, 3, total, 2, 8, 128), jnp.float32),
+            scratch((4, 2 * layers, 8, 128)),
+            scratch((3, 2 * layers, 2, 8, 128)),
+            scratch((3, 3, 2 * layers, 2, 8, 128)),
         ],
         compiler_params=PARAMS,
         name="krylov",
-    )(own, z_low, z_high, x_low, x_high, splat)
+    )(own_low, own_high, ring, x_low, x_high, corner_low, corner_high, splat)
 
     gathered = lax.all_to_all(sums, ("col", "slab"), 0, 0, tiled=True)
 
     return pl.pallas_call(
-        functools.partial(finish, layers),
+        finish,
         out_shape=(f32((3, layers, 8, 128)), f32((layers, 8, 128))),
         in_specs=[VMEM] * 4,
-        out_specs=(VMEM,) * 2,
-        scratch_shapes=[pltpu.VMEM((3, layers + 2, 2, 8, 128), jnp.float32)],
+        out_specs=(HBM,) * 2,
+        scratch_shapes=[
+            scratch((3, layers, 8, 128)),
+            scratch((layers, 8, 128)),
+            scratch((3, layers + 2, 2, 8, 128)),
+            pltpu.SemaphoreType.DMA((5,)),
+        ],
         compiler_params=PARAMS,
         name="finish",
     )(gathered, near, basis, splat)

time: 35 us -> 29.5 us (0.84)
  local copies, waits for them, and re-layouts: 3.76 us -> 0 us
  waiting for transfers between devices: 5.54 us -> 3.51 us
  starting transfers between devices: 7.96 us -> 8.57 us
    unnamed x10 -> x0, local copies, waits for them, and re-layouts: 3.74 us -> none
    ppermute x2 -> x4, waiting for transfers between devices: 3 us -> 1.6 us  [the longest x1 1.44 us: shards(): corner_low = lax.ppermute(high_corner, 'col', forward)]
    ppermute x1, waiting for transfers between devices: 2.22 us -> 1.58 us  [shards(): z_low = lax.ppermute(high_rows, 'slab', forward)]
    ppermute x2 -> x4, starting transfers between devices: 1.83 us -> 2.44 us  [the longest x1 1.73 us: shards(): corner_high = lax.ppermute(low_corner, 'col', backward)]
    pallas_call x3 -> x4, Pallas kernels: 3.57 us -> 3.6 us  [the longest x1 1.43 us: shards(): pl.pallas_call(functools.partial(krylov, peers), out_shape=(f32((4, layer...]
  transfers between devices with their start and end apart: 4 -> 6, of which waited for: 4 -> 4; matrix products, arithmetic and copies ran while one was open for 0% -> 0% of each run, Pallas kernels for 0% -> 0%
where the time goes in v3:
time: 29.5 us; the launch traced here: 29.3 us
  blocking collectives  13 us (44%)
  starting transfers between devices  8.57 us (29%)
  Pallas kernels  3.6 us (12%)
  waiting for transfers between devices  3.51 us (12%)
  between operations  0.66 us (2%)
    all_to_all x1, blocking collectives, shards(): gathered = lax.all_to_all(sums, ('col', 'slab'), 0, 0, tiled=True)  13 us
    ppermute x1, starting transfers between devices, shards(): z_high = lax.ppermute(low_rows, 'slab', backward)  3.1 us
    ppermute x1, starting transfers between devices, shards(): z_low = lax.ppermute(high_rows, 'slab', forward)  3.02 us
    ppermute x1, starting transfers between devices, shards(): corner_high = lax.ppermute(low_corner, 'col', backward)  1.73 us
    ppermute x1, waiting for transfers between devices, shards(): z_low = lax.ppermute(high_rows, 'slab', forward)  1.58 us
    ppermute x1, waiting for transfers between devices, shards(): corner_low = lax.ppermute(high_corner, 'col', forward)  1.44 us
    pallas_call x1, Pallas kernels, shards(): pl.pallas_call(functools.partial(krylov, peers), out_shape=(f32((4, layer...  1.43 us
    pallas_call x1, Pallas kernels, shards(): pl.pallas_call(finish, out_shape=(f32((3, layers, 8, 128)), f32((layers,...  1.21 us
  transfers between devices with their start and end apart: 6, of which 4 were waited for; matrix products, arithmetic and copies ran while one was open for 0% of the time, Pallas kernels for 0%

profile of v3, /device:TPU:0, one launch (start us, length us, event | category | flops | bytes accessed | tf_op | source)
XLA Modules:
  0.0 29.3 jit_solution(6884846831165505334)
XLA Ops:
  0.6 0.9 %prepare.1 = (f32[4,4,8,128]{3,2,1,0:T(8,128)S(1)}, f32[4,4,8,128]{3,2,1,0:T(8,128)S(1)}, f32[4,4,8,128]{3,2,1,0:T(8,128)S(1)}, f32[4,4,8,128]{3,2,1,0:T(8,128)S(1)}, f32[9,8,128]{2,1,0:T(8,128)S(1)}) custom-call(s32[8,8,128]{2,1,0:T(8,128)} %labels_hbm.1, f32[3]{0:T(128)} %table_hbm.1, f32[8,8,128]{2,1,0:T(8,128)} %factor_hbm.1, f32[3,8,8,128]{3,2,1,0:T(8,128)} %chi_hbm.1, ...), custom_call_target="tpu_custom_call" | custom-call | tf_op jit(solution)/shard_map/prepare/pallas_call | solution.py:406
  1.6 3.0 %collective-permute-start = (f32[4,4,8,128]{3,2,1,0:T(8,128)S(1)}, f32[4,4,8,128]{3,2,1,0:T(8,128)S(1)}, u32[]{:S(2)}, u32[]{:S(2)}) collective-permute-start(f32[4,4,8,128]{3,2,1,0:T(8,128)S(1)} %get-tuple-element.15), channel_id=1, source_target_pairs={{0,1},{1,2},{2,3},{3,4},{4,5},{5,6},{6,7},{7,0},{8,9},{9,10},{10,1... | collective-permute-start | bytes 196616 | tf_op jit(solution)/shard_map/ppermute | solution.py:423
  4.6 3.1 %collective-permute-start.1 = (f32[4,4,8,128]{3,2,1,0:T(8,128)S(1)}, f32[4,4,8,128]{3,2,1,0:T(8,128)S(1)}, u32[]{:S(2)}, u32[]{:S(2)}) collective-permute-start(f32[4,4,8,128]{3,2,1,0:T(8,128)S(1)} %get-tuple-element.16), channel_id=1, source_target_pairs={{1,0},{2,1},{3,2},{4,3},{5,4},{6,5},{7,6},{0,7},{9,8},{10,9},{11,1... | collective-permute-start | bytes 196616 | tf_op jit(solution)/shard_map/ppermute | solution.py:424
  7.7 0.7 %collective-permute-start.3 = (f32[4,4,8,128]{3,2,1,0:T(8,128)S(1)}, f32[4,4,8,128]{3,2,1,0:T(8,128)S(1)}, u32[]{:S(2)}, u32[]{:S(2)}) collective-permute-start(f32[4,4,8,128]{3,2,1,0:T(8,128)S(1)} %get-tuple-element.13.own_low), channel_id=1, source_target_pairs={{8,0},{16,8},{24,16},{0,24},{9,1},{17,9},{25,17},{1,25},{10,2},{18... | collective-permute-start | bytes 196616 | tf_op jit(solution)/shard_map/ppermute | solution.py:427
  8.4 0.0 collective-permute-start.2
  8.4 1.6 %collective-permute-done.z_low = f32[4,4,8,128]{3,2,1,0:T(8,128)S(1)} collective-permute-done((f32[4,4,8,128]{3,2,1,0:T(8,128)S(1)}, f32[4,4,8,128]{3,2,1,0:T(8,128)S(1)}, u32[]{:S(2)}, u32[]{:S(2)}) %collective-permute-start) | collective-permute-done | bytes 65568 | tf_op jit(solution)/shard_map/ppermute | solution.py:423
  9.9 0.3 %collective-permute-done.1.z_high = f32[4,4,8,128]{3,2,1,0:T(8,128)S(1)} collective-permute-done((f32[4,4,8,128]{3,2,1,0:T(8,128)S(1)}, f32[4,4,8,128]{3,2,1,0:T(8,128)S(1)}, u32[]{:S(2)}, u32[]{:S(2)}) %collective-permute-start.1) | collective-permute-done | bytes 65568 | tf_op jit(solution)/shard_map/ppermute | solution.py:424
  10.3 0.1 collective-permute-start.4
  10.4 1.7 %collective-permute-start.5 = (f32[4,2,8,128]{3,2,1,0:T(8,128)S(1)}, f32[4,2,8,128]{3,2,1,0:T(8,128)S(1)}, u32[]{:S(2)}, u32[]{:S(2)}) collective-permute-start(f32[4,2,8,128]{3,2,1,0:T(8,128)S(1)} %get-tuple-element.19), channel_id=1, source_target_pairs={{8,0},{16,8},{24,16},{0,24},{9,1},{17,9},{25,17},{1,25},{10,2},{18... | collective-permute-start | bytes 98312 | tf_op jit(solution)/shard_map/ppermute | solution.py:438
  12.1 0.0 collective-permute-done.3.x_high
  12.1 0.1 collective-permute-done.2.x_low
  12.2 1.4 %collective-permute-done.4.corner_low = f32[4,2,8,128]{3,2,1,0:T(8,128)S(1)} collective-permute-done((f32[4,2,8,128]{3,2,1,0:T(8,128)S(1)}, f32[4,2,8,128]{3,2,1,0:T(8,128)S(1)}, u32[]{:S(2)}, u32[]{:S(2)}) %collective-permute-start.4) | collective-permute-done | bytes 32800 | tf_op jit(solution)/shard_map/ppermute | solution.py:437
  13.7 0.0 collective-permute-done.5.corner_high
  13.7 1.4 %krylov.1 = (f32[4,10,2,8,128]{4,3,2,1,0:T(8,128)S(1)}, f32[3,3,10,2,8,128]{5,4,3,2,1,0:T(8,128)S(1)}, f32[32,128]{1,0:T(8,128)S(1)}) custom-call(f32[4,4,8,128]{3,2,1,0:T(8,128)S(1)} %get-tuple-element.13.own_low, f32[4,4,8,128]{3,2,1,0:T(8,128)S(1)} %get-tuple-element.14.own_high, f32[4,8,8,128]{3,2,1,0:T(8,128)S(1)} %get-tuple-element.17.z_ring, ...), custom_call_target="tpu_custom_call" | custom-call | tf_op jit(solution)/shard_map/krylov/pallas_call | solution.py:440
  15.1 13.0 %all_to_all.11 = f32[32,1,128]{2,1,0:T(1,128)S(1)} all-to-all(f32[32,1,128]{2,1,0:T(1,128)S(1)} %bitcast.5), channel_id=1, replica_groups=mesh['col'=4,'slab'=8] {'col','slab'}, dimensions={0} | all-to-all | bytes 32768 | tf_op jit(solution)/shard_map/all_to_all | solution.py:454
  28.1 1.2 %finish.1 = (f32[3,8,8,128]{3,2,1,0:T(8,128)}, f32[8,8,128]{2,1,0:T(8,128)}) custom-call(f32[32,128]{1,0:T(8,128)S(1)} %bitcast.4, f32[4,10,2,8,128]{4,3,2,1,0:T(8,128)S(1)} %get-tuple-element.22.near, f32[3,3,10,2,8,128]{5,4,3,2,1,0:T(8,128)S(1)} %get-tuple-element.23.basis, f32[9,8,128]{2,1,0:T(8,128)S(1)} %get-tuple-element.20.splat), custom_call_target="tpu_custom_call" | custom-call | tf_op jit(solution)/shard_map/finish/pallas_call | solution.py:456
  (1 shorter events, 0.0 us)
Async XLA Ops:
  1.6 8.4 %collective-permute-start = (f32[4,4,8,128]{3,2,1,0:T(8,128)S(1)}, f32[4,4,8,128]{3,2,1,0:T(8,128)S(1)}, u32[]{:S(2)}, u32[]{:S(2)}) collective-permute-start(f32[4,4,8,128]{3,2,1,0:T(8,128)S(1)} %get-tuple-element.15), channel_id=1, source_target_pairs={{0,1},{1,2},{2,3},{3,4},{4,5},{5,6},{6,7},{7,0},{8,9},{9,10},{10,1... | collective-permute-start | bytes 196616 | tf_op jit(solution)/shard_map/ppermute | solution.py:423
  4.6 5.7 %collective-permute-start.1 = (f32[4,4,8,128]{3,2,1,0:T(8,128)S(1)}, f32[4,4,8,128]{3,2,1,0:T(8,128)S(1)}, u32[]{:S(2)}, u32[]{:S(2)}) collective-permute-start(f32[4,4,8,128]{3,2,1,0:T(8,128)S(1)} %get-tuple-element.16), channel_id=1, source_target_pairs={{1,0},{2,1},{3,2},{4,3},{5,4},{6,5},{7,6},{0,7},{9,8},{10,9},{11,1... | collective-permute-start | bytes 196616 | tf_op jit(solution)/shard_map/ppermute | solution.py:424
  7.7 4.4 %collective-permute-start.3 = (f32[4,4,8,128]{3,2,1,0:T(8,128)S(1)}, f32[4,4,8,128]{3,2,1,0:T(8,128)S(1)}, u32[]{:S(2)}, u32[]{:S(2)}) collective-permute-start(f32[4,4,8,128]{3,2,1,0:T(8,128)S(1)} %get-tuple-element.13.own_low), channel_id=1, source_target_pairs={{8,0},{16,8},{24,16},{0,24},{9,1},{17,9},{25,17},{1,25},{10,2},{18... | collective-permute-start | bytes 196616 | tf_op jit(solution)/shard_map/ppermute | solution.py:427
  8.4 3.9 %collective-permute-start.2 = (f32[4,4,8,128]{3,2,1,0:T(8,128)S(1)}, f32[4,4,8,128]{3,2,1,0:T(8,128)S(1)}, u32[]{:S(2)}, u32[]{:S(2)}) collective-permute-start(f32[4,4,8,128]{3,2,1,0:T(8,128)S(1)} %get-tuple-element.14.own_high), channel_id=1, source_target_pairs={{0,8},{8,16},{16,24},{24,0},{1,9},{9,17},{17,25},{25,1},{2,10},{10... | collective-permute-start | bytes 196616 | tf_op jit(solution)/shard_map/ppermute | solution.py:426
  10.3 3.4 %collective-permute-start.4 = (f32[4,2,8,128]{3,2,1,0:T(8,128)S(1)}, f32[4,2,8,128]{3,2,1,0:T(8,128)S(1)}, u32[]{:S(2)}, u32[]{:S(2)}) collective-permute-start(f32[4,2,8,128]{3,2,1,0:T(8,128)S(1)} %get-tuple-element.18), channel_id=1, source_target_pairs={{0,8},{8,16},{16,24},{24,0},{1,9},{9,17},{17,25},{25,1},{2,10},{10... | collective-permute-start | bytes 98312 | tf_op jit(solution)/shard_map/ppermute | solution.py:437
  10.4 3.3 %collective-permute-start.5 = (f32[4,2,8,128]{3,2,1,0:T(8,128)S(1)}, f32[4,2,8,128]{3,2,1,0:T(8,128)S(1)}, u32[]{:S(2)}, u32[]{:S(2)}) collective-permute-start(f32[4,2,8,128]{3,2,1,0:T(8,128)S(1)} %get-tuple-element.19), channel_id=1, source_target_pairs={{8,0},{16,8},{24,16},{0,24},{9,1},{17,9},{25,17},{1,25},{10,2},{18... | collective-permute-start | bytes 98312 | tf_op jit(solution)/shard_map/ppermute | solution.py:438

commit v4 on v3

v4 whole, which is shorter than its diff:
```python
import functools

import jax
import jax.numpy as jnp
from jax import lax
from jax.experimental import pallas as pl
from jax.experimental.pallas import tpu as pltpu
from jax.sharding import PartitionSpec as P


mass_shift = 0.01
HALO = 4
MOMENTS = 6

VMEM = pl.BlockSpec(memory_space=pltpu.VMEM)
HBM = pl.BlockSpec(memory_space=pltpu.HBM)
PARAMS = pltpu.CompilerParams(vmem_limit_bytes=8 * 2**20)


def tile_iota(axis):
    return lax.broadcasted_iota(jnp.int32, (8, 128), axis)


def y_next(tile):
    return pltpu.roll(tile, 127, 1)


def y_prev(tile):
    return pltpu.roll(tile, 1, 1)


def z_next(pair):
    last = tile_iota(0) == 7
    first, second = (pltpu.roll(tile, 7, 0) for tile in pair)
    return jnp.where(last, second, first), jnp.where(last, first, second)


def z_prev(pair):
    top = tile_iota(0) == 0
    first, second = (pltpu.roll(tile, 1, 0) for tile in pair)
    return jnp.where(top, second, first), jnp.where(top, first, second)


def parity(axis):
    return lax.rem(lax.axis_index(axis), 2)


def choose(odd, if_even, if_odd):
    return jnp.where(jnp.full((8, 128), odd, jnp.int32) == 0, if_even, if_odd)


def prepare(
    labels_hbm, table_hbm, factor_hbm, chi_hbm, weights_hbm, own, x_a, x_b, z_a, z_b, splat,
    labels, table, factor, weights, sems,
):
    odd_col = parity("col")
    start_a, start_b = HALO * (1 - odd_col), HALO * odd_col
    moves = (
        (labels_hbm, labels),
        (table_hbm, table),
        (factor_hbm, factor),
        (weights_hbm, weights),
        (chi_hbm, own.at[pl.ds(0, 3)]),
        (chi_hbm.at[:, pl.ds(start_a, HALO)], x_a.at[pl.ds(0, 3)]),
        (chi_hbm.at[:, pl.ds(start_b, HALO)], x_b.at[pl.ds(0, 3)]),
    )
    copies = [pltpu.make_async_copy(source, target, sems.at[n]) for n, (source, target) in enumerate(moves)]
    for copy in copies:
        copy.start()
    for copy in copies:
        copy.wait()
    for x in range(2 * HALO):
        label = labels[x]
        own[3, x] = jnp.where(label == 0, table[0], jnp.where(label == 1, table[1], table[2])) * factor[x]
    for x in range(HALO):
        low, high = own[3, x], own[3, HALO + x]
        x_a[3, x] = choose(odd_col, high, low)
        x_b[3, x] = choose(odd_col, low, high)
    for i in range(3):
        for j in range(3):
            splat[3 * i + j] = jnp.full((8, 128), weights[i, j], jnp.float32)
    odd_slab = parity("slab")
    half = tile_iota(0) < 4
    for f in range(4):
        for i in range(HALO):
            even, odd = own[f, 2 * i], own[f, 2 * i + 1]
            low_rows = jnp.where(half, even, pltpu.roll(odd, 4, 0))
            high_rows = jnp.where(half, pltpu.roll(even, 4, 0), odd)
            z_a[f, i] = choose(odd_slab, high_rows, low_rows)
            z_b[f, i] = choose(odd_slab, low_rows, high_rows)


def fold(z_a, z_b, ring, corner_a, corner_b):
    odd_col, odd_slab = parity("col"), parity("slab")
    half = tile_iota(0) < 4
    outer = (tile_iota(0) < 2) | (tile_iota(0) >= 6)

    def packed(first, second, third):
        return first, jnp.where(outer, second, jnp.where(half, pltpu.roll(third, 2, 0), pltpu.roll(third, 6, 0)))

    for f in range(4):
        tiles = []
        for i in range(HALO):
            up, down = choose(odd_slab, z_a[f, i], z_b[f, i]), choose(odd_slab, z_b[f, i], z_a[f, i])
            tiles.append(jnp.where(half, up, pltpu.roll(down, 4, 0)))
            tiles.append(jnp.where(half, pltpu.roll(up, 4, 0), down))
        for x, tile in enumerate(tiles):
            ring[f, x] = tile
        for n, (low, high) in enumerate(zip(packed(*tiles[:3]), packed(*tiles[:-4:-1]))):
            corner_a[f, n] = choose(odd_col, high, low)
            corner_b[f, n] = choose(odd_col, low, high)


def two_sum(a, b):
    total = a + b
    part = total - a
    return total, (a - (total - part)) + (b - part)


def two_product(a, b):
    product = a * b
    a_top, b_top = [4097.0 * v - (4097.0 * v - v) for v in (a, b)]
    a_rest, b_rest = a - a_top, b - b_top
    return product, ((a_top * b_top - product) + a_top * b_rest + a_rest * b_top) + a_rest * b_rest


def pair_sum(a, b):
    total, error = two_sum(a[0], b[0])
    return total, error + (a[1] + b[1])


def pair_product(a, b):
    product, error = two_product(a[0], b[0])
    return product, error + (a[0] * b[1] + a[1] * b[0])


def total_row(tiles):
    row = tile_iota(0)
    lane = tile_iota(1)
    pairs = [(tile, jnp.zeros((8, 128), jnp.float32)) for tile in tiles]
    place = [[n] for n in range(len(tiles))]
    for width in (4, 2, 1):
        lower = (row & width) == 0
        merged, spots = [], []
        for n in range(0, len(pairs), 2):
            first, second = pairs[n], pairs[min(n + 1, len(pairs) - 1)]
            kept = [jnp.where(lower, a, b) for a, b in zip(first, second)]
            moved = [jnp.where(lower, pltpu.roll(a, 8 - width, 0), pltpu.roll(b, width, 0)) for a, b in zip(first, second)]
            merged.append(pair_sum(kept, moved))
            spots.append((place[n], place[n + 1] if n + 1 < len(pairs) else None))
        pairs, place = merged, spots
    result = jnp.zeros((8, 128), jnp.float32)

    def home(spot, at, width):
        if spot is None:
            return
        if len(spot) == 1:
            yield spot[0], at
            return
        yield from home(spot[0], at, 2 * width)
        yield from home(spot[1], at + width, 2 * width)

    for pair, spot in zip(pairs, place):
        for shift in (64, 32, 16, 8, 4, 2, 1):
            pair = pair_sum(pair, [pltpu.roll(a, shift, 1) for a in pair])
        for n, at in home(spot, 0, 1):
            result = jnp.where((row == at) & (lane == 4 * n), pair[0], result)
            result = jnp.where((row == at) & (lane == 4 * n + 1), pair[1], result)
    return jnp.sum(result, axis=0, keepdims=True)


LAYERS = 2 * HALO
TOTAL = 2 * LAYERS


def inner(k):
    return range(HALO + 1 + k, HALO + LAYERS - 1 - k)


def harmonic(here, after):
    return 2.0 * here * after / (here + after)


def out_flow(here, after, x_cond, z_cond, y_cond, offset, flows):
    beside = z_next(here)
    z_flux = [z_cond[t] * (offset[1] + (beside[t] - here[t])) for t in range(2)]
    z_back = z_prev(z_flux)
    added = []
    for t in range(2):
        x_flux = x_cond[t] * (offset[0] + (after[t] - here[t]))
        y_flux = y_cond[t] * (offset[2] + (y_next(here[t]) - here[t]))
        before = flows[t]
        flows[t] = x_flux
        added.append((before - x_flux) + (z_back[t] - z_flux[t]) + (y_prev(y_flux) - y_flux))
    return added


def both(read, *index):
    return [read(*index, t) for t in range(2)]


def add_source(layers, grid, cond, splat, field):
    offset = [[1.0 if d == j else 0.0 for d in range(3)] for j in range(3)]
    flows = []
    for j in range(3):
        here, after = both(grid, j, layers[0] - 1), both(grid, j, layers[0])
        flows.append([cond(0, layers[0] - 1, t) * (offset[j][0] + (after[t] - here[t])) for t in range(2)])
    for x in layers:
        conds = [both(cond, d, x) for d in range(3)]
        drive = [
            out_flow(both(grid, j, x), both(grid, j, x + 1), *conds, offset[j], flows[j]) for j in range(3)
        ]
        for i in range(3):
            for t in range(2):
                field[0, i, x, t] = (
                    splat[3 * i] * drive[0][t] + splat[3 * i + 1] * drive[1][t] + splat[3 * i + 2] * drive[2][t]
                )


def applied(k, i, layers, v, cond):
    here, after = both(v, k, i, layers[0] - 1), both(v, k, i, layers[0])
    flow = [cond(0, layers[0] - 1, t) * (after[t] - here[t]) for t in range(2)]
    for x in layers:
        here, after = both(v, k, i, x), both(v, k, i, x + 1)
        added = out_flow(here, after, *[both(cond, d, x) for d in range(3)], (0.0, 0.0, 0.0), flow)
        yield x, [mass_shift * here[t] + added[t] for t in range(2)]


def face_parts(d, here, after, chi_here, chi_after, splat):
    local = [(1.0 if j == d else 0.0) + (chi_after[j] - chi_here[j]) for j in range(3)]
    energy = None
    for i in range(3):
        part = local[i] * (splat[3 * i] * local[0] + splat[3 * i + 1] * local[1] + splat[3 * i + 2] * local[2])
        energy = part if energy is None else energy + part
    inverse = 1.0 / (here + after)
    share = after * inverse
    rest = here * inverse
    now, back = 2.0 * share * share, 2.0 * rest * rest
    return [energy * now] + [value * now for value in local], [energy * back] + [value * back for value in local]


def early(own, ring, x_a, x_b, splat, halo, cond, field, base, slopes):
    odd_col = parity("col")
    for f in range(4):
        for n in range(HALO):
            halo[f, n] = choose(odd_col, x_b[f, n], x_a[f, n])
            halo[f, HALO + n] = choose(odd_col, x_a[f, n], x_b[f, n])

    def grid(f, x, t):
        if t == 1:
            return ring[f, x - HALO]
        if x < HALO:
            return halo[f, x]
        return own[f, x - HALO] if x < HALO + LAYERS else halo[f, x - LAYERS]

    for x in range(TOTAL):
        here = grid(3, x, 0)
        cond[2, x, 0] = harmonic(here, y_next(here))
        if x + 1 < TOTAL:
            cond[0, x, 0] = harmonic(here, grid(3, x + 1, 0))
        if HALO <= x < HALO + LAYERS:
            other = grid(3, x, 1)
            cond[2, x, 1] = harmonic(other, y_next(other))
            if x + 1 < HALO + LAYERS:
                cond[0, x, 1] = harmonic(other, grid(3, x + 1, 1))
            for t, (tile, beside) in enumerate(zip((here, other), z_next((here, other)))):
                cond[1, x, t] = harmonic(tile, beside)

    def ready(*index):
        return cond[index]

    def v(*index):
        return field[index]

    add_source(inner(0), grid, ready, splat, field)
    for k in (1, 2):
        for i in range(3):
            for x, value in applied(k - 1, i, inner(k), v, ready):
                field[k, i, x, 0], field[k, i, x, 1] = value

    carried = None
    for x in range(HALO - 1, HALO + LAYERS):
        here, after = [[grid(f, n, 0) for f in range(4)] for n in (x, x + 1)]
        now, back = face_parts(0, here[3], after[3], here[:3], after[:3], splat)
        if carried is not None:
            beside = [y_next(tile) for tile in here]
            y_now, y_back = face_parts(2, here[3], beside[3], here[:3], beside[:3], splat)
            y_back = [y_prev(tile) for tile in y_back]
            pairs = [(here[f], grid(f, x, 1)) for f in range(4)]
            nexts = [z_next(pair) for pair in pairs]
            z_now, z_back = zip(
                *[
                    face_parts(1, pairs[3][t], nexts[3][t], [p[t] for p in pairs[:3]], [p[t] for p in nexts[:3]], splat)
                    for t in range(2)
                ]
            )
            z_now, z_back = z_now[0], [z_prev(pair)[0] for pair in zip(*z_back)]
            sides = ((now, carried), (z_now, z_back), (y_now, y_back))
            base[x - HALO] = sum(side[0] for pair in sides for side in pair)
            for d in range(3):
                for n in range(2):
                    for j in range(3):
                        slopes[d, n, j, x - HALO] = sides[d][n][1 + j]
        carried = back


def krylov(peers, own, z_ring, halo, corner_a, corner_b, splat, early_cond, early_field, field, sums, ring, cond):
    odd_col = parity("col")
    half = tile_iota(0) < 4
    for f in range(4):
        tiles = [(corner_a[f, n], corner_b[f, n]) for n in range(2)]
        low = [choose(odd_col, b, a) for a, b in tiles]
        high = [choose(odd_col, a, b) for a, b in tiles]
        for (first, shared), spots in ((low, (3, 2, 1, 0)), (high, (4, 5, 6, 7))):
            third = jnp.where(half, pltpu.roll(shared, 6, 0), pltpu.roll(shared, 2, 0))
            for spot, tile in zip(spots, (first, shared, third, third)):
                ring[f, spot] = tile

    def grid(f, x, t):
        if x < HALO:
            return (halo, ring)[t][f, x]
        if x < HALO + LAYERS:
            return (own, z_ring)[t][f, x - HALO]
        return (halo, ring)[t][f, x - LAYERS]

    def is_early(d, x, t):
        return HALO <= x < HALO + LAYERS - (1 if d == 0 and t == 1 else 0) or (t == 0 and d != 1)

    def ready(d, x, t):
        return (early_cond if is_early(d, x, t) else cond)[d, x, t]

    def v(k, i, x, t):
        return (early_field if x in inner(k) else field)[k, i, x, t]

    for x in range(TOTAL - 1):
        here = both(grid, 3, x)
        if not is_early(0, x, 1):
            cond[0, x, 1] = harmonic(here[1], grid(3, x + 1, 1))
        if not is_early(2, x, 1):
            cond[2, x, 1] = harmonic(here[1], y_next(here[1]))
        if not is_early(1, x, 1):
            for t, beside in enumerate(z_next(here)):
                cond[1, x, t] = harmonic(here[t], beside)

    def outer(k):
        done = inner(k)
        return range(1 + k, done.start), range(done.stop, TOTAL - 1 - k)

    for layers in outer(0):
        add_source(layers, grid, ready, splat, field)
    for k in (1, 2):
        for layers in outer(k):
            for i in range(3):
                for x, value in applied(k - 1, i, layers, v, ready):
                    field[k, i, x, 0], field[k, i, x, 1] = value

    partial = [jnp.zeros((8, 128), jnp.float32) for _ in range(3 * MOMENTS)]
    for i in range(3):
        for x, value in applied(2, i, range(HALO, HALO + LAYERS), v, ready):
            tiles = [v(k, i, x, 0) for k in range(3)] + [value[0]]
            for m, (a, b) in enumerate(((0, 0), (0, 1), (1, 1), (1, 2), (2, 2), (2, 3))):
                partial[3 * m + i] = partial[3 * m + i] + tiles[a] * tiles[b]
    sums[...] = jnp.broadcast_to(total_row(partial), (peers, 128))


def quadratic(terms):
    products = [pair_product(a, b) for a, b in terms]
    total = products[0]
    for product in products[1:]:
        total = pair_sum(total, product)
    return total[0] + total[1]


def coefficients(sums):
    count = sums.shape[0] // 8
    pairs = [(sums[8 * n : 8 * n + 8], jnp.zeros((8, 128), jnp.float32)) for n in range(count)]
    while len(pairs) > 1:
        tail = pairs[len(pairs) // 2 * 2 :]
        pairs = [pair_sum(pairs[n], pairs[n + 1]) for n in range(0, len(pairs) - 1, 2)] + tail
    pair = pairs[0]
    for shift in (4, 2, 1):
        pair = pair_sum(pair, [pltpu.roll(a, shift, 0) for a in pair])
    value, error = pair[0], pair[1] + pltpu.roll(pair[0], 127, 1)

    def moment(m):
        if m == 0:
            return value, error
        return pltpu.roll(value, 128 - 12 * m, 1), pltpu.roll(error, 128 - 12 * m, 1)

    m0, m1, m2, m3, m4, m5 = [moment(m) for m in range(MOMENTS)]
    none = jnp.zeros((8, 128), jnp.float32)
    one = (jnp.ones((8, 128), jnp.float32), none)
    alpha0 = m0[0] / m1[0]
    alpha0_squared = two_product(alpha0, alpha0)
    norm1 = quadratic(((one, m0), ((-2.0 * alpha0, none), m1), (alpha0_squared, m2)))
    grow = 1.0 + norm1 / m0[0]
    curve1 = quadratic(
        ((two_product(grow, grow), m1), (two_product(-2.0 * grow, alpha0), m2), (alpha0_squared, m3))
    )
    alpha1 = norm1 / curve1
    r1 = -(alpha0 + alpha1 * grow)
    r2 = alpha1 * alpha0
    norm2 = quadratic(
        (
            (one, m0),
            ((2.0 * r1, none), m1),
            (pair_sum(two_product(r1, r1), (2.0 * r2, none)), m2),
            (two_product(2.0 * r1, r2), m3),
            (two_product(r2, r2), m4),
        )
    )
    beta1 = norm2 / norm1
    p0, p1, p2 = 1.0 + beta1 * grow, r1 - beta1 * alpha0, r2
    curve2 = quadratic(
        (
            (two_product(p0, p0), m1),
            (two_product(2.0 * p0, p1), m2),
            (pair_sum(two_product(p1, p1), two_product(2.0 * p0, p2)), m3),
            (two_product(2.0 * p1, p2), m4),
            (two_product(p2, p2), m5),
        )
    )
    alpha2 = norm2 / curve2
    return alpha0 + alpha1 * grow + alpha2 * p0, alpha2 * p1 - alpha1 * alpha0, alpha2 * p2


def finish(sums, early_field, field, base, slopes, adjoint_hbm, gradient_hbm, adjoint, gradient, lam, sems):
    lane = tile_iota(1)
    copies = []
    scale = []
    for c in coefficients(sums):
        scale.append([jnp.sum(jnp.where(lane == 4 * i, c, 0.0), axis=1, keepdims=True) for i in range(3)])
    for i in range(3):
        for x in range(LAYERS + 2):
            for t in range(2):
                if t == 1 and x in (0, LAYERS + 1):
                    continue
                at = x + HALO - 1
                v = [(early_field if at in inner(k) else field)[k, i, at, t] for k in range(3)]
                value = scale[0][i] * v[0] + scale[1][i] * v[1] + scale[2][i] * v[2]
                lam[i, x, t] = value
                if t == 0 and 0 < x <= LAYERS:
                    adjoint[i, x - 1] = value
        copies.append(pltpu.make_async_copy(adjoint.at[i], adjoint_hbm.at[i], sems.at[i]))
        copies[-1].start()

    for x in range(1, LAYERS + 1):
        total = base[x - 1]
        for j in range(3):
            pair = (lam[j, x, 0], lam[j, x, 1])
            here = pair[0]
            around = (
                (lam[j, x + 1, 0], lam[j, x - 1, 0]),
                (z_next(pair)[0], z_prev(pair)[0]),
                (y_next(here), y_prev(here)),
            )
            for d, (after, before) in enumerate(around):
                total = total - (after - here) * slopes[d, 0, j, x - 1] - (here - before) * slopes[d, 1, j, x - 1]
        gradient[x - 1] = total
        if x % HALO == 0:
            part = pl.ds(x - HALO, HALO)
            copies.append(pltpu.make_async_copy(gradient.at[part], gradient_hbm.at[part], sems.at[2 + x // HALO]))
            copies[-1].start()
    for copy in copies:
        copy.wait()


def swap_a(axis):
    return [(i, i ^ 1) for i in range(lax.axis_size(axis))]


def swap_b(axis):
    count = lax.axis_size(axis)
    return [(i, (i + 1 if i % 2 else i - 1) % count) for i in range(count)]


def in_hbm(*arrays):
    return [pltpu.with_memory_space_constraint(a, pltpu.HBM) for a in arrays]


def shards(labels, table, factor, chi, weights):
    assert factor.shape == (LAYERS, 8, 128)
    assert lax.axis_size("col") % 2 == 0 and lax.axis_size("slab") % 2 == 0
    peers = lax.axis_size("col") * lax.axis_size("slab")
    f32 = functools.partial(jax.ShapeDtypeStruct, dtype=jnp.float32)
    scratch = functools.partial(pltpu.VMEM, dtype=jnp.float32)
    block = (4, LAYERS, 8, 128)
    half_block = f32((4, HALO, 8, 128))
    corner = f32((4, 2, 8, 128))
    fields = f32((3, 3, TOTAL, 2, 8, 128))

    own, x_a, x_b, z_a, z_b, splat = pl.pallas_call(
        prepare,
        out_shape=(f32(block),) + (half_block,) * 4 + (f32((9, 8, 128)),),
        in_specs=[HBM] * 5,
        out_specs=(VMEM,) * 6,
        scratch_shapes=[
            pltpu.VMEM((LAYERS, 8, 128), jnp.int32),
            pltpu.SMEM((3,), jnp.float32),
            scratch((LAYERS, 8, 128)),
            pltpu.SMEM((3, 3), jnp.float32),
            pltpu.SemaphoreType.DMA((7,)),
        ],
        compiler_params=PARAMS,
        name="prepare",
    )(*in_hbm(labels, table, factor, chi, weights))

    z_b = lax.ppermute(z_b, "slab", swap_b("slab"))
    z_a = lax.ppermute(z_a, "slab", swap_a("slab"))
    x_b = lax.ppermute(x_b, "col", swap_b("col"))
    x_a = lax.ppermute(x_a, "col", swap_a("col"))

    ring, corner_a, corner_b = pl.pallas_call(
        fold,
        out_shape=(f32(block), corner, corner),
        in_specs=[VMEM] * 2,
        out_specs=(VMEM,) * 3,
        compiler_params=PARAMS,
        name="fold",
    )(z_a, z_b)
    corner_b = lax.ppermute(corner_b, "col", swap_b("col"))
    corner_a = lax.ppermute(corner_a, "col", swap_a("col"))

    halo, cond, early_field, base, slopes = pl.pallas_call(
        early,
        out_shape=(
            f32(block),
            f32((3, TOTAL, 2, 8, 128)),
            fields,
            f32((LAYERS, 8, 128)),
            f32((3, 2, 3, LAYERS, 8, 128)),
        ),
        in_specs=[VMEM] * 5,
        out_specs=(VMEM,) * 5,
        compiler_params=PARAMS,
        name="early",
    )(own, ring, x_a, x_b, splat)

    field, sums = pl.pallas_call(
        functools.partial(krylov, peers),
        out_shape=(fields, f32((peers, 128))),
        in_specs=[VMEM] * 8,
        out_specs=(VMEM,) * 2,
        scratch_shapes=[scratch(block), scratch((3, TOTAL, 2, 8, 128))],
        compiler_params=PARAMS,
        name="krylov",
    )(own, ring, halo, corner_a, corner_b, splat, cond, early_field)

    gathered = lax.all_to_all(sums, ("col", "slab"), 0, 0, tiled=True)

    return pl.pallas_call(
        finish,
        out_shape=(f32((3, LAYERS, 8, 128)), f32((LAYERS, 8, 128))),
        in_specs=[VMEM] * 5,
        out_specs=(HBM,) * 2,
        scratch_shapes=[
            scratch((3, LAYERS, 8, 128)),
            scratch((LAYERS, 8, 128)),
            scratch((3, LAYERS + 2, 2, 8, 128)),
            pltpu.SemaphoreType.DMA((5,)),
        ],
        compiler_params=PARAMS,
        name="finish",
    )(gathered, early_field, field, base, slopes)


def solution(mesh):
    in_specs = (
        P("col", "slab", None),
        P(),
        P("col", "slab", None),
        P(None, "col", "slab", None),
        P(),
    )
    out_specs = (P(None, "col", "slab", None), P("col", "slab", None))
    return jax.shard_map(shards, mesh=mesh, in_specs=in_specs, out_specs=out_specs, check_vma=False)
```

time: 29.5 us -> 29.5 us (level)
  starting transfers between devices: 8.57 us -> 9.86 us
  blocking collectives: 13 us -> 11.8 us
  waiting for transfers between devices: 3.51 us -> 2.93 us
  Pallas kernels: 3.6 us -> 4.07 us
    ppermute x6, starting transfers between devices: 8.57 us -> 9.86 us  [the longest x1 3.54 us: shards(): z_b = lax.ppermute(z_b, 'slab', swap_b('slab'))]
    all_to_all x1, blocking collectives: 13 us -> 11.8 us  [shards(): gathered = lax.all_to_all(sums, ('col', 'slab'), 0, 0, tiled=True)]
    ppermute x6, waiting for transfers between devices: 3.51 us -> 2.93 us  [the longest x1 1.81 us: shards(): z_b = lax.ppermute(z_b, 'slab', swap_b('slab'))]
    pallas_call x4 -> x5, Pallas kernels: 3.6 us -> 4.07 us  [the longest x1 1.23 us: shards(): pl.pallas_call(functools.partial(krylov, peers), out_shape=(fields, f32((...]
  transfers between devices with their start and end apart: 6 -> 6, of which waited for: 4 -> 2; matrix products, arithmetic and copies ran while one was open for 0% -> 0% of each run, Pallas kernels for 0% -> 2%
where the time goes in v4:
time: 29.5 us; the launch traced here: 29.3 us
  blocking collectives  11.8 us (40%)
  starting transfers between devices  9.86 us (33%)
  Pallas kernels  4.07 us (14%)
  waiting for transfers between devices  2.93 us (10%)
  between operations  0.66 us (2%)
    all_to_all x1, blocking collectives, shards(): gathered = lax.all_to_all(sums, ('col', 'slab'), 0, 0, tiled=True)  11.8 us
    ppermute x1, starting transfers between devices, shards(): z_b = lax.ppermute(z_b, 'slab', swap_b('slab'))  3.54 us
    ppermute x1, starting transfers between devices, shards(): z_a = lax.ppermute(z_a, 'slab', swap_a('slab'))  3.03 us
    ppermute x1, waiting for transfers between devices, shards(): z_b = lax.ppermute(z_b, 'slab', swap_b('slab'))  1.81 us
    ppermute x1, starting transfers between devices, shards(): corner_b = lax.ppermute(corner_b, 'col', swap_b('col'))  1.61 us
    ppermute x1, starting transfers between devices, shards(): x_b = lax.ppermute(x_b, 'col', swap_b('col'))  1.6 us
    pallas_call x1, Pallas kernels, shards(): pl.pallas_call(functools.partial(krylov, peers), out_shape=(fields, f32((...  1.23 us
    pallas_call x1, Pallas kernels, shards(): pl.pallas_call(finish, out_shape=(f32((3, LAYERS, 8, 128)), f32((LAYERS,...  1.11 us
  transfers between devices with their start and end apart: 6, of which 2 were waited for; matrix products, arithmetic and copies ran while one was open for 0% of the time, Pallas kernels for 2%

profile of v4, /device:TPU:0, one launch (start us, length us, event | category | flops | bytes accessed | tf_op | source)
XLA Modules:
  0.0 29.3 jit_solution(3313747617811717152)
XLA Ops:
  0.6 1.0 %prepare.1 = (f32[4,8,8,128]{3,2,1,0:T(8,128)S(1)}, f32[4,4,8,128]{3,2,1,0:T(8,128)S(1)}, f32[4,4,8,128]{3,2,1,0:T(8,128)S(1)}, f32[4,4,8,128]{3,2,1,0:T(8,128)S...) custom-call(s32[8,8,128]{2,1,0:T(8,128)} %labels_hbm.1, f32[3]{0:T(128)} %table_hbm.1, ...), custom_call_target="tpu_custom_call" | custom-call | tf_op jit(solution)/shard_map/prepare/pallas_call | solution.py:492
  1.7 3.0 %collective-permute-start = (f32[4,4,8,128]{3,2,1,0:T(8,128)S(1)}, f32[4,4,8,128]{3,2,1,0:T(8,128)S(1)}, u32[]{:S(2)}, u32[]{:S(2)}) collective-permute-start(f32[4,4,8,128]{3,2,1,0:T(8,128)S(1)} %get-tuple-element.19), channel_id=1, source_target_pairs={{0,1},{1,0},{2,3},{3,2},{4,5},{5,4},{6,7},{7,6},{8,9},{9,8},{10,11... | collective-permute-start | bytes 196616 | tf_op jit(solution)/shard_map/ppermute | solution.py:509
  4.7 3.5 %collective-permute-start.1 = (f32[4,4,8,128]{3,2,1,0:T(8,128)S(1)}, f32[4,4,8,128]{3,2,1,0:T(8,128)S(1)}, u32[]{:S(2)}, u32[]{:S(2)}) collective-permute-start(f32[4,4,8,128]{3,2,1,0:T(8,128)S(1)} %get-tuple-element.20), channel_id=1, source_target_pairs={{0,7},{1,2},{2,1},{3,4},{4,3},{5,6},{6,5},{7,0},{8,15},{9,10},{10,... | collective-permute-start | bytes 196616 | tf_op jit(solution)/shard_map/ppermute | solution.py:508
  8.2 0.0 collective-permute-start.2
  8.2 1.6 %collective-permute-start.3 = (f32[4,4,8,128]{3,2,1,0:T(8,128)S(1)}, f32[4,4,8,128]{3,2,1,0:T(8,128)S(1)}, u32[]{:S(2)}, u32[]{:S(2)}) collective-permute-start(f32[4,4,8,128]{3,2,1,0:T(8,128)S(1)} %get-tuple-element.23), channel_id=1, source_target_pairs={{0,24},{8,16},{16,8},{24,0},{1,25},{9,17},{17,9},{25,1},{2,26},{10... | collective-permute-start | bytes 196616 | tf_op jit(solution)/shard_map/ppermute | solution.py:510
  9.8 0.0 collective-permute-done.z_a
  9.8 1.8 %collective-permute-done.1.z_b = f32[4,4,8,128]{3,2,1,0:T(8,128)S(1)} collective-permute-done((f32[4,4,8,128]{3,2,1,0:T(8,128)S(1)}, f32[4,4,8,128]{3,2,1,0:T(8,128)S(1)}, u32[]{:S(2)}, u32[]{:S(2)}) %collective-permute-start.1) | collective-permute-done | bytes 65568 | tf_op jit(solution)/shard_map/ppermute | solution.py:508
  11.7 0.1 collective-permute-start.4
  11.8 1.6 %collective-permute-start.5 = (f32[4,2,8,128]{3,2,1,0:T(8,128)S(1)}, f32[4,2,8,128]{3,2,1,0:T(8,128)S(1)}, u32[]{:S(2)}, u32[]{:S(2)}) collective-permute-start(f32[4,2,8,128]{3,2,1,0:T(8,128)S(1)} %get-tuple-element.27), channel_id=1, source_target_pairs={{0,24},{8,16},{16,8},{24,0},{1,25},{9,17},{17,9},{25,1},{2,26},{10... | collective-permute-start | bytes 98312 | tf_op jit(solution)/shard_map/ppermute | solution.py:521
  13.4 0.0 collective-permute-done.2.x_a
  13.4 0.0 collective-permute-done.3.x_b
  13.4 0.7 %early.1 = (f32[4,8,8,128]{3,2,1,0:T(8,128)S(1)}, f32[3,16,2,8,128]{4,3,2,1,0:T(8,128)S(1)}, f32[3,3,16,2,8,128]{5,4,3,2,1,0:T(8,128)S(1)}, f32[8,8,128]{2,1,0:T(8,128)S(1)}, f32[3,2,3,8,8,128]{5,4,3,2,1,0:T(8,128)S(1)}) custom-call(f32[4,8,8,128]{3,2,1,0:T(8,128)S(1)} %get-tuple-element.18.own, f32[4,8,8,128]{3,2,1,0:T(8,128)S(1)} %get-tuple-element.21.ring.z_ring, ...), custom_call_target="tpu_custom_call" | custom-call | tf_op jit(solution)/shard_map/early/pallas_call | solution.py:524
  14.1 0.0 collective-permute-done.4.corner_a
  14.1 1.1 %collective-permute-done.5.corner_b = f32[4,2,8,128]{3,2,1,0:T(8,128)S(1)} collective-permute-done((f32[4,2,8,128]{3,2,1,0:T(8,128)S(1)}, f32[4,2,8,128]{3,2,1,0:T(8,128)S(1)}, u32[]{:S(2)}, u32[]{:S(2)}) %collective-permute-start.5) | collective-permute-done | bytes 32800 | tf_op jit(solution)/shard_map/ppermute | solution.py:521
  15.2 1.2 %krylov.1 = (f32[3,3,16,2,8,128]{5,4,3,2,1,0:T(8,128)S(1)}, f32[32,128]{1,0:T(8,128)S(1)}) custom-call(f32[4,8,8,128]{3,2,1,0:T(8,128)S(1)} %get-tuple-element.18.own, f32[4,8,8,128]{3,2,1,0:T(8,128)S(1)} %get-tuple-element.21.ring.z_ring, f32[4,8,8,128]{3,2,1,0:T(8,128)S(1)} %get-tuple-element.25.halo, ...), custom_call_target="tpu_custom_call" | custom-call | tf_op jit(solution)/shard_map/krylov/pallas_call | solution.py:539
  16.4 11.8 %all_to_all.11 = f32[32,1,128]{2,1,0:T(1,128)S(1)} all-to-all(f32[32,1,128]{2,1,0:T(1,128)S(1)} %bitcast.5), channel_id=1, replica_groups=mesh['col'=4,'slab'=8] {'col','slab'}, dimensions={0} | all-to-all | bytes 32768 | tf_op jit(solution)/shard_map/all_to_all | solution.py:549
  28.2 1.1 %finish.1 = (f32[3,8,8,128]{3,2,1,0:T(8,128)}, f32[8,8,128]{2,1,0:T(8,128)}) custom-call(f32[32,128]{1,0:T(8,128)S(1)} %bitcast.4, f32[3,3,16,2,8,128]{5,4,3,2,1,0:T(8,128)S(1)} %get-tuple-element.29.early_field, f32[3,3,16,2,8,128]{5,4,3,2,1,0:T(8,128)S(1)} %get-tuple-element.31.field, f32[8,8,128]{2,1,0:T(8,128)S(1)} %get-tuple-element.32.base, ...), custom_call_target="tpu_custom_call" | custom-call | tf_op jit(solution)/shard_map/finish/pallas_call | solution.py:551
  (1 shorter events, 0.0 us)
Async XLA Ops:
  1.7 8.2 %collective-permute-start = (f32[4,4,8,128]{3,2,1,0:T(8,128)S(1)}, f32[4,4,8,128]{3,2,1,0:T(8,128)S(1)}, u32[]{:S(2)}, u32[]{:S(2)}) collective-permute-start(f32[4,4,8,128]{3,2,1,0:T(8,128)S(1)} %get-tuple-element.19), channel_id=1, source_target_pairs={{0,1},{1,0},{2,3},{3,2},{4,5},{5,4},{6,7},{7,6},{8,9},{9,8},{10,11... | collective-permute-start | bytes 196616 | tf_op jit(solution)/shard_map/ppermute | solution.py:509
  4.7 7.0 %collective-permute-start.1 = (f32[4,4,8,128]{3,2,1,0:T(8,128)S(1)}, f32[4,4,8,128]{3,2,1,0:T(8,128)S(1)}, u32[]{:S(2)}, u32[]{:S(2)}) collective-permute-start(f32[4,4,8,128]{3,2,1,0:T(8,128)S(1)} %get-tuple-element.20), channel_id=1, source_target_pairs={{0,7},{1,2},{2,1},{3,4},{4,3},{5,6},{6,5},{7,0},{8,15},{9,10},{10,... | collective-permute-start | bytes 196616 | tf_op jit(solution)/shard_map/ppermute | solution.py:508
  8.2 5.1 %collective-permute-start.2 = (f32[4,4,8,128]{3,2,1,0:T(8,128)S(1)}, f32[4,4,8,128]{3,2,1,0:T(8,128)S(1)}, u32[]{:S(2)}, u32[]{:S(2)}) collective-permute-start(f32[4,4,8,128]{3,2,1,0:T(8,128)S(1)} %get-tuple-element.22), channel_id=1, source_target_pairs={{0,8},{8,0},{16,24},{24,16},{1,9},{9,1},{17,25},{25,17},{2,10},{10... | collective-permute-start | bytes 196616 | tf_op jit(solution)/shard_map/ppermute | solution.py:511
  8.2 5.1 %collective-permute-start.3 = (f32[4,4,8,128]{3,2,1,0:T(8,128)S(1)}, f32[4,4,8,128]{3,2,1,0:T(8,128)S(1)}, u32[]{:S(2)}, u32[]{:S(2)}) collective-permute-start(f32[4,4,8,128]{3,2,1,0:T(8,128)S(1)} %get-tuple-element.23), channel_id=1, source_target_pairs={{0,24},{8,16},{16,8},{24,0},{1,25},{9,17},{17,9},{25,1},{2,26},{10... | collective-permute-start | bytes 196616 | tf_op jit(solution)/shard_map/ppermute | solution.py:510
  11.7 2.4 %collective-permute-start.4 = (f32[4,2,8,128]{3,2,1,0:T(8,128)S(1)}, f32[4,2,8,128]{3,2,1,0:T(8,128)S(1)}, u32[]{:S(2)}, u32[]{:S(2)}) collective-permute-start(f32[4,2,8,128]{3,2,1,0:T(8,128)S(1)} %get-tuple-element.26), channel_id=1, source_target_pairs={{0,8},{8,0},{16,24},{24,16},{1,9},{9,1},{17,25},{25,17},{2,10},{10... | collective-permute-start | bytes 98312 | tf_op jit(solution)/shard_map/ppermute | solution.py:522
  11.8 3.4 %collective-permute-start.5 = (f32[4,2,8,128]{3,2,1,0:T(8,128)S(1)}, f32[4,2,8,128]{3,2,1,0:T(8,128)S(1)}, u32[]{:S(2)}, u32[]{:S(2)}) collective-permute-start(f32[4,2,8,128]{3,2,1,0:T(8,128)S(1)} %get-tuple-element.27), channel_id=1, source_target_pairs={{0,24},{8,16},{16,8},{24,0},{1,25},{9,17},{17,9},{25,1},{2,26},{10... | collective-permute-start | bytes 98312 | tf_op jit(solution)/shard_map/ppermute | solution.py:521

commit v5 on v4

--- a/solution.py
+++ b/solution.py
@@ -54,16 +54,11 @@
     labels, table, factor, weights, sems,
 ):
     odd_col = parity("col")
-    start_a, start_b = HALO * (1 - odd_col), HALO * odd_col
-    moves = (
-        (labels_hbm, labels),
-        (table_hbm, table),
-        (factor_hbm, factor),
-        (weights_hbm, weights),
-        (chi_hbm, own.at[pl.ds(0, 3)]),
-        (chi_hbm.at[:, pl.ds(start_a, HALO)], x_a.at[pl.ds(0, 3)]),
-        (chi_hbm.at[:, pl.ds(start_b, HALO)], x_b.at[pl.ds(0, 3)]),
-    )
+    moves = [(table_hbm, table), (weights_hbm, weights)]
+    for n in range(2):
+        part = pl.ds(HALO * n, HALO)
+        moves += [(chi_hbm.at[j, part], own.at[j, part]) for j in range(3)]
+        moves += [(labels_hbm.at[part], labels.at[part]), (factor_hbm.at[part], factor.at[part])]
     copies = [pltpu.make_async_copy(source, target, sems.at[n]) for n, (source, target) in enumerate(moves)]
     for copy in copies:
         copy.start()
@@ -72,10 +67,11 @@
     for x in range(2 * HALO):
         label = labels[x]
         own[3, x] = jnp.where(label == 0, table[0], jnp.where(label == 1, table[1], table[2])) * factor[x]
-    for x in range(HALO):
-        low, high = own[3, x], own[3, HALO + x]
-        x_a[3, x] = choose(odd_col, high, low)
-        x_b[3, x] = choose(odd_col, low, high)
+    for f in range(4):
+        for x in range(HALO):
+            low, high = own[f, x], own[f, HALO + x]
+            x_a[f, x] = choose(odd_col, high, low)
+            x_b[f, x] = choose(odd_col, low, high)
     for i in range(3):
         for j in range(3):
             splat[3 * i + j] = jnp.full((8, 128), weights[i, j], jnp.float32)
@@ -90,7 +86,7 @@
             z_b[f, i] = choose(odd_slab, low_rows, high_rows)
 
 
-def fold(z_a, z_b, ring, corner_a, corner_b):
+def fold(z_b, z_a, ring, corner_a, corner_b):
     odd_col, odd_slab = parity("col"), parity("slab")
     half = tile_iota(0) < 4
     outer = (tile_iota(0) < 2) | (tile_iota(0) >= 6)
@@ -173,25 +169,49 @@
 TOTAL = 2 * LAYERS
 
 
-def inner(k):
-    return range(HALO + 1 + k, HALO + LAYERS - 1 - k)
+PAIRS = ((0, 0), (0, 1), (1, 1), (1, 2), (2, 2), (2, 3))
+
+
+def needed(k, t):
+    return range(1 + k + t, TOTAL - 1 - k - t)
+
+
+def inner(k, t):
+    return range(HALO + k + t, HALO + LAYERS - k - t)
 
 
 def harmonic(here, after):
     return 2.0 * here * after / (here + after)
 
 
-def out_flow(here, after, x_cond, z_cond, y_cond, offset, flows):
-    beside = z_next(here)
-    z_flux = [z_cond[t] * (offset[1] + (beside[t] - here[t])) for t in range(2)]
-    z_back = z_prev(z_flux)
-    added = []
-    for t in range(2):
-        x_flux = x_cond[t] * (offset[0] + (after[t] - here[t]))
-        y_flux = y_cond[t] * (offset[2] + (y_next(here[t]) - here[t]))
-        before = flows[t]
-        flows[t] = x_flux
-        added.append((before - x_flux) + (z_back[t] - z_flux[t]) + (y_prev(y_flux) - y_flux))
+def keep_y(cond, x, t, here):
+    value = harmonic(here, y_next(here))
+    cond[2, x, t] = value
+    cond[4, x, t] = y_prev(value)
+
+
+def keep_z(cond, x, here):
+    values = [harmonic(tile, beside) for tile, beside in zip(here, z_next(here))]
+    for t, before in enumerate(z_prev(values)):
+        cond[1, x, t] = values[t]
+        cond[3, x, t] = before
+
+
+def out_flow(x, tiles, value, cond, offset, fluxes):
+    def x_flux(face, t):
+        if (face, t) not in fluxes:
+            fluxes[face, t] = cond(0, face, t) * (offset[0] + (value(face + 1, t) - value(face, t)))
+        return fluxes[face, t]
+
+    here = [value(x, t) for t in range(2)]
+    above, below = z_next(here), z_prev(here)
+    added = {}
+    for t in tiles:
+        z_part = cond(3, x, t) * (offset[1] + (here[t] - below[t])) - cond(1, x, t) * (offset[1] + (above[t] - here[t]))
+        y_part = cond(4, x, t) * (offset[2] + (here[t] - y_prev(here[t]))) - cond(2, x, t) * (
+            offset[2] + (y_next(here[t]) - here[t])
+        )
+        added[t] = (x_flux(x - 1, t) - x_flux(x, t)) + z_part + y_part
     return added
 
 
@@ -199,31 +219,43 @@
     return [read(*index, t) for t in range(2)]
 
 
-def add_source(layers, grid, cond, splat, field):
+def by_layer(wanted):
+    for x in range(TOTAL):
+        tiles = [t for t in range(2) if wanted(x, t)]
+        if tiles:
+            yield x, tiles
+
+
+def add_source(wanted, grid, cond, splat, field):
     offset = [[1.0 if d == j else 0.0 for d in range(3)] for j in range(3)]
-    flows = []
-    for j in range(3):
-        here, after = both(grid, j, layers[0] - 1), both(grid, j, layers[0])
-        flows.append([cond(0, layers[0] - 1, t) * (offset[j][0] + (after[t] - here[t])) for t in range(2)])
-    for x in layers:
-        conds = [both(cond, d, x) for d in range(3)]
+    fluxes = [{} for _ in range(3)]
+    for x, tiles in by_layer(wanted):
         drive = [
-            out_flow(both(grid, j, x), both(grid, j, x + 1), *conds, offset[j], flows[j]) for j in range(3)
+            out_flow(x, tiles, functools.partial(grid, j), cond, offset[j], fluxes[j]) for j in range(3)
         ]
         for i in range(3):
-            for t in range(2):
+            for t in tiles:
                 field[0, i, x, t] = (
                     splat[3 * i] * drive[0][t] + splat[3 * i + 1] * drive[1][t] + splat[3 * i + 2] * drive[2][t]
                 )
 
 
-def applied(k, i, layers, v, cond):
-    here, after = both(v, k, i, layers[0] - 1), both(v, k, i, layers[0])
-    flow = [cond(0, layers[0] - 1, t) * (after[t] - here[t]) for t in range(2)]
-    for x in layers:
-        here, after = both(v, k, i, x), both(v, k, i, x + 1)
-        added = out_flow(here, after, *[both(cond, d, x) for d in range(3)], (0.0, 0.0, 0.0), flow)
-        yield x, [mass_shift * here[t] + added[t] for t in range(2)]
+def applied(k, i, wanted, v, cond):
+    fluxes = {}
+    value = functools.partial(v, k, i)
+    for x, tiles in by_layer(wanted):
+        added = out_flow(x, tiles, value, cond, (0.0, 0.0, 0.0), fluxes)
+        yield x, {t: mass_shift * value(x, t) + added[t] for t in tiles}
+
+
+def add_moments(partial, wanted, v, last):
+    for i in range(3):
+        for x in range(HALO, HALO + LAYERS):
+            for m, (a, b) in enumerate(PAIRS):
+                if wanted(b, x):
+                    product = v(a, i, x, 0) * (last[i, x] if b == 3 else v(b, i, x, 0))
+                    key = 3 * m + i
+                    partial[key] = product if partial.get(key) is None else partial[key] + product
 
 
 def face_parts(d, here, after, chi_here, chi_after, splat):
@@ -239,7 +271,7 @@
     return [energy * now] + [value * now for value in local], [energy * back] + [value * back for value in local]
 
 
-def early(own, ring, x_a, x_b, splat, halo, cond, field, base, slopes):
+def early(own, ring, x_b, x_a, splat, halo, cond, field, base, slopes, moments):
     odd_col = parity("col")
     for f in range(4):
         for n in range(HALO):
@@ -255,16 +287,15 @@
 
     for x in range(TOTAL):
         here = grid(3, x, 0)
-        cond[2, x, 0] = harmonic(here, y_next(here))
+        keep_y(cond, x, 0, here)
         if x + 1 < TOTAL:
             cond[0, x, 0] = harmonic(here, grid(3, x + 1, 0))
         if HALO <= x < HALO + LAYERS:
             other = grid(3, x, 1)
-            cond[2, x, 1] = harmonic(other, y_next(other))
+            keep_y(cond, x, 1, other)
             if x + 1 < HALO + LAYERS:
                 cond[0, x, 1] = harmonic(other, grid(3, x + 1, 1))
-            for t, (tile, beside) in enumerate(zip((here, other), z_next((here, other)))):
-                cond[1, x, t] = harmonic(tile, beside)
+            keep_z(cond, x, (here, other))
 
     def ready(*index):
         return cond[index]
@@ -272,11 +303,20 @@
     def v(*index):
         return field[index]
 
-    add_source(inner(0), grid, ready, splat, field)
+    add_source(lambda x, t: x in inner(0, t), grid, ready, splat, field)
     for k in (1, 2):
         for i in range(3):
-            for x, value in applied(k - 1, i, inner(k), v, ready):
-                field[k, i, x, 0], field[k, i, x, 1] = value
+            for x, value in applied(k - 1, i, lambda x, t: x in inner(k, t), v, ready):
+                for t in value:
+                    field[k, i, x, t] = value[t]
+    last = {}
+    for i in range(3):
+        for x, value in applied(2, i, lambda x, t: t == 0 and x in inner(3, 0), v, ready):
+            last[i, x] = value[0]
+    partial = {}
+    add_moments(partial, lambda k, x: x in inner(k, 0), v, last)
+    for n, value in partial.items():
+        moments[n] = value
 
     carried = None
     for x in range(HALO - 1, HALO + LAYERS):
@@ -304,7 +344,9 @@
         carried = back
 
 
-def krylov(peers, own, z_ring, halo, corner_a, corner_b, splat, early_cond, early_field, field, sums, ring, cond):
+def krylov(
+    peers, own, z_ring, halo, corner_b, corner_a, splat, early_cond, early_field, moments, field, sums, ring, cond
+):
     odd_col = parity("col")
     half = tile_iota(0) < 4
     for f in range(4):
@@ -324,43 +366,35 @@
         return (halo, ring)[t][f, x - LAYERS]
 
     def is_early(d, x, t):
-        return HALO <= x < HALO + LAYERS - (1 if d == 0 and t == 1 else 0) or (t == 0 and d != 1)
+        return HALO <= x < HALO + LAYERS - (1 if d == 0 and t == 1 else 0) or (t == 0 and d in (0, 2, 4))
 
     def ready(d, x, t):
         return (early_cond if is_early(d, x, t) else cond)[d, x, t]
 
     def v(k, i, x, t):
-        return (early_field if x in inner(k) else field)[k, i, x, t]
-
-    for x in range(TOTAL - 1):
-        here = both(grid, 3, x)
-        if not is_early(0, x, 1):
-            cond[0, x, 1] = harmonic(here[1], grid(3, x + 1, 1))
-        if not is_early(2, x, 1):
-            cond[2, x, 1] = harmonic(here[1], y_next(here[1]))
+        return (early_field if x in inner(k, t) else field)[k, i, x, t]
+
+    for x in range(1, TOTAL - 1):
+        if x < TOTAL - 2 and not is_early(0, x, 1):
+            cond[0, x, 1] = harmonic(grid(3, x, 1), grid(3, x + 1, 1))
+        if x in needed(0, 1) and not is_early(2, x, 1):
+            keep_y(cond, x, 1, grid(3, x, 1))
         if not is_early(1, x, 1):
-            for t, beside in enumerate(z_next(here)):
-                cond[1, x, t] = harmonic(here[t], beside)
-
-    def outer(k):
-        done = inner(k)
-        return range(1 + k, done.start), range(done.stop, TOTAL - 1 - k)
-
-    for layers in outer(0):
-        add_source(layers, grid, ready, splat, field)
+            keep_z(cond, x, both(grid, 3, x))
+
+    add_source(lambda x, t: x in needed(0, t) and x not in inner(0, t), grid, ready, splat, field)
     for k in (1, 2):
-        for layers in outer(k):
-            for i in range(3):
-                for x, value in applied(k - 1, i, layers, v, ready):
-                    field[k, i, x, 0], field[k, i, x, 1] = value
-
-    partial = [jnp.zeros((8, 128), jnp.float32) for _ in range(3 * MOMENTS)]
+        for i in range(3):
+            for x, value in applied(k - 1, i, lambda x, t: x in needed(k, t) and x not in inner(k, t), v, ready):
+                for t in value:
+                    field[k, i, x, t] = value[t]
+    last = {}
     for i in range(3):
-        for x, value in applied(2, i, range(HALO, HALO + LAYERS), v, ready):
-            tiles = [v(k, i, x, 0) for k in range(3)] + [value[0]]
-            for m, (a, b) in enumerate(((0, 0), (0, 1), (1, 1), (1, 2), (2, 2), (2, 3))):
-                partial[3 * m + i] = partial[3 * m + i] + tiles[a] * tiles[b]
-    sums[...] = jnp.broadcast_to(total_row(partial), (peers, 128))
+        for x, value in applied(2, i, lambda x, t: t == 0 and x in needed(3, 0) and x not in inner(3, 0), v, ready):
+            last[i, x] = value[0]
+    partial = {n: moments[n] for n in range(3 * MOMENTS)}
+    add_moments(partial, lambda k, x: x not in inner(k, 0), v, last)
+    sums[...] = jnp.broadcast_to(total_row([partial[n] for n in range(3 * MOMENTS)]), (peers, 128))
 
 
 def quadratic(terms):
@@ -391,9 +425,11 @@
     none = jnp.zeros((8, 128), jnp.float32)
     one = (jnp.ones((8, 128), jnp.float32), none)
     alpha0 = m0[0] / m1[0]
+    inverse0 = 1.0 / m0[0]
     alpha0_squared = two_product(alpha0, alpha0)
     norm1 = quadratic(((one, m0), ((-2.0 * alpha0, none), m1), (alpha0_squared, m2)))
-    grow = 1.0 + norm1 / m0[0]
+    inverse1 = 1.0 / norm1
+    grow = 1.0 + norm1 * inverse0
     curve1 = quadratic(
         ((two_product(grow, grow), m1), (two_product(-2.0 * grow, alpha0), m2), (alpha0_squared, m3))
     )
@@ -409,7 +445,7 @@
             (two_product(r2, r2), m4),
         )
     )
-    beta1 = norm2 / norm1
+    beta1 = norm2 * inverse1
     p0, p1, p2 = 1.0 + beta1 * grow, r1 - beta1 * alpha0, r2
     curve2 = quadratic(
         (
@@ -436,7 +472,7 @@
                 if t == 1 and x in (0, LAYERS + 1):
                     continue
                 at = x + HALO - 1
-                v = [(early_field if at in inner(k) else field)[k, i, at, t] for k in range(3)]
+                v = [(early_field if at in inner(k, t) else field)[k, i, at, t] for k in range(3)]
                 value = scale[0][i] * v[0] + scale[1][i] * v[1] + scale[2][i] * v[2]
                 lam[i, x, t] = value
                 if t == 0 and 0 < x <= LAYERS:
@@ -499,7 +535,7 @@
             pltpu.SMEM((3,), jnp.float32),
             scratch((LAYERS, 8, 128)),
             pltpu.SMEM((3, 3), jnp.float32),
-            pltpu.SemaphoreType.DMA((7,)),
+            pltpu.SemaphoreType.DMA((12,)),
         ],
         compiler_params=PARAMS,
         name="prepare",
@@ -517,34 +553,35 @@
         out_specs=(VMEM,) * 3,
         compiler_params=PARAMS,
         name="fold",
-    )(z_a, z_b)
+    )(z_b, z_a)
     corner_b = lax.ppermute(corner_b, "col", swap_b("col"))
     corner_a = lax.ppermute(corner_a, "col", swap_a("col"))
 
-    halo, cond, early_field, base, slopes = pl.pallas_call(
+    halo, cond, early_field, base, slopes, moments = pl.pallas_call(
         early,
         out_shape=(
             f32(block),
-            f32((3, TOTAL, 2, 8, 128)),
+            f32((5, TOTAL, 2, 8, 128)),
             fields,
             f32((LAYERS, 8, 128)),
             f32((3, 2, 3, LAYERS, 8, 128)),
+            f32((3 * MOMENTS, 8, 128)),
         ),
         in_specs=[VMEM] * 5,
-        out_specs=(VMEM,) * 5,
+        out_specs=(VMEM,) * 6,
         compiler_params=PARAMS,
         name="early",
-    )(own, ring, x_a, x_b, splat)
+    )(own, ring, x_b, x_a, splat)
 
     field, sums = pl.pallas_call(
         functools.partial(krylov, peers),
         out_shape=(fields, f32((peers, 128))),
-        in_specs=[VMEM] * 8,
+        in_specs=[VMEM] * 9,
         out_specs=(VMEM,) * 2,
-        scratch_shapes=[scratch(block), scratch((3, TOTAL, 2, 8, 128))],
+        scratch_shapes=[scratch(block), scratch((5, TOTAL, 2, 8, 128))],
         compiler_params=PARAMS,
         name="krylov",
-    )(own, ring, halo, corner_a, corner_b, splat, cond, early_field)
+    )(own, ring, halo, corner_b, corner_a, splat, cond, early_field, moments)
 
     gathered = lax.all_to_all(sums, ("col", "slab"), 0, 0, tiled=True)
 

time: 29.5 us -> 28.8 us (0.976)
  blocking collectives: 11.8 us -> 10.6 us
  waiting for transfers between devices: 2.93 us -> 4 us
  starting transfers between devices: 9.86 us -> 9.35 us
    ppermute x1, starting transfers between devices: 3.03 us -> 0.01 us  [shards(): z_a = lax.ppermute(z_a, 'slab', swap_a('slab'))]
    ppermute x1, starting transfers between devices: 3.54 us -> 6.07 us  [shards(): z_b = lax.ppermute(z_b, 'slab', swap_b('slab'))]
    ppermute x1, waiting for transfers between devices: 0.01 us -> 2.01 us  [shards(): z_a = lax.ppermute(z_a, 'slab', swap_a('slab'))]
    ppermute x1, starting transfers between devices: 1.61 us -> 0.12 us  [shards(): corner_b = lax.ppermute(corner_b, 'col', swap_b('col'))]
    ppermute x1, starting transfers between devices: 0.07 us -> 1.55 us  [shards(): corner_a = lax.ppermute(corner_a, 'col', swap_a('col'))]
    all_to_all x1, blocking collectives: 11.8 us -> 10.6 us  [shards(): gathered = lax.all_to_all(sums, ('col', 'slab'), 0, 0, tiled=True)]
    ppermute x1, waiting for transfers between devices: 1.81 us -> 0.64 us  [shards(): z_b = lax.ppermute(z_b, 'slab', swap_b('slab'))]
    ppermute x1, starting transfers between devices: 0.01 us -> 0.96 us  [shards(): x_a = lax.ppermute(x_a, 'col', swap_a('col'))]
  transfers between devices with their start and end apart: 6 -> 6, of which waited for: 2 -> 3; matrix products, arithmetic and copies ran while one was open for 0% -> 0% of each run, Pallas kernels for 2% -> 3%
where the time goes in v5:
time: 28.8 us; the launch traced here: 28.5 us
  blocking collectives  10.6 us (37%)
  starting transfers between devices  9.35 us (32%)
  waiting for transfers between devices  4 us (14%)
  Pallas kernels  3.9 us (14%)
  between operations  0.66 us (2%)
    all_to_all x1, blocking collectives, shards(): gathered = lax.all_to_all(sums, ('col', 'slab'), 0, 0, tiled=True)  10.6 us
    ppermute x1, starting transfers between devices, shards(): z_b = lax.ppermute(z_b, 'slab', swap_b('slab'))  6.07 us
    ppermute x1, waiting for transfers between devices, shards(): z_a = lax.ppermute(z_a, 'slab', swap_a('slab'))  2.01 us
    ppermute x1, starting transfers between devices, shards(): corner_a = lax.ppermute(corner_a, 'col', swap_a('col'))  1.55 us
    ppermute x1, waiting for transfers between devices, shards(): corner_b = lax.ppermute(corner_b, 'col', swap_b('col'))  1.33 us
    pallas_call x1, Pallas kernels, shards(): pl.pallas_call(finish, out_shape=(f32((3, LAYERS, 8, 128)), f32((LAYERS,...  1.12 us
    pallas_call x1, Pallas kernels, shards(): pl.pallas_call(functools.partial(krylov, peers), out_shape=(fields, f32((...  1.06 us
    pallas_call x1, Pallas kernels, shards(): pl.pallas_call(prepare, out_shape=(f32(block),) + (half_block,) * 4 + (f3...  1 us
  transfers between devices with their start and end apart: 6, of which 3 were waited for; matrix products, arithmetic and copies ran while one was open for 0% of the time, Pallas kernels for 3%

profile of v5, /device:TPU:0, one launch (start us, length us, event | category | flops | bytes accessed | tf_op | source)
XLA Modules:
  0.0 28.5 jit_solution(10115135811610877765)
XLA Ops:
  0.6 1.0 %prepare.1 = (f32[4,8,8,128]{3,2,1,0:T(8,128)S(1)}, f32[4,4,8,128]{3,2,1,0:T(8,128)S(1)}, f32[4,4,8,128]{3,2,1,0:T(8,128)S(1)}, f32[4,4,8,128]{3,2,1,0:T(8,128)S...) custom-call(s32[8,8,128]{2,1,0:T(8,128)} %labels_hbm.1, f32[3]{0:T(128)} %table_hbm.1, ...), custom_call_target="tpu_custom_call" | custom-call | tf_op jit(solution)/shard_map/prepare/pallas_call | solution.py:528
  1.6 6.1 %collective-permute-start = (f32[4,4,8,128]{3,2,1,0:T(8,128)S(1)}, f32[4,4,8,128]{3,2,1,0:T(8,128)S(1)}, u32[]{:S(2)}, u32[]{:S(2)}) collective-permute-start(f32[4,4,8,128]{3,2,1,0:T(8,128)S(1)} %get-tuple-element.20), channel_id=1, source_target_pairs={{0,7},{1,2},{2,1},{3,4},{4,3},{5,6},{6,5},{7,0},{8,15},{9,10},{10,... | collective-permute-start | bytes 196616 | tf_op jit(solution)/shard_map/ppermute | solution.py:544
  7.7 0.0 collective-permute-start.1
  7.7 0.7 %collective-permute-start.2 = (f32[4,4,8,128]{3,2,1,0:T(8,128)S(1)}, f32[4,4,8,128]{3,2,1,0:T(8,128)S(1)}, u32[]{:S(2)}, u32[]{:S(2)}) collective-permute-start(f32[4,4,8,128]{3,2,1,0:T(8,128)S(1)} %get-tuple-element.23), channel_id=1, source_target_pairs={{0,24},{8,16},{16,8},{24,0},{1,25},{9,17},{17,9},{25,1},{2,26},{10... | collective-permute-start | bytes 196616 | tf_op jit(solution)/shard_map/ppermute | solution.py:546
  8.4 1.0 %collective-permute-start.3 = (f32[4,4,8,128]{3,2,1,0:T(8,128)S(1)}, f32[4,4,8,128]{3,2,1,0:T(8,128)S(1)}, u32[]{:S(2)}, u32[]{:S(2)}) collective-permute-start(f32[4,4,8,128]{3,2,1,0:T(8,128)S(1)} %get-tuple-element.24), channel_id=1, source_target_pairs={{0,8},{8,0},{16,24},{24,16},{1,9},{9,1},{17,25},{25,17},{2,10},{10... | collective-permute-start | bytes 196616 | tf_op jit(solution)/shard_map/ppermute | solution.py:547
  9.3 0.6 %collective-permute-done.z_b = f32[4,4,8,128]{3,2,1,0:T(8,128)S(1)} collective-permute-done((f32[4,4,8,128]{3,2,1,0:T(8,128)S(1)}, f32[4,4,8,128]{3,2,1,0:T(8,128)S(1)}, u32[]{:S(2)}, u32[]{:S(2)}) %collective-permute-start) | collective-permute-done | bytes 65568 | tf_op jit(solution)/shard_map/ppermute | solution.py:544
  10.0 2.0 %collective-permute-done.1.z_a = f32[4,4,8,128]{3,2,1,0:T(8,128)S(1)} collective-permute-done((f32[4,4,8,128]{3,2,1,0:T(8,128)S(1)}, f32[4,4,8,128]{3,2,1,0:T(8,128)S(1)}, u32[]{:S(2)}, u32[]{:S(2)}) %collective-permute-start.1) | collective-permute-done | bytes 65568 | tf_op jit(solution)/shard_map/ppermute | solution.py:545
  12.0 0.1 collective-permute-start.4
  12.1 1.6 %collective-permute-start.5 = (f32[4,2,8,128]{3,2,1,0:T(8,128)S(1)}, f32[4,2,8,128]{3,2,1,0:T(8,128)S(1)}, u32[]{:S(2)}, u32[]{:S(2)}) collective-permute-start(f32[4,2,8,128]{3,2,1,0:T(8,128)S(1)} %get-tuple-element.28), channel_id=1, source_target_pairs={{0,8},{8,0},{16,24},{24,16},{1,9},{9,1},{17,25},{25,17},{2,10},{10... | collective-permute-start | bytes 98312 | tf_op jit(solution)/shard_map/ppermute | solution.py:558
  13.7 0.0 collective-permute-done.2.x_b
  13.7 0.0 collective-permute-done.3.x_a
  13.7 0.7 %early.1 = (f32[4,8,8,128]{3,2,1,0:T(8,128)S(1)}, f32[5,16,2,8,128]{4,3,2,1,0:T(8,128)S(1)}, f32[3,3,16,2,8,128]{5,4,3,2,1,0:T(8,128)S(1)}, f32[8,8,128]{2,1,0:T...) custom-call(f32[4,8,8,128]{3,2,1,0:T(8,128)S(1)} %get-tuple-element.19.own, ...), custom_call_target="tpu_custom_call" | custom-call | tf_op jit(solution)/shard_map/early/pallas_call | solution.py:560
  14.4 1.3 %collective-permute-done.4.corner_b = f32[4,2,8,128]{3,2,1,0:T(8,128)S(1)} collective-permute-done((f32[4,2,8,128]{3,2,1,0:T(8,128)S(1)}, f32[4,2,8,128]{3,2,1,0:T(8,128)S(1)}, u32[]{:S(2)}, u32[]{:S(2)}) %collective-permute-start.4) | collective-permute-done | bytes 32800 | tf_op jit(solution)/shard_map/ppermute | solution.py:557
  15.7 0.0 collective-permute-done.5.corner_a
  15.7 1.1 %krylov.1 = (f32[3,3,16,2,8,128]{5,4,3,2,1,0:T(8,128)S(1)}, f32[32,128]{1,0:T(8,128)S(1)}) custom-call(f32[4,8,8,128]{3,2,1,0:T(8,128)S(1)} %get-tuple-element.19.own, f32[4,8,8,128]{3,2,1,0:T(8,128)S(1)} %get-tuple-element.22.ring.z_ring, f32[4,8,8,128]{3,2,1,0:T(8,128)S(1)} %get-tuple-element.26.halo, ...), custom_call_target="tpu_custom_call" | custom-call | tf_op jit(solution)/shard_map/krylov/pallas_call | solution.py:576
  16.8 10.6 %all_to_all.11 = f32[32,1,128]{2,1,0:T(1,128)S(1)} all-to-all(f32[32,1,128]{2,1,0:T(1,128)S(1)} %bitcast.5), channel_id=1, replica_groups=mesh['col'=4,'slab'=8] {'col','slab'}, dimensions={0} | all-to-all | bytes 32768 | tf_op jit(solution)/shard_map/all_to_all | solution.py:586
  27.4 1.1 %finish.1 = (f32[3,8,8,128]{3,2,1,0:T(8,128)}, f32[8,8,128]{2,1,0:T(8,128)}) custom-call(f32[32,128]{1,0:T(8,128)S(1)} %bitcast.4, f32[3,3,16,2,8,128]{5,4,3,2,1,0:T(8,128)S(1)} %get-tuple-element.30.early_field, f32[3,3,16,2,8,128]{5,4,3,2,1,0:T(8,128)S(1)} %get-tuple-element.33.field, f32[8,8,128]{2,1,0:T(8,128)S(1)} %get-tuple-element.34.base, ...), custom_call_target="tpu_custom_call" | custom-call | tf_op jit(solution)/shard_map/finish/pallas_call | solution.py:588
  (1 shorter events, 0.0 us)
Async XLA Ops:
  1.6 8.3 %collective-permute-start = (f32[4,4,8,128]{3,2,1,0:T(8,128)S(1)}, f32[4,4,8,128]{3,2,1,0:T(8,128)S(1)}, u32[]{:S(2)}, u32[]{:S(2)}) collective-permute-start(f32[4,4,8,128]{3,2,1,0:T(8,128)S(1)} %get-tuple-element.20), channel_id=1, source_target_pairs={{0,7},{1,2},{2,1},{3,4},{4,3},{5,6},{6,5},{7,0},{8,15},{9,10},{10,... | collective-permute-start | bytes 196616 | tf_op jit(solution)/shard_map/ppermute | solution.py:544
  7.7 4.3 %collective-permute-start.1 = (f32[4,4,8,128]{3,2,1,0:T(8,128)S(1)}, f32[4,4,8,128]{3,2,1,0:T(8,128)S(1)}, u32[]{:S(2)}, u32[]{:S(2)}) collective-permute-start(f32[4,4,8,128]{3,2,1,0:T(8,128)S(1)} %get-tuple-element.21), channel_id=1, source_target_pairs={{0,1},{1,0},{2,3},{3,2},{4,5},{5,4},{6,7},{7,6},{8,9},{9,8},{10,11... | collective-permute-start | bytes 196616 | tf_op jit(solution)/shard_map/ppermute | solution.py:545
  7.7 6.0 %collective-permute-start.2 = (f32[4,4,8,128]{3,2,1,0:T(8,128)S(1)}, f32[4,4,8,128]{3,2,1,0:T(8,128)S(1)}, u32[]{:S(2)}, u32[]{:S(2)}) collective-permute-start(f32[4,4,8,128]{3,2,1,0:T(8,128)S(1)} %get-tuple-element.23), channel_id=1, source_target_pairs={{0,24},{8,16},{16,8},{24,0},{1,25},{9,17},{17,9},{25,1},{2,26},{10... | collective-permute-start | bytes 196616 | tf_op jit(solution)/shard_map/ppermute | solution.py:546
  8.4 5.3 %collective-permute-start.3 = (f32[4,4,8,128]{3,2,1,0:T(8,128)S(1)}, f32[4,4,8,128]{3,2,1,0:T(8,128)S(1)}, u32[]{:S(2)}, u32[]{:S(2)}) collective-permute-start(f32[4,4,8,128]{3,2,1,0:T(8,128)S(1)} %get-tuple-element.24), channel_id=1, source_target_pairs={{0,8},{8,0},{16,24},{24,16},{1,9},{9,1},{17,25},{25,17},{2,10},{10... | collective-permute-start | bytes 196616 | tf_op jit(solution)/shard_map/ppermute | solution.py:547
  12.0 3.7 %collective-permute-start.4 = (f32[4,2,8,128]{3,2,1,0:T(8,128)S(1)}, f32[4,2,8,128]{3,2,1,0:T(8,128)S(1)}, u32[]{:S(2)}, u32[]{:S(2)}) collective-permute-start(f32[4,2,8,128]{3,2,1,0:T(8,128)S(1)} %get-tuple-element.27), channel_id=1, source_target_pairs={{0,24},{8,16},{16,8},{24,0},{1,25},{9,17},{17,9},{25,1},{2,26},{10... | collective-permute-start | bytes 98312 | tf_op jit(solution)/shard_map/ppermute | solution.py:557
  12.1 3.6 %collective-permute-start.5 = (f32[4,2,8,128]{3,2,1,0:T(8,128)S(1)}, f32[4,2,8,128]{3,2,1,0:T(8,128)S(1)}, u32[]{:S(2)}, u32[]{:S(2)}) collective-permute-start(f32[4,2,8,128]{3,2,1,0:T(8,128)S(1)} %get-tuple-element.28), channel_id=1, source_target_pairs={{0,8},{8,0},{16,24},{24,16},{1,9},{9,1},{17,25},{25,17},{2,10},{10... | collective-permute-start | bytes 98312 | tf_op jit(solution)/shard_map/ppermute | solution.py:558

commit v6 on v5

--- a/solution.py
+++ b/solution.py
@@ -11,6 +11,7 @@
 mass_shift = 0.01
 HALO = 4
 MOMENTS = 6
+NORM_FLOOR = 1e-14
 
 VMEM = pl.BlockSpec(memory_space=pltpu.VMEM)
 HBM = pl.BlockSpec(memory_space=pltpu.HBM)
@@ -54,11 +55,8 @@
     labels, table, factor, weights, sems,
 ):
     odd_col = parity("col")
-    moves = [(table_hbm, table), (weights_hbm, weights)]
-    for n in range(2):
-        part = pl.ds(HALO * n, HALO)
-        moves += [(chi_hbm.at[j, part], own.at[j, part]) for j in range(3)]
-        moves += [(labels_hbm.at[part], labels.at[part]), (factor_hbm.at[part], factor.at[part])]
+    moves = [(chi_hbm.at[j], own.at[j]) for j in range(3)] + [(factor_hbm, factor), (labels_hbm, labels)]
+    moves += [(table_hbm, table), (weights_hbm, weights)]
     copies = [pltpu.make_async_copy(source, target, sems.at[n]) for n, (source, target) in enumerate(moves)]
     for copy in copies:
         copy.start()
@@ -113,11 +111,20 @@
     return total, (a - (total - part)) + (b - part)
 
 
+def split(value):
+    scaled = 4097.0 * value
+    top = scaled - (scaled - value)
+    return top, value - top
+
+
+def exact_product(a, a_parts, b, b_parts):
+    product = a * b
+    (a_top, a_rest), (b_top, b_rest) = a_parts, b_parts
+    return product, ((a_top * b_top - product) + a_top * b_rest + a_rest * b_top) + a_rest * b_rest
+
+
 def two_product(a, b):
-    product = a * b
-    a_top, b_top = [4097.0 * v - (4097.0 * v - v) for v in (a, b)]
-    a_rest, b_rest = a - a_top, b - b_top
-    return product, ((a_top * b_top - product) + a_top * b_rest + a_rest * b_top) + a_rest * b_rest
+    return exact_product(a, split(a), b, split(b))
 
 
 def pair_sum(a, b):
@@ -130,11 +137,10 @@
     return product, error + (a[0] * b[1] + a[1] * b[0])
 
 
-def total_row(tiles):
+def total_row(pairs):
     row = tile_iota(0)
     lane = tile_iota(1)
-    pairs = [(tile, jnp.zeros((8, 128), jnp.float32)) for tile in tiles]
-    place = [[n] for n in range(len(tiles))]
+    place = [[n] for n in range(len(pairs))]
     for width in (4, 2, 1):
         lower = (row & width) == 0
         merged, spots = [], []
@@ -251,11 +257,14 @@
 def add_moments(partial, wanted, v, last):
     for i in range(3):
         for x in range(HALO, HALO + LAYERS):
-            for m, (a, b) in enumerate(PAIRS):
-                if wanted(b, x):
-                    product = v(a, i, x, 0) * (last[i, x] if b == 3 else v(b, i, x, 0))
-                    key = 3 * m + i
-                    partial[key] = product if partial.get(key) is None else partial[key] + product
+            pairs = [(m, pair) for m, pair in enumerate(PAIRS) if wanted(pair[1], x)]
+            used = sorted({k for m, pair in pairs for k in pair})
+            tiles = {k: last[i, x] if k == 3 else v(k, i, x, 0) for k in used}
+            parts = {k: split(tiles[k]) for k in used}
+            for m, (a, b) in pairs:
+                product = exact_product(tiles[a], parts[a], tiles[b], parts[b])
+                key = 3 * m + i
+                partial[key] = pair_sum(partial[key], product) if key in partial else product
 
 
 def face_parts(d, here, after, chi_here, chi_after, splat):
@@ -315,8 +324,8 @@
             last[i, x] = value[0]
     partial = {}
     add_moments(partial, lambda k, x: x in inner(k, 0), v, last)
-    for n, value in partial.items():
-        moments[n] = value
+    for n, pair in partial.items():
+        moments[0, n], moments[1, n] = pair
 
     carried = None
     for x in range(HALO - 1, HALO + LAYERS):
@@ -392,7 +401,7 @@
     for i in range(3):
         for x, value in applied(2, i, lambda x, t: t == 0 and x in needed(3, 0) and x not in inner(3, 0), v, ready):
             last[i, x] = value[0]
-    partial = {n: moments[n] for n in range(3 * MOMENTS)}
+    partial = {n: (moments[0, n], moments[1, n]) for n in range(3 * MOMENTS)}
     add_moments(partial, lambda k, x: x not in inner(k, 0), v, last)
     sums[...] = jnp.broadcast_to(total_row([partial[n] for n in range(3 * MOMENTS)]), (peers, 128))
 
@@ -428,12 +437,13 @@
     inverse0 = 1.0 / m0[0]
     alpha0_squared = two_product(alpha0, alpha0)
     norm1 = quadratic(((one, m0), ((-2.0 * alpha0, none), m1), (alpha0_squared, m2)))
+    norm1 = jnp.maximum(norm1, NORM_FLOOR * m0[0])
     inverse1 = 1.0 / norm1
     grow = 1.0 + norm1 * inverse0
     curve1 = quadratic(
         ((two_product(grow, grow), m1), (two_product(-2.0 * grow, alpha0), m2), (alpha0_squared, m3))
     )
-    alpha1 = norm1 / curve1
+    alpha1 = norm1 / jnp.maximum(curve1, mass_shift * norm1)
     r1 = -(alpha0 + alpha1 * grow)
     r2 = alpha1 * alpha0
     norm2 = quadratic(
@@ -445,6 +455,7 @@
             (two_product(r2, r2), m4),
         )
     )
+    norm2 = jnp.maximum(norm2, NORM_FLOOR * norm1)
     beta1 = norm2 * inverse1
     p0, p1, p2 = 1.0 + beta1 * grow, r1 - beta1 * alpha0, r2
     curve2 = quadratic(
@@ -456,7 +467,7 @@
             (two_product(p2, p2), m5),
         )
     )
-    alpha2 = norm2 / curve2
+    alpha2 = norm2 / jnp.maximum(curve2, mass_shift * norm2)
     return alpha0 + alpha1 * grow + alpha2 * p0, alpha2 * p1 - alpha1 * alpha0, alpha2 * p2
 
 
@@ -565,7 +576,7 @@
             fields,
             f32((LAYERS, 8, 128)),
             f32((3, 2, 3, LAYERS, 8, 128)),
-            f32((3 * MOMENTS, 8, 128)),
+            f32((2, 3 * MOMENTS, 8, 128)),
         ),
         in_specs=[VMEM] * 5,
         out_specs=(VMEM,) * 6,

time: 28.8 us -> 28.8 us (level)
  no operation moved by 1% of the time
where the time goes in v6:
time: 28.8 us; the launch traced here: 28.6 us
  blocking collectives  10.6 us (37%)
  starting transfers between devices  9.35 us (32%)
  Pallas kernels  4.15 us (14%)
  waiting for transfers between devices  3.84 us (13%)
  between operations  0.66 us (2%)
    all_to_all x1, blocking collectives, shards(): gathered = lax.all_to_all(sums, ('col', 'slab'), 0, 0, tiled=True)  10.6 us
    ppermute x1, starting transfers between devices, shards(): z_b = lax.ppermute(z_b, 'slab', swap_b('slab'))  6.07 us
    ppermute x1, waiting for transfers between devices, shards(): z_a = lax.ppermute(z_a, 'slab', swap_a('slab'))  2.01 us
    ppermute x1, starting transfers between devices, shards(): corner_a = lax.ppermute(corner_a, 'col', swap_a('col'))  1.55 us
    pallas_call x1, Pallas kernels, shards(): pl.pallas_call(functools.partial(krylov, peers), out_shape=(fields, f32((...  1.19 us
    ppermute x1, waiting for transfers between devices, shards(): corner_b = lax.ppermute(corner_b, 'col', swap_b('col'))  1.18 us
    pallas_call x1, Pallas kernels, shards(): pl.pallas_call(finish, out_shape=(f32((3, LAYERS, 8, 128)), f32((LAYERS,...  1.12 us
    pallas_call x1, Pallas kernels, shards(): pl.pallas_call(prepare, out_shape=(f32(block),) + (half_block,) * 4 + (f3...  0.98 us
  transfers between devices with their start and end apart: 6, of which 3 were waited for; matrix products, arithmetic and copies ran while one was open for 0% of the time, Pallas kernels for 3%

profile of v6, /device:TPU:0, one launch (start us, length us, event | category | flops | bytes accessed | tf_op | source)
XLA Modules:
  0.0 28.6 jit_solution(17028562133870417210)
XLA Ops:
  0.6 1.0 %prepare.1 = (f32[4,8,8,128]{3,2,1,0:T(8,128)S(1)}, f32[4,4,8,128]{3,2,1,0:T(8,128)S(1)}, f32[4,4,8,128]{3,2,1,0:T(8,128)S(1)}, f32[4,4,8,128]{3,2,1,0:T(8,128)S...) custom-call(s32[8,8,128]{2,1,0:T(8,128)} %labels_hbm.1, f32[3]{0:T(128)} %table_hbm.1, ...), custom_call_target="tpu_custom_call" | custom-call | tf_op jit(solution)/shard_map/prepare/pallas_call | solution.py:539
  1.6 6.1 %collective-permute-start = (f32[4,4,8,128]{3,2,1,0:T(8,128)S(1)}, f32[4,4,8,128]{3,2,1,0:T(8,128)S(1)}, u32[]{:S(2)}, u32[]{:S(2)}) collective-permute-start(f32[4,4,8,128]{3,2,1,0:T(8,128)S(1)} %get-tuple-element.20), channel_id=1, source_target_pairs={{0,7},{1,2},{2,1},{3,4},{4,3},{5,6},{6,5},{7,0},{8,15},{9,10},{10,... | collective-permute-start | bytes 196616 | tf_op jit(solution)/shard_map/ppermute | solution.py:555
  7.7 0.0 collective-permute-start.1
  7.7 0.7 %collective-permute-start.2 = (f32[4,4,8,128]{3,2,1,0:T(8,128)S(1)}, f32[4,4,8,128]{3,2,1,0:T(8,128)S(1)}, u32[]{:S(2)}, u32[]{:S(2)}) collective-permute-start(f32[4,4,8,128]{3,2,1,0:T(8,128)S(1)} %get-tuple-element.23), channel_id=1, source_target_pairs={{0,24},{8,16},{16,8},{24,0},{1,25},{9,17},{17,9},{25,1},{2,26},{10... | collective-permute-start | bytes 196616 | tf_op jit(solution)/shard_map/ppermute | solution.py:557
  8.3 1.0 %collective-permute-start.3 = (f32[4,4,8,128]{3,2,1,0:T(8,128)S(1)}, f32[4,4,8,128]{3,2,1,0:T(8,128)S(1)}, u32[]{:S(2)}, u32[]{:S(2)}) collective-permute-start(f32[4,4,8,128]{3,2,1,0:T(8,128)S(1)} %get-tuple-element.24), channel_id=1, source_target_pairs={{0,8},{8,0},{16,24},{24,16},{1,9},{9,1},{17,25},{25,17},{2,10},{10... | collective-permute-start | bytes 196616 | tf_op jit(solution)/shard_map/ppermute | solution.py:558
  9.3 0.6 %collective-permute-done.z_b = f32[4,4,8,128]{3,2,1,0:T(8,128)S(1)} collective-permute-done((f32[4,4,8,128]{3,2,1,0:T(8,128)S(1)}, f32[4,4,8,128]{3,2,1,0:T(8,128)S(1)}, u32[]{:S(2)}, u32[]{:S(2)}) %collective-permute-start) | collective-permute-done | bytes 65568 | tf_op jit(solution)/shard_map/ppermute | solution.py:555
  9.9 2.0 %collective-permute-done.1.z_a = f32[4,4,8,128]{3,2,1,0:T(8,128)S(1)} collective-permute-done((f32[4,4,8,128]{3,2,1,0:T(8,128)S(1)}, f32[4,4,8,128]{3,2,1,0:T(8,128)S(1)}, u32[]{:S(2)}, u32[]{:S(2)}) %collective-permute-start.1) | collective-permute-done | bytes 65568 | tf_op jit(solution)/shard_map/ppermute | solution.py:556
  12.0 0.1 collective-permute-start.4
  12.1 1.6 %collective-permute-start.5 = (f32[4,2,8,128]{3,2,1,0:T(8,128)S(1)}, f32[4,2,8,128]{3,2,1,0:T(8,128)S(1)}, u32[]{:S(2)}, u32[]{:S(2)}) collective-permute-start(f32[4,2,8,128]{3,2,1,0:T(8,128)S(1)} %get-tuple-element.28), channel_id=1, source_target_pairs={{0,8},{8,0},{16,24},{24,16},{1,9},{9,1},{17,25},{25,17},{2,10},{10... | collective-permute-start | bytes 98312 | tf_op jit(solution)/shard_map/ppermute | solution.py:569
  13.7 0.0 collective-permute-done.2.x_b
  13.7 0.0 collective-permute-done.3.x_a
  13.7 0.8 %early.1 = (f32[4,8,8,128]{3,2,1,0:T(8,128)S(1)}, f32[5,16,2,8,128]{4,3,2,1,0:T(8,128)S(1)}, f32[3,3,16,2,8,128]{5,4,3,2,1,0:T(8,128)S(1)}, f32[8,8,128]{2,1,0:T...) custom-call(f32[4,8,8,128]{3,2,1,0:T(8,128)S(1)} %get-tuple-element.19.own, ...), custom_call_target="tpu_custom_call" | custom-call | tf_op jit(solution)/shard_map/early/pallas_call | solution.py:571
  14.5 1.2 %collective-permute-done.4.corner_b = f32[4,2,8,128]{3,2,1,0:T(8,128)S(1)} collective-permute-done((f32[4,2,8,128]{3,2,1,0:T(8,128)S(1)}, f32[4,2,8,128]{3,2,1,0:T(8,128)S(1)}, u32[]{:S(2)}, u32[]{:S(2)}) %collective-permute-start.4) | collective-permute-done | bytes 32800 | tf_op jit(solution)/shard_map/ppermute | solution.py:568
  15.7 0.0 collective-permute-done.5.corner_a
  15.7 1.2 %krylov.1 = (f32[3,3,16,2,8,128]{5,4,3,2,1,0:T(8,128)S(1)}, f32[32,128]{1,0:T(8,128)S(1)}) custom-call(f32[4,8,8,128]{3,2,1,0:T(8,128)S(1)} %get-tuple-element.19.own, f32[4,8,8,128]{3,2,1,0:T(8,128)S(1)} %get-tuple-element.22.ring.z_ring, f32[4,8,8,128]{3,2,1,0:T(8,128)S(1)} %get-tuple-element.26.halo, ...), custom_call_target="tpu_custom_call" | custom-call | tf_op jit(solution)/shard_map/krylov/pallas_call | solution.py:587
  16.9 10.6 %all_to_all.11 = f32[32,1,128]{2,1,0:T(1,128)S(1)} all-to-all(f32[32,1,128]{2,1,0:T(1,128)S(1)} %bitcast.5), channel_id=1, replica_groups=mesh['col'=4,'slab'=8] {'col','slab'}, dimensions={0} | all-to-all | bytes 32768 | tf_op jit(solution)/shard_map/all_to_all | solution.py:597
  27.5 1.1 %finish.1 = (f32[3,8,8,128]{3,2,1,0:T(8,128)}, f32[8,8,128]{2,1,0:T(8,128)}) custom-call(f32[32,128]{1,0:T(8,128)S(1)} %bitcast.4, f32[3,3,16,2,8,128]{5,4,3,2,1,0:T(8,128)S(1)} %get-tuple-element.30.early_field, f32[3,3,16,2,8,128]{5,4,3,2,1,0:T(8,128)S(1)} %get-tuple-element.33.field, f32[8,8,128]{2,1,0:T(8,128)S(1)} %get-tuple-element.34.base, ...), custom_call_target="tpu_custom_call" | custom-call | tf_op jit(solution)/shard_map/finish/pallas_call | solution.py:599
  (1 shorter events, 0.0 us)
Async XLA Ops:
  1.6 8.3 %collective-permute-start = (f32[4,4,8,128]{3,2,1,0:T(8,128)S(1)}, f32[4,4,8,128]{3,2,1,0:T(8,128)S(1)}, u32[]{:S(2)}, u32[]{:S(2)}) collective-permute-start(f32[4,4,8,128]{3,2,1,0:T(8,128)S(1)} %get-tuple-element.20), channel_id=1, source_target_pairs={{0,7},{1,2},{2,1},{3,4},{4,3},{5,6},{6,5},{7,0},{8,15},{9,10},{10,... | collective-permute-start | bytes 196616 | tf_op jit(solution)/shard_map/ppermute | solution.py:555
  7.7 4.3 %collective-permute-start.1 = (f32[4,4,8,128]{3,2,1,0:T(8,128)S(1)}, f32[4,4,8,128]{3,2,1,0:T(8,128)S(1)}, u32[]{:S(2)}, u32[]{:S(2)}) collective-permute-start(f32[4,4,8,128]{3,2,1,0:T(8,128)S(1)} %get-tuple-element.21), channel_id=1, source_target_pairs={{0,1},{1,0},{2,3},{3,2},{4,5},{5,4},{6,7},{7,6},{8,9},{9,8},{10,11... | collective-permute-start | bytes 196616 | tf_op jit(solution)/shard_map/ppermute | solution.py:556
  7.7 6.0 %collective-permute-start.2 = (f32[4,4,8,128]{3,2,1,0:T(8,128)S(1)}, f32[4,4,8,128]{3,2,1,0:T(8,128)S(1)}, u32[]{:S(2)}, u32[]{:S(2)}) collective-permute-start(f32[4,4,8,128]{3,2,1,0:T(8,128)S(1)} %get-tuple-element.23), channel_id=1, source_target_pairs={{0,24},{8,16},{16,8},{24,0},{1,25},{9,17},{17,9},{25,1},{2,26},{10... | collective-permute-start | bytes 196616 | tf_op jit(solution)/shard_map/ppermute | solution.py:557
  8.3 5.3 %collective-permute-start.3 = (f32[4,4,8,128]{3,2,1,0:T(8,128)S(1)}, f32[4,4,8,128]{3,2,1,0:T(8,128)S(1)}, u32[]{:S(2)}, u32[]{:S(2)}) collective-permute-start(f32[4,4,8,128]{3,2,1,0:T(8,128)S(1)} %get-tuple-element.24), channel_id=1, source_target_pairs={{0,8},{8,0},{16,24},{24,16},{1,9},{9,1},{17,25},{25,17},{2,10},{10... | collective-permute-start | bytes 196616 | tf_op jit(solution)/shard_map/ppermute | solution.py:558
  12.0 3.7 %collective-permute-start.4 = (f32[4,2,8,128]{3,2,1,0:T(8,128)S(1)}, f32[4,2,8,128]{3,2,1,0:T(8,128)S(1)}, u32[]{:S(2)}, u32[]{:S(2)}) collective-permute-start(f32[4,2,8,128]{3,2,1,0:T(8,128)S(1)} %get-tuple-element.27), channel_id=1, source_target_pairs={{0,24},{8,16},{16,8},{24,0},{1,25},{9,17},{17,9},{25,1},{2,26},{10... | collective-permute-start | bytes 98312 | tf_op jit(solution)/shard_map/ppermute | solution.py:568
  12.1 3.6 %collective-permute-start.5 = (f32[4,2,8,128]{3,2,1,0:T(8,128)S(1)}, f32[4,2,8,128]{3,2,1,0:T(8,128)S(1)}, u32[]{:S(2)}, u32[]{:S(2)}) collective-permute-start(f32[4,2,8,128]{3,2,1,0:T(8,128)S(1)} %get-tuple-element.28), channel_id=1, source_target_pairs={{0,8},{8,0},{16,24},{24,16},{1,9},{9,1},{17,25},{25,17},{2,10},{10... | collective-permute-start | bytes 98312 | tf_op jit(solution)/shard_map/ppermute | solution.py:569

commit v7 on v6

--- a/solution.py
+++ b/solution.py
@@ -60,28 +60,33 @@
     copies = [pltpu.make_async_copy(source, target, sems.at[n]) for n, (source, target) in enumerate(moves)]
     for copy in copies:
         copy.start()
-    for copy in copies:
-        copy.wait()
-    for x in range(2 * HALO):
-        label = labels[x]
-        own[3, x] = jnp.where(label == 0, table[0], jnp.where(label == 1, table[1], table[2])) * factor[x]
-    for f in range(4):
+    odd_slab = parity("slab")
+    half = tile_iota(0) < 4
+
+    def fill(f):
         for x in range(HALO):
             low, high = own[f, x], own[f, HALO + x]
             x_a[f, x] = choose(odd_col, high, low)
             x_b[f, x] = choose(odd_col, low, high)
-    for i in range(3):
-        for j in range(3):
-            splat[3 * i + j] = jnp.full((8, 128), weights[i, j], jnp.float32)
-    odd_slab = parity("slab")
-    half = tile_iota(0) < 4
-    for f in range(4):
         for i in range(HALO):
             even, odd = own[f, 2 * i], own[f, 2 * i + 1]
             low_rows = jnp.where(half, even, pltpu.roll(odd, 4, 0))
             high_rows = jnp.where(half, pltpu.roll(even, 4, 0), odd)
             z_a[f, i] = choose(odd_slab, high_rows, low_rows)
             z_b[f, i] = choose(odd_slab, low_rows, high_rows)
+
+    for f in range(3):
+        copies[f].wait()
+        fill(f)
+    for copy in copies[3:]:
+        copy.wait()
+    for x in range(2 * HALO):
+        label = labels[x]
+        own[3, x] = jnp.where(label == 0, table[0], jnp.where(label == 1, table[1], table[2])) * factor[x]
+    fill(3)
+    for i in range(3):
+        for j in range(3):
+            splat[3 * i + j] = jnp.full((8, 128), weights[i, j], jnp.float32)
 
 
 def fold(z_b, z_a, ring, corner_a, corner_b):

time: 28.8 us -> 28.8 us (level)
  no operation moved by 1% of the time
where the time goes in v7:
time: 28.8 us; the launch traced here: 28.6 us
  blocking collectives  10.6 us (37%)
  starting transfers between devices  9.35 us (32%)
  Pallas kernels  4.14 us (14%)
  waiting for transfers between devices  3.84 us (13%)
  between operations  0.66 us (2%)
    all_to_all x1, blocking collectives, shards(): gathered = lax.all_to_all(sums, ('col', 'slab'), 0, 0, tiled=True)  10.6 us
    ppermute x1, starting transfers between devices, shards(): z_b = lax.ppermute(z_b, 'slab', swap_b('slab'))  6.07 us
    ppermute x1, waiting for transfers between devices, shards(): z_a = lax.ppermute(z_a, 'slab', swap_a('slab'))  2.01 us
    ppermute x1, starting transfers between devices, shards(): corner_a = lax.ppermute(corner_a, 'col', swap_a('col'))  1.55 us
    pallas_call x1, Pallas kernels, shards(): pl.pallas_call(functools.partial(krylov, peers), out_shape=(fields, f32((...  1.19 us
    ppermute x1, waiting for transfers between devices, shards(): corner_b = lax.ppermute(corner_b, 'col', swap_b('col'))  1.18 us
    pallas_call x1, Pallas kernels, shards(): pl.pallas_call(finish, out_shape=(f32((3, LAYERS, 8, 128)), f32((LAYERS,...  1.12 us
    pallas_call x1, Pallas kernels, shards(): pl.pallas_call(prepare, out_shape=(f32(block),) + (half_block,) * 4 + (f3...  0.97 us
  transfers between devices with their start and end apart: 6, of which 3 were waited for; matrix products, arithmetic and copies ran while one was open for 0% of the time, Pallas kernels for 3%

profile of v7, /device:TPU:0, one launch (start us, length us, event | category | flops | bytes accessed | tf_op | source)
XLA Modules:
  0.0 28.6 jit_solution(11586719162503402342)
XLA Ops:
  0.6 1.0 %prepare.1 = (f32[4,8,8,128]{3,2,1,0:T(8,128)S(1)}, f32[4,4,8,128]{3,2,1,0:T(8,128)S(1)}, f32[4,4,8,128]{3,2,1,0:T(8,128)S(1)}, f32[4,4,8,128]{3,2,1,0:T(8,128)S...) custom-call(s32[8,8,128]{2,1,0:T(8,128)} %labels_hbm.1, f32[3]{0:T(128)} %table_hbm.1, ...), custom_call_target="tpu_custom_call" | custom-call | tf_op jit(solution)/shard_map/prepare/pallas_call | solution.py:544
  1.6 6.1 %collective-permute-start = (f32[4,4,8,128]{3,2,1,0:T(8,128)S(1)}, f32[4,4,8,128]{3,2,1,0:T(8,128)S(1)}, u32[]{:S(2)}, u32[]{:S(2)}) collective-permute-start(f32[4,4,8,128]{3,2,1,0:T(8,128)S(1)} %get-tuple-element.20), channel_id=1, source_target_pairs={{0,7},{1,2},{2,1},{3,4},{4,3},{5,6},{6,5},{7,0},{8,15},{9,10},{10,... | collective-permute-start | bytes 196616 | tf_op jit(solution)/shard_map/ppermute | solution.py:560
  7.7 0.0 collective-permute-start.1
  7.7 0.7 %collective-permute-start.2 = (f32[4,4,8,128]{3,2,1,0:T(8,128)S(1)}, f32[4,4,8,128]{3,2,1,0:T(8,128)S(1)}, u32[]{:S(2)}, u32[]{:S(2)}) collective-permute-start(f32[4,4,8,128]{3,2,1,0:T(8,128)S(1)} %get-tuple-element.23), channel_id=1, source_target_pairs={{0,24},{8,16},{16,8},{24,0},{1,25},{9,17},{17,9},{25,1},{2,26},{10... | collective-permute-start | bytes 196616 | tf_op jit(solution)/shard_map/ppermute | solution.py:562
  8.3 1.0 %collective-permute-start.3 = (f32[4,4,8,128]{3,2,1,0:T(8,128)S(1)}, f32[4,4,8,128]{3,2,1,0:T(8,128)S(1)}, u32[]{:S(2)}, u32[]{:S(2)}) collective-permute-start(f32[4,4,8,128]{3,2,1,0:T(8,128)S(1)} %get-tuple-element.24), channel_id=1, source_target_pairs={{0,8},{8,0},{16,24},{24,16},{1,9},{9,1},{17,25},{25,17},{2,10},{10... | collective-permute-start | bytes 196616 | tf_op jit(solution)/shard_map/ppermute | solution.py:563
  9.3 0.6 %collective-permute-done.z_b = f32[4,4,8,128]{3,2,1,0:T(8,128)S(1)} collective-permute-done((f32[4,4,8,128]{3,2,1,0:T(8,128)S(1)}, f32[4,4,8,128]{3,2,1,0:T(8,128)S(1)}, u32[]{:S(2)}, u32[]{:S(2)}) %collective-permute-start) | collective-permute-done | bytes 65568 | tf_op jit(solution)/shard_map/ppermute | solution.py:560
  9.9 2.0 %collective-permute-done.1.z_a = f32[4,4,8,128]{3,2,1,0:T(8,128)S(1)} collective-permute-done((f32[4,4,8,128]{3,2,1,0:T(8,128)S(1)}, f32[4,4,8,128]{3,2,1,0:T(8,128)S(1)}, u32[]{:S(2)}, u32[]{:S(2)}) %collective-permute-start.1) | collective-permute-done | bytes 65568 | tf_op jit(solution)/shard_map/ppermute | solution.py:561
  12.0 0.1 collective-permute-start.4
  12.1 1.6 %collective-permute-start.5 = (f32[4,2,8,128]{3,2,1,0:T(8,128)S(1)}, f32[4,2,8,128]{3,2,1,0:T(8,128)S(1)}, u32[]{:S(2)}, u32[]{:S(2)}) collective-permute-start(f32[4,2,8,128]{3,2,1,0:T(8,128)S(1)} %get-tuple-element.28), channel_id=1, source_target_pairs={{0,8},{8,0},{16,24},{24,16},{1,9},{9,1},{17,25},{25,17},{2,10},{10... | collective-permute-start | bytes 98312 | tf_op jit(solution)/shard_map/ppermute | solution.py:574
  13.6 0.0 collective-permute-done.2.x_b
  13.6 0.0 collective-permute-done.3.x_a
  13.7 0.8 %early.1 = (f32[4,8,8,128]{3,2,1,0:T(8,128)S(1)}, f32[5,16,2,8,128]{4,3,2,1,0:T(8,128)S(1)}, f32[3,3,16,2,8,128]{5,4,3,2,1,0:T(8,128)S(1)}, f32[8,8,128]{2,1,0:T...) custom-call(f32[4,8,8,128]{3,2,1,0:T(8,128)S(1)} %get-tuple-element.19.own, ...), custom_call_target="tpu_custom_call" | custom-call | tf_op jit(solution)/shard_map/early/pallas_call | solution.py:576
  14.5 1.2 %collective-permute-done.4.corner_b = f32[4,2,8,128]{3,2,1,0:T(8,128)S(1)} collective-permute-done((f32[4,2,8,128]{3,2,1,0:T(8,128)S(1)}, f32[4,2,8,128]{3,2,1,0:T(8,128)S(1)}, u32[]{:S(2)}, u32[]{:S(2)}) %collective-permute-start.4) | collective-permute-done | bytes 32800 | tf_op jit(solution)/shard_map/ppermute | solution.py:573
  15.7 0.0 collective-permute-done.5.corner_a
  15.7 1.2 %krylov.1 = (f32[3,3,16,2,8,128]{5,4,3,2,1,0:T(8,128)S(1)}, f32[32,128]{1,0:T(8,128)S(1)}) custom-call(f32[4,8,8,128]{3,2,1,0:T(8,128)S(1)} %get-tuple-element.19.own, f32[4,8,8,128]{3,2,1,0:T(8,128)S(1)} %get-tuple-element.22.ring.z_ring, f32[4,8,8,128]{3,2,1,0:T(8,128)S(1)} %get-tuple-element.26.halo, ...), custom_call_target="tpu_custom_call" | custom-call | tf_op jit(solution)/shard_map/krylov/pallas_call | solution.py:592
  16.9 10.6 %all_to_all.11 = f32[32,1,128]{2,1,0:T(1,128)S(1)} all-to-all(f32[32,1,128]{2,1,0:T(1,128)S(1)} %bitcast.5), channel_id=1, replica_groups=mesh['col'=4,'slab'=8] {'col','slab'}, dimensions={0} | all-to-all | bytes 32768 | tf_op jit(solution)/shard_map/all_to_all | solution.py:602
  27.5 1.1 %finish.1 = (f32[3,8,8,128]{3,2,1,0:T(8,128)}, f32[8,8,128]{2,1,0:T(8,128)}) custom-call(f32[32,128]{1,0:T(8,128)S(1)} %bitcast.4, f32[3,3,16,2,8,128]{5,4,3,2,1,0:T(8,128)S(1)} %get-tuple-element.30.early_field, f32[3,3,16,2,8,128]{5,4,3,2,1,0:T(8,128)S(1)} %get-tuple-element.33.field, f32[8,8,128]{2,1,0:T(8,128)S(1)} %get-tuple-element.34.base, ...), custom_call_target="tpu_custom_call" | custom-call | tf_op jit(solution)/shard_map/finish/pallas_call | solution.py:604
  (1 shorter events, 0.0 us)
Async XLA Ops:
  1.6 8.3 %collective-permute-start = (f32[4,4,8,128]{3,2,1,0:T(8,128)S(1)}, f32[4,4,8,128]{3,2,1,0:T(8,128)S(1)}, u32[]{:S(2)}, u32[]{:S(2)}) collective-permute-start(f32[4,4,8,128]{3,2,1,0:T(8,128)S(1)} %get-tuple-element.20), channel_id=1, source_target_pairs={{0,7},{1,2},{2,1},{3,4},{4,3},{5,6},{6,5},{7,0},{8,15},{9,10},{10,... | collective-permute-start | bytes 196616 | tf_op jit(solution)/shard_map/ppermute | solution.py:560
  7.7 4.3 %collective-permute-start.1 = (f32[4,4,8,128]{3,2,1,0:T(8,128)S(1)}, f32[4,4,8,128]{3,2,1,0:T(8,128)S(1)}, u32[]{:S(2)}, u32[]{:S(2)}) collective-permute-start(f32[4,4,8,128]{3,2,1,0:T(8,128)S(1)} %get-tuple-element.21), channel_id=1, source_target_pairs={{0,1},{1,0},{2,3},{3,2},{4,5},{5,4},{6,7},{7,6},{8,9},{9,8},{10,11... | collective-permute-start | bytes 196616 | tf_op jit(solution)/shard_map/ppermute | solution.py:561
  7.7 6.0 %collective-permute-start.2 = (f32[4,4,8,128]{3,2,1,0:T(8,128)S(1)}, f32[4,4,8,128]{3,2,1,0:T(8,128)S(1)}, u32[]{:S(2)}, u32[]{:S(2)}) collective-permute-start(f32[4,4,8,128]{3,2,1,0:T(8,128)S(1)} %get-tuple-element.23), channel_id=1, source_target_pairs={{0,24},{8,16},{16,8},{24,0},{1,25},{9,17},{17,9},{25,1},{2,26},{10... | collective-permute-start | bytes 196616 | tf_op jit(solution)/shard_map/ppermute | solution.py:562
  8.3 5.3 %collective-permute-start.3 = (f32[4,4,8,128]{3,2,1,0:T(8,128)S(1)}, f32[4,4,8,128]{3,2,1,0:T(8,128)S(1)}, u32[]{:S(2)}, u32[]{:S(2)}) collective-permute-start(f32[4,4,8,128]{3,2,1,0:T(8,128)S(1)} %get-tuple-element.24), channel_id=1, source_target_pairs={{0,8},{8,0},{16,24},{24,16},{1,9},{9,1},{17,25},{25,17},{2,10},{10... | collective-permute-start | bytes 196616 | tf_op jit(solution)/shard_map/ppermute | solution.py:563
  12.0 3.7 %collective-permute-start.4 = (f32[4,2,8,128]{3,2,1,0:T(8,128)S(1)}, f32[4,2,8,128]{3,2,1,0:T(8,128)S(1)}, u32[]{:S(2)}, u32[]{:S(2)}) collective-permute-start(f32[4,2,8,128]{3,2,1,0:T(8,128)S(1)} %get-tuple-element.27), channel_id=1, source_target_pairs={{0,24},{8,16},{16,8},{24,0},{1,25},{9,17},{17,9},{25,1},{2,26},{10... | collective-permute-start | bytes 98312 | tf_op jit(solution)/shard_map/ppermute | solution.py:573
  12.1 3.6 %collective-permute-start.5 = (f32[4,2,8,128]{3,2,1,0:T(8,128)S(1)}, f32[4,2,8,128]{3,2,1,0:T(8,128)S(1)}, u32[]{:S(2)}, u32[]{:S(2)}) collective-permute-start(f32[4,2,8,128]{3,2,1,0:T(8,128)S(1)} %get-tuple-element.28), channel_id=1, source_target_pairs={{0,8},{8,0},{16,24},{24,16},{1,9},{9,1},{17,25},{25,17},{2,10},{10... | collective-permute-start | bytes 98312 | tf_op jit(solution)/shard_map/ppermute | solution.py:574

commit v8 on v7

--- a/solution.py
+++ b/solution.py
@@ -142,7 +142,7 @@
     return product, error + (a[0] * b[1] + a[1] * b[0])
 
 
-def total_row(pairs):
+def total_row(pairs, start):
     row = tile_iota(0)
     lane = tile_iota(1)
     place = [[n] for n in range(len(pairs))]
@@ -171,8 +171,8 @@
         for shift in (64, 32, 16, 8, 4, 2, 1):
             pair = pair_sum(pair, [pltpu.roll(a, shift, 1) for a in pair])
         for n, at in home(spot, 0, 1):
-            result = jnp.where((row == at) & (lane == 4 * n), pair[0], result)
-            result = jnp.where((row == at) & (lane == 4 * n + 1), pair[1], result)
+            result = jnp.where((row == at) & (lane == 4 * (start + n)), pair[0], result)
+            result = jnp.where((row == at) & (lane == 4 * (start + n) + 1), pair[1], result)
     return jnp.sum(result, axis=0, keepdims=True)
 
 
@@ -402,13 +402,17 @@
             for x, value in applied(k - 1, i, lambda x, t: x in needed(k, t) and x not in inner(k, t), v, ready):
                 for t in value:
                     field[k, i, x, t] = value[t]
+    partial = {n: (moments[0, n], moments[1, n]) for n in range(3 * MOMENTS)}
+    add_moments(partial, lambda k, x: k < 3 and x not in inner(k, 0), v, None)
+    others = 3 * (MOMENTS - 1)
+    row = total_row([partial[n] for n in range(others)], 0)
     last = {}
     for i in range(3):
         for x, value in applied(2, i, lambda x, t: t == 0 and x in needed(3, 0) and x not in inner(3, 0), v, ready):
             last[i, x] = value[0]
-    partial = {n: (moments[0, n], moments[1, n]) for n in range(3 * MOMENTS)}
-    add_moments(partial, lambda k, x: x not in inner(k, 0), v, last)
-    sums[...] = jnp.broadcast_to(total_row([partial[n] for n in range(3 * MOMENTS)]), (peers, 128))
+    add_moments(partial, lambda k, x: k == 3 and x not in inner(k, 0), v, last)
+    row = row + total_row([partial[n] for n in range(others, 3 * MOMENTS)], others)
+    sums[...] = jnp.broadcast_to(row, (peers, 128))
 
 
 def quadratic(terms):

time: 28.8 us -> 28.8 us (level)
  no operation moved by 1% of the time
where the time goes in v8:
time: 28.8 us; the launch traced here: 28.6 us
  blocking collectives  10.6 us (37%)
  starting transfers between devices  9.35 us (32%)
  Pallas kernels  4.12 us (14%)
  waiting for transfers between devices  3.84 us (13%)
  between operations  0.66 us (2%)
    all_to_all x1, blocking collectives, shards(): gathered = lax.all_to_all(sums, ('col', 'slab'), 0, 0, tiled=True)  10.6 us
    ppermute x1, starting transfers between devices, shards(): z_b = lax.ppermute(z_b, 'slab', swap_b('slab'))  6.07 us
    ppermute x1, waiting for transfers between devices, shards(): z_a = lax.ppermute(z_a, 'slab', swap_a('slab'))  2.01 us
    ppermute x1, starting transfers between devices, shards(): corner_a = lax.ppermute(corner_a, 'col', swap_a('col'))  1.55 us
    ppermute x1, waiting for transfers between devices, shards(): corner_b = lax.ppermute(corner_b, 'col', swap_b('col'))  1.18 us
    pallas_call x1, Pallas kernels, shards(): pl.pallas_call(functools.partial(krylov, peers), out_shape=(fields, f32((...  1.17 us
    pallas_call x1, Pallas kernels, shards(): pl.pallas_call(finish, out_shape=(f32((3, LAYERS, 8, 128)), f32((LAYERS,...  1.12 us
    pallas_call x1, Pallas kernels, shards(): pl.pallas_call(prepare, out_shape=(f32(block),) + (half_block,) * 4 + (f3...  0.97 us
  transfers between devices with their start and end apart: 6, of which 3 were waited for; matrix products, arithmetic and copies ran while one was open for 0% of the time, Pallas kernels for 3%

profile of v8, /device:TPU:0, one launch (start us, length us, event | category | flops | bytes accessed | tf_op | source)
XLA Modules:
  0.0 28.6 jit_solution(7123024829461787394)
XLA Ops:
  0.6 1.0 %prepare.1 = (f32[4,8,8,128]{3,2,1,0:T(8,128)S(1)}, f32[4,4,8,128]{3,2,1,0:T(8,128)S(1)}, f32[4,4,8,128]{3,2,1,0:T(8,128)S(1)}, f32[4,4,8,128]{3,2,1,0:T(8,128)S...) custom-call(s32[8,8,128]{2,1,0:T(8,128)} %labels_hbm.1, f32[3]{0:T(128)} %table_hbm.1, ...), custom_call_target="tpu_custom_call" | custom-call | tf_op jit(solution)/shard_map/prepare/pallas_call | solution.py:548
  1.6 6.1 %collective-permute-start = (f32[4,4,8,128]{3,2,1,0:T(8,128)S(1)}, f32[4,4,8,128]{3,2,1,0:T(8,128)S(1)}, u32[]{:S(2)}, u32[]{:S(2)}) collective-permute-start(f32[4,4,8,128]{3,2,1,0:T(8,128)S(1)} %get-tuple-element.20), channel_id=1, source_target_pairs={{0,7},{1,2},{2,1},{3,4},{4,3},{5,6},{6,5},{7,0},{8,15},{9,10},{10,... | collective-permute-start | bytes 196616 | tf_op jit(solution)/shard_map/ppermute | solution.py:564
  7.7 0.0 collective-permute-start.1
  7.7 0.7 %collective-permute-start.2 = (f32[4,4,8,128]{3,2,1,0:T(8,128)S(1)}, f32[4,4,8,128]{3,2,1,0:T(8,128)S(1)}, u32[]{:S(2)}, u32[]{:S(2)}) collective-permute-start(f32[4,4,8,128]{3,2,1,0:T(8,128)S(1)} %get-tuple-element.23), channel_id=1, source_target_pairs={{0,24},{8,16},{16,8},{24,0},{1,25},{9,17},{17,9},{25,1},{2,26},{10... | collective-permute-start | bytes 196616 | tf_op jit(solution)/shard_map/ppermute | solution.py:566
  8.3 1.0 %collective-permute-start.3 = (f32[4,4,8,128]{3,2,1,0:T(8,128)S(1)}, f32[4,4,8,128]{3,2,1,0:T(8,128)S(1)}, u32[]{:S(2)}, u32[]{:S(2)}) collective-permute-start(f32[4,4,8,128]{3,2,1,0:T(8,128)S(1)} %get-tuple-element.24), channel_id=1, source_target_pairs={{0,8},{8,0},{16,24},{24,16},{1,9},{9,1},{17,25},{25,17},{2,10},{10... | collective-permute-start | bytes 196616 | tf_op jit(solution)/shard_map/ppermute | solution.py:567
  9.3 0.6 %collective-permute-done.z_b = f32[4,4,8,128]{3,2,1,0:T(8,128)S(1)} collective-permute-done((f32[4,4,8,128]{3,2,1,0:T(8,128)S(1)}, f32[4,4,8,128]{3,2,1,0:T(8,128)S(1)}, u32[]{:S(2)}, u32[]{:S(2)}) %collective-permute-start) | collective-permute-done | bytes 65568 | tf_op jit(solution)/shard_map/ppermute | solution.py:564
  9.9 2.0 %collective-permute-done.1.z_a = f32[4,4,8,128]{3,2,1,0:T(8,128)S(1)} collective-permute-done((f32[4,4,8,128]{3,2,1,0:T(8,128)S(1)}, f32[4,4,8,128]{3,2,1,0:T(8,128)S(1)}, u32[]{:S(2)}, u32[]{:S(2)}) %collective-permute-start.1) | collective-permute-done | bytes 65568 | tf_op jit(solution)/shard_map/ppermute | solution.py:565
  12.0 0.1 collective-permute-start.4
  12.1 1.6 %collective-permute-start.5 = (f32[4,2,8,128]{3,2,1,0:T(8,128)S(1)}, f32[4,2,8,128]{3,2,1,0:T(8,128)S(1)}, u32[]{:S(2)}, u32[]{:S(2)}) collective-permute-start(f32[4,2,8,128]{3,2,1,0:T(8,128)S(1)} %get-tuple-element.28), channel_id=1, source_target_pairs={{0,8},{8,0},{16,24},{24,16},{1,9},{9,1},{17,25},{25,17},{2,10},{10... | collective-permute-start | bytes 98312 | tf_op jit(solution)/shard_map/ppermute | solution.py:578
  13.6 0.0 collective-permute-done.2.x_b
  13.6 0.0 collective-permute-done.3.x_a
  13.7 0.8 %early.1 = (f32[4,8,8,128]{3,2,1,0:T(8,128)S(1)}, f32[5,16,2,8,128]{4,3,2,1,0:T(8,128)S(1)}, f32[3,3,16,2,8,128]{5,4,3,2,1,0:T(8,128)S(1)}, f32[8,8,128]{2,1,0:T...) custom-call(f32[4,8,8,128]{3,2,1,0:T(8,128)S(1)} %get-tuple-element.19.own, ...), custom_call_target="tpu_custom_call" | custom-call | tf_op jit(solution)/shard_map/early/pallas_call | solution.py:580
  14.5 1.2 %collective-permute-done.4.corner_b = f32[4,2,8,128]{3,2,1,0:T(8,128)S(1)} collective-permute-done((f32[4,2,8,128]{3,2,1,0:T(8,128)S(1)}, f32[4,2,8,128]{3,2,1,0:T(8,128)S(1)}, u32[]{:S(2)}, u32[]{:S(2)}) %collective-permute-start.4) | collective-permute-done | bytes 32800 | tf_op jit(solution)/shard_map/ppermute | solution.py:577
  15.7 0.0 collective-permute-done.5.corner_a
  15.7 1.2 %krylov.1 = (f32[3,3,16,2,8,128]{5,4,3,2,1,0:T(8,128)S(1)}, f32[32,128]{1,0:T(8,128)S(1)}) custom-call(f32[4,8,8,128]{3,2,1,0:T(8,128)S(1)} %get-tuple-element.19.own, f32[4,8,8,128]{3,2,1,0:T(8,128)S(1)} %get-tuple-element.22.ring.z_ring, f32[4,8,8,128]{3,2,1,0:T(8,128)S(1)} %get-tuple-element.26.halo, ...), custom_call_target="tpu_custom_call" | custom-call | tf_op jit(solution)/shard_map/krylov/pallas_call | solution.py:596
  16.9 10.6 %all_to_all.11 = f32[32,1,128]{2,1,0:T(1,128)S(1)} all-to-all(f32[32,1,128]{2,1,0:T(1,128)S(1)} %bitcast.5), channel_id=1, replica_groups=mesh['col'=4,'slab'=8] {'col','slab'}, dimensions={0} | all-to-all | bytes 32768 | tf_op jit(solution)/shard_map/all_to_all | solution.py:606
  27.5 1.1 %finish.1 = (f32[3,8,8,128]{3,2,1,0:T(8,128)}, f32[8,8,128]{2,1,0:T(8,128)}) custom-call(f32[32,128]{1,0:T(8,128)S(1)} %bitcast.4, f32[3,3,16,2,8,128]{5,4,3,2,1,0:T(8,128)S(1)} %get-tuple-element.30.early_field, f32[3,3,16,2,8,128]{5,4,3,2,1,0:T(8,128)S(1)} %get-tuple-element.33.field, f32[8,8,128]{2,1,0:T(8,128)S(1)} %get-tuple-element.34.base, ...), custom_call_target="tpu_custom_call" | custom-call | tf_op jit(solution)/shard_map/finish/pallas_call | solution.py:608
  (1 shorter events, 0.0 us)
Async XLA Ops:
  1.6 8.3 %collective-permute-start = (f32[4,4,8,128]{3,2,1,0:T(8,128)S(1)}, f32[4,4,8,128]{3,2,1,0:T(8,128)S(1)}, u32[]{:S(2)}, u32[]{:S(2)}) collective-permute-start(f32[4,4,8,128]{3,2,1,0:T(8,128)S(1)} %get-tuple-element.20), channel_id=1, source_target_pairs={{0,7},{1,2},{2,1},{3,4},{4,3},{5,6},{6,5},{7,0},{8,15},{9,10},{10,... | collective-permute-start | bytes 196616 | tf_op jit(solution)/shard_map/ppermute | solution.py:564
  7.7 4.3 %collective-permute-start.1 = (f32[4,4,8,128]{3,2,1,0:T(8,128)S(1)}, f32[4,4,8,128]{3,2,1,0:T(8,128)S(1)}, u32[]{:S(2)}, u32[]{:S(2)}) collective-permute-start(f32[4,4,8,128]{3,2,1,0:T(8,128)S(1)} %get-tuple-element.21), channel_id=1, source_target_pairs={{0,1},{1,0},{2,3},{3,2},{4,5},{5,4},{6,7},{7,6},{8,9},{9,8},{10,11... | collective-permute-start | bytes 196616 | tf_op jit(solution)/shard_map/ppermute | solution.py:565
  7.7 6.0 %collective-permute-start.2 = (f32[4,4,8,128]{3,2,1,0:T(8,128)S(1)}, f32[4,4,8,128]{3,2,1,0:T(8,128)S(1)}, u32[]{:S(2)}, u32[]{:S(2)}) collective-permute-start(f32[4,4,8,128]{3,2,1,0:T(8,128)S(1)} %get-tuple-element.23), channel_id=1, source_target_pairs={{0,24},{8,16},{16,8},{24,0},{1,25},{9,17},{17,9},{25,1},{2,26},{10... | collective-permute-start | bytes 196616 | tf_op jit(solution)/shard_map/ppermute | solution.py:566
  8.3 5.3 %collective-permute-start.3 = (f32[4,4,8,128]{3,2,1,0:T(8,128)S(1)}, f32[4,4,8,128]{3,2,1,0:T(8,128)S(1)}, u32[]{:S(2)}, u32[]{:S(2)}) collective-permute-start(f32[4,4,8,128]{3,2,1,0:T(8,128)S(1)} %get-tuple-element.24), channel_id=1, source_target_pairs={{0,8},{8,0},{16,24},{24,16},{1,9},{9,1},{17,25},{25,17},{2,10},{10... | collective-permute-start | bytes 196616 | tf_op jit(solution)/shard_map/ppermute | solution.py:567
  12.0 3.7 %collective-permute-start.4 = (f32[4,2,8,128]{3,2,1,0:T(8,128)S(1)}, f32[4,2,8,128]{3,2,1,0:T(8,128)S(1)}, u32[]{:S(2)}, u32[]{:S(2)}) collective-permute-start(f32[4,2,8,128]{3,2,1,0:T(8,128)S(1)} %get-tuple-element.27), channel_id=1, source_target_pairs={{0,24},{8,16},{16,8},{24,0},{1,25},{9,17},{17,9},{25,1},{2,26},{10... | collective-permute-start | bytes 98312 | tf_op jit(solution)/shard_map/ppermute | solution.py:577
  12.1 3.6 %collective-permute-start.5 = (f32[4,2,8,128]{3,2,1,0:T(8,128)S(1)}, f32[4,2,8,128]{3,2,1,0:T(8,128)S(1)}, u32[]{:S(2)}, u32[]{:S(2)}) collective-permute-start(f32[4,2,8,128]{3,2,1,0:T(8,128)S(1)} %get-tuple-element.28), channel_id=1, source_target_pairs={{0,8},{8,0},{16,24},{24,16},{1,9},{9,1},{17,25},{25,17},{2,10},{10... | collective-permute-start | bytes 98312 | tf_op jit(solution)/shard_map/ppermute | solution.py:578
